TPU v7x, 256 devices: a whole 4x4x8 slice. The times are simulated.
256 devices in a mesh: cplx: 4 (over y_hi, core), row: 64 (over z, x, y_lo).
Axes of the slice: x: 4, y: 4 (y_hi: 2, y_lo: 2; y = y_hi * 2 + y_lo), z: 8, core: 2. Of those that a mesh axis runs over, the one named last changes fastest.
Arguments:
- pair_state: bfloat16 [2048, 512, 128], P(('cplx', 'row')), parts along dimension 0, may hold values from -60 to 60
- cotangent: bfloat16 [2048, 512, 128], P(('cplx', 'row')), parts along dimension 0, may hold values from -6 to 6
- token_mask: int32 [2048], P('cplx'), parts along dimension 0, may hold values 0 or 1
- input_gain: float32 [128], replicated, may hold values from 0.25 to 1.75
- input_bias: float32 [128], replicated, may hold values from -3 to 3
- input_weight: bfloat16 [128, 640], replicated, may hold values from -0.5 to 0.5
- output_gain: float32 [128], replicated, may hold values from 0.25 to 1.75
- output_bias: float32 [128], replicated, may hold values from -3 to 3
- output_weight: bfloat16 [128, 128], replicated, may hold values from -0.5 to 0.5
Outputs:
- pair_gradient: bfloat16 [2048, 512, 128], P(('cplx', 'row')), parts along dimension 0
- input_gradient: float32 [512, 640], P(('cplx', 'row')), parts along dimension 0
- output_gradient: float32 [512, 128], P(('cplx', 'row')), parts along dimension 0
There are 4 independent parts, one for each index of `cplx`. A program takes and returns all parts, laid end to end along the dimension named above; an argument that names none is the same for every part. Nothing has to cross between parts.
Inputs may be any that keep to these rules, and one draw needn't show every extreme that they name: `token_mask`: 1 marks a token of the complex, 0 a padding slot.
All inputs are finite; a program needn't handle non-finite values.
Results may differ from a plain program's by a relative error of at most 0.0076.
Values may be sent and summed in bfloat16 or wider, within the bound.
No kernel may reach another device: no remote copies, remote signals or barrier semaphores. Data moves between devices by JAX's collectives and lax.ppermute only.
A program may use at most 64 MiB of HBM per device.

v0:
```python
import jax
import jax.numpy as jnp
from jax import lax
from jax.sharding import PartitionSpec as P

epsilon = 1e-05


def norm_parts(values, norm_axis):
    average = jnp.mean(values, axis=norm_axis, keepdims=True)
    centered = values - average
    variance = jnp.mean(centered * centered, axis=norm_axis, keepdims=True)
    inverse = lax.rsqrt(variance + epsilon)
    return (centered * inverse, inverse)


def norm_backward(upstream, scaled, inverse, norm_axis):
    first_mean = jnp.mean(upstream, axis=norm_axis, keepdims=True)
    second = jnp.mean(upstream * scaled, axis=norm_axis, keepdims=True)
    return inverse * (upstream - first_mean - scaled * second)


def to_pieces(values, slab_count):
    return values.reshape(
        slab_count, values.shape[0] // slab_count, values.shape[1], values.shape[2]
    )


def from_pieces(values):
    return values.reshape(values.shape[0] * values.shape[1], values.shape[2], values.shape[3])


def triangle(left_slab, right_slab):
    result = jnp.einsum(
        "xcik,xcjk->xcij", left_slab, right_slab, preferred_element_type=jnp.float32
    )
    return result.astype(jnp.bfloat16)


def factor_gradients(grad_slab, left_slab, right_slab):
    left_part = jnp.einsum(
        "xcij,xcjk->xcik", grad_slab, right_slab, preferred_element_type=jnp.float32
    )
    right_part = jnp.einsum(
        "xcij,xcik->xcjk", grad_slab, left_slab, preferred_element_type=jnp.float32
    )
    return (left_part.astype(jnp.bfloat16), right_part.astype(jnp.bfloat16))


def project(normed, weight_block):
    return jnp.einsum("rnd,de->ern", normed, weight_block, preferred_element_type=jnp.float32)


def on_device(
    pair_state,
    cotangent,
    token_mask,
    input_gain,
    input_bias,
    input_weight,
    output_gain,
    output_bias,
    output_weight,
):
    row_count = pair_state.shape[0]
    tokens = pair_state.shape[1]
    channels = pair_state.shape[2]
    slab_count = lax.axis_size("row")
    token_float = token_mask.astype(jnp.float32)
    row_start = lax.axis_index("row") * row_count
    row_float = lax.dynamic_slice_in_dim(token_float, row_start, row_count)
    pair_mask = (row_float[:, None] * token_float[None, :])[None]
    scaled_in, inverse_in = norm_parts(pair_state.astype(jnp.float32), 2)
    normed = (scaled_in * input_gain + input_bias).astype(jnp.bfloat16)
    left_proj = project(normed, input_weight[:, 0 : 2 * channels])
    right_proj = project(normed, input_weight[:, 2 * channels : 4 * channels])
    out_gate = jax.nn.sigmoid(project(normed, input_weight[:, 4 * channels :]))
    left_lin = left_proj[:channels]
    left_gate = jax.nn.sigmoid(left_proj[channels:])
    right_lin = right_proj[:channels]
    right_gate = jax.nn.sigmoid(right_proj[channels:])
    left_rows = to_pieces((pair_mask * left_gate * left_lin).astype(jnp.bfloat16), slab_count)
    right_rows = to_pieces((pair_mask * right_gate * right_lin).astype(jnp.bfloat16), slab_count)
    left_slab, right_slab = (
        lax.all_to_all(left_rows, "row", split_axis=0, concat_axis=2, tiled=True),
        lax.all_to_all(right_rows, "row", split_axis=0, concat_axis=2, tiled=True),
    )
    product_slab = triangle(left_slab, right_slab)
    product_pieces = lax.all_to_all(product_slab, "row", split_axis=2, concat_axis=0, tiled=True)
    product_rows = from_pieces(product_pieces).astype(jnp.float32)
    scaled_out, inverse_out = norm_parts(product_rows, 0)
    normed_out = (scaled_out * output_gain[:, None, None] + output_bias[:, None, None]).astype(
        jnp.bfloat16
    )
    projected = jnp.einsum(
        "crn,cd->drn", normed_out, output_weight, preferred_element_type=jnp.float32
    )
    upstream = jnp.transpose(cotangent, (2, 0, 1)).astype(jnp.float32)
    mixed_grad = (upstream * out_gate).astype(jnp.bfloat16)
    gate_grad = upstream * projected * out_gate * (1.0 - out_gate)
    out_norm_grad = jnp.einsum(
        "drn,cd->crn", mixed_grad, output_weight, preferred_element_type=jnp.float32
    )
    product_grad = norm_backward(
        out_norm_grad * output_gain[:, None, None], scaled_out, inverse_out, 0
    ).astype(jnp.bfloat16)
    grad_rows = to_pieces(product_grad, slab_count)
    grad_slab = lax.all_to_all(grad_rows, "row", split_axis=0, concat_axis=2, tiled=True)
    left_part, right_part = factor_gradients(grad_slab, left_slab, right_slab)
    left_pieces, right_pieces = (
        lax.all_to_all(left_part, "row", split_axis=2, concat_axis=0, tiled=True),
        lax.all_to_all(right_part, "row", split_axis=2, concat_axis=0, tiled=True),
    )
    left_back = from_pieces(left_pieces).astype(jnp.float32) * pair_mask
    right_back = from_pieces(right_pieces).astype(jnp.float32) * pair_mask
    proj_grad = jnp.concatenate(
        [
            (left_back * left_gate).astype(jnp.bfloat16),
            (left_back * left_lin * left_gate * (1.0 - left_gate)).astype(jnp.bfloat16),
            (right_back * right_gate).astype(jnp.bfloat16),
            (right_back * right_lin * right_gate * (1.0 - right_gate)).astype(jnp.bfloat16),
            gate_grad.astype(jnp.bfloat16),
        ],
        axis=0,
    )
    normed_grad = jnp.einsum(
        "ern,de->rnd", proj_grad, input_weight, preferred_element_type=jnp.float32
    )
    pair_gradient = norm_backward(normed_grad * input_gain, scaled_in, inverse_in, 2).astype(
        jnp.bfloat16
    )
    input_term = (
        jnp.einsum("rnd,ern->de", normed, proj_grad, preferred_element_type=jnp.float32) / tokens
    )
    output_term = (
        jnp.einsum("crn,drn->cd", normed_out, mixed_grad, preferred_element_type=jnp.float32)
        / tokens
    )
    input_gradient, output_gradient = (
        lax.psum_scatter(input_term, "row", scatter_dimension=0, tiled=True),
        lax.psum_scatter(output_term, "row", scatter_dimension=0, tiled=True),
    )
    return (pair_gradient, input_gradient, output_gradient)


def solution(mesh):
    return jax.shard_map(
        on_device,
        mesh=mesh,
        in_specs=(
            P(("cplx", "row"), None, None),
            P(("cplx", "row"), None, None),
            P("cplx"),
            P(),
            P(),
            P(),
            P(),
            P(),
            P(),
        ),
        out_specs=(
            P(("cplx", "row"), None, None),
            P(("cplx", "row"), None),
            P(("cplx", "row"), None),
        ),
        check_vma=False,
    )
```

profile of v0, /device:TPU:16, one launch (start us, length us, event | category | flops | bytes accessed | tf_op | source)
XLA Modules:
  0.0 879.4 jit_solution(5712075969375751696)
XLA Ops:
  7.2 1.6 copy.29
  8.8 0.2 convert_reduce_fusion
  9.0 0.3 fusion.11
  9.3 2.7 convolution_bitcast_fusion
  12.1 2.8 convolution_bitcast_fusion.1
  14.8 0.1 dynamic_slice.3
  14.9 0.1 broadcast_multiply_fusion
  15.0 4.7 multiply_convert_fusion.5
  19.7 1.2 reshape.130
  21.0 3.4 copy.32
  24.4 12.9 %all-to-all-start = ((bf16[64,2,8,512]{3,1,2,0:T(2,128)(2,1)}), bf16[64,2,8,512]{3,1,2,0:T(2,128)(2,1)}, u32[]{:S(2)}, u32[]{:S(2)}) async-start(bf16[64,2,8,512]{3,1,2,0:T(2,128)(2,1)} %copy.32), calls=%async_computation | async-start | bytes 2097152 | tf_op jit(solution)/shard_map/all_to_all | solution.py:85
  37.3 0.4 reshape.132
  37.8 1.1 copy.36
  38.9 27.1 %all-to-all-done = bf16[64,2,8,512]{3,1,2,0:T(2,128)(2,1)} async-done(((bf16[64,2,8,512]{3,1,2,0:T(2,128)(2,1)}), bf16[64,2,8,512]{3,1,2,0:T(2,128)(2,1)}, u32[]{:S(2)}, u32[]{:S(2)}) %all-to-all-start) | async-done | bytes 1048608 | tf_op jit(solution)/shard_map/all_to_all | solution.py:85
  66.0 34.1 %all_to_all.72 = bf16[64,2,8,512]{3,1,2,0:T(2,128)(2,1)S(1)} all-to-all(bf16[64,2,8,512]{3,1,2,0:T(2,128)(2,1)S(1)} %copy.36), channel_id=1, replica_groups=mesh['cplx'=4,'row'=64] {'row'}, dimensions={0} | all-to-all | bytes 2097152 | tf_op jit(solution)/shard_map/all_to_all | solution.py:86
  100.1 1.0 copy-done.9
  101.1 2.0 fusion.27
  103.1 2.0 copy.38
  105.2 5.8 all-to-all-start.2
  111.0 1.3 copy.40
  112.3 2.3 add_divide_fusion
  114.6 24.3 %all-to-all-done.2 = bf16[1,2,512,512]{3,1,0,2:T(2,128)(2,1)S(1)} async-done(((bf16[1,2,512,512]{3,1,0,2:T(2,128)(2,1)}), bf16[1,2,512,512]{3,1,0,2:T(2,128)(2,1)S(1)}, u32[]{:S(2)}, u32[]{:S(2)}) %all-to-all-start.2) | async-done | bytes 1048608 | tf_op jit(solution)/shard_map/all_to_all | solution.py:89
  138.9 2.1 copy_bitcast_fusion.2
  141.0 0.8 fusion.61
  141.8 2.7 reshape.136
  144.6 2.6 multiply_reduce_fusion
  147.2 2.7 bitcast_reduce_fusion
  149.9 1.7 fusion.23
  151.5 2.2 reshape.134
  153.8 2.4 copy.43
  156.2 33.4 %all_to_all.73 = bf16[64,2,8,512]{3,1,2,0:T(2,128)(2,1)S(1)} all-to-all(bf16[64,2,8,512]{3,1,2,0:T(2,128)(2,1)S(1)} %copy.43), channel_id=1, replica_groups=mesh['cplx'=4,'row'=64] {'row'}, dimensions={0} | all-to-all | bytes 2097152 | tf_op jit(solution)/shard_map/all_to_all | solution.py:108
  189.6 1.0 copy-done.10
  190.6 2.0 fusion.29
  192.5 2.1 copy.48
  194.6 6.2 all-to-all-start.5
  200.9 2.3 fusion.28
  203.1 2.0 copy.45
  205.2 23.1 %all-to-all-done.5 = bf16[1,2,512,512]{3,1,0,2:T(2,128)(2,1)} async-done(((bf16[1,2,512,512]{3,1,0,2:T(2,128)(2,1)}), bf16[1,2,512,512]{3,1,0,2:T(2,128)(2,1)}, u32[]{:S(2)}, u32[]{:S(2)}) %all-to-all-start.5) | async-done | bytes 1048608 | tf_op jit(solution)/shard_map/all_to_all | solution.py:112
  228.3 6.0 all-to-all-start.4
  234.4 0.6 dynamic-slice
  235.7 3.1 fusion.31
  238.8 3.3 copy_bitcast_fusion
  242.1 3.7 reshape.138
  245.8 16.2 %all-to-all-done.4 = bf16[1,2,512,512]{3,1,0,2:T(2,128)(2,1)} async-done(((bf16[1,2,512,512]{3,1,0,2:T(2,128)(2,1)}), bf16[1,2,512,512]{3,1,0,2:T(2,128)(2,1)}, u32[]{:S(2)}, u32[]{:S(2)}) %all-to-all-start.4) | async-done | bytes 1048608 | tf_op jit(solution)/shard_map/all_to_all | solution.py:111
  262.0 3.3 copy_bitcast_fusion.1
  265.3 3.6 reshape.137
  269.0 3.0 fusion.32
  272.0 0.4 copy-done.2
  272.4 2.6 fusion.33
  275.1 0.2 copy-done.1
  275.2 0.7 copy-done.3
  275.9 0.6 fusion.34
  276.6 0.9 fusion.35
  277.5 0.7 copy-done.4
  278.1 0.3 copy-done.6
  278.4 0.9 fusion.26
  279.3 2.3 copy-done.7
  281.6 2.5 fusion.30
  284.1 3.5 multiply_reduce_fusion.1
  287.7 1.6 fusion.10
  289.2 2.3 copy.51
  291.5 578.5 %all-reduce.5.cloned.1.call-done = (f32[128,640]{1,0:T(8,128)}, f32[128,128]{1,0:T(8,128)}) async-done(((f32[128,640]{1,0:T(8,128)}, f32[128,128]{1,0:T(8,128)}), (f32[128,640]{1,0:T(8,128)}, f32[128,128]{1,0:T(8,128)})) %all-reduce.5.cloned.1.call-update) | async-done | bytes 393232
  870.0 1.3 constant_dynamic-slice_fusion.1
  871.3 1.2 constant_dynamic-slice_fusion
  (38 shorter events, 0.2 us)
Async XLA Ops:
  7.2 140.0 %copy-start = (bf16[128,128]{1,0:T(8,128)(2,1)S(1)}, bf16[128,128]{1,0:T(8,128)(2,1)}, u32[]{:S(2)}) copy-start(bf16[128,128]{1,0:T(8,128)(2,1)} %param.17) | copy-start | bytes 98308
  7.2 2.1 copy-start.12
  7.2 2.1 copy-start.14
  7.2 2.1 copy-start.11
  12.1 2.8 copy-start.15
  24.4 41.6 %all-to-all-start = ((bf16[64,2,8,512]{3,1,2,0:T(2,128)(2,1)}), bf16[64,2,8,512]{3,1,2,0:T(2,128)(2,1)}, u32[]{:S(2)}, u32[]{:S(2)}) async-start(bf16[64,2,8,512]{3,1,2,0:T(2,128)(2,1)} %copy.32), calls=%async_computation | async-start | bytes 2097152 | tf_op jit(solution)/shard_map/all_to_all | solution.py:85
  100.1 1.0 copy-start.9
  103.1 7.9 copy-start.8
  105.2 33.7 %all-to-all-start.2 = ((bf16[1,2,512,512]{3,1,0,2:T(2,128)(2,1)}), bf16[1,2,512,512]{3,1,0,2:T(2,128)(2,1)S(1)}, u32[]{:S(2)}, u32[]{:S(2)}) async-start(bf16[1,2,512,512]{3,1,0,2:T(2,128)(2,1)} %copy.38), calls=%async_computation.2 | async-start | bytes 2097152 | tf_op jit(solution)/shard_map/all_to_all | solution.py:89
  138.9 2.1 copy-start.5
  141.8 5.4 copy-start.13
  189.6 1.0 copy-start.10
  194.6 33.7 %all-to-all-start.5 = ((bf16[1,2,512,512]{3,1,0,2:T(2,128)(2,1)}), bf16[1,2,512,512]{3,1,0,2:T(2,128)(2,1)}, u32[]{:S(2)}, u32[]{:S(2)}) async-start(bf16[1,2,512,512]{3,1,0,2:T(2,128)(2,1)} %copy.48), calls=%async_computation.5 | async-start | bytes 2097152 | tf_op jit(solution)/shard_map/all_to_all | solution.py:112
  203.1 31.3 %copy-start.17 = (u32[256]{0:T(256)S(1)}, u32[256]{0:T(256)}, u32[]{:S(2)}) copy-start(u32[256]{0:T(256)} %constant.37) | copy-start | bytes 3076
  203.1 32.5 %copy-start.16 = (f32[128]{0:T(128)S(1)}, f32[128]{0:T(128)}, u32[]{:S(2)}) copy-start(f32[128]{0:T(128)} %param.16) | copy-start | bytes 1540
  228.3 33.7 %all-to-all-start.4 = ((bf16[1,2,512,512]{3,1,0,2:T(2,128)(2,1)}), bf16[1,2,512,512]{3,1,0,2:T(2,128)(2,1)}, u32[]{:S(2)}, u32[]{:S(2)}) async-start(bf16[1,2,512,512]{3,1,0,2:T(2,128)(2,1)} %copy.45), calls=%async_computation.4 | async-start | bytes 2097152 | tf_op jit(solution)/shard_map/all_to_all | solution.py:111
  234.4 635.6 %all-reduce.5.cloned.1.call-start = ((), (), s32[]{:S(2)}) async-start(), calls=%async_computation.6 | async-start | bytes 786432
  269.0 3.4 copy-start.2
  272.4 2.8 copy-start.1
  272.4 3.5 copy-start.3
  276.6 1.6 copy-start.4
  276.6 1.8 copy-start.6
  279.3 2.3 copy-start.7
Sparse Core Ops, SparseCore 0:
  287.8 582.1 all-reduce.4
where the time goes:
time: 880 us; the launch traced here: 879 us
  waiting for transfers between devices  669 us (76%)
  blocking collectives  67.5 us (8%)
  local copies, waits for them, and re-layouts  41.9 us (5%)
  starting transfers between devices  31.1 us (4%)
  other arithmetic  27.9 us (3%)
  matrix products  26.7 us (3%)
  between operations  15.1 us (2%)
    unnamed x2, waiting for transfers between devices  578 us
    all_to_all x1, blocking collectives, on_device(): lax.all_to_all(right_rows, 'row', split_axis=0, concat_axis=2, tiled=True)  34.1 us
    all_to_all x1, blocking collectives, on_device(): lax.all_to_all(grad_rows, 'row', split_axis=0, concat_axis=2, tiled=True)  33.4 us
    all_to_all x1, waiting for transfers between devices, on_device(): lax.all_to_all(left_rows, 'row', split_axis=0, concat_axis=2, tiled=True)  27.1 us
    all_to_all x1, waiting for transfers between devices, on_device(): lax.all_to_all(product_slab, 'row', split_axis=2, concat_axis=0, tiled=True)  24.3 us
    all_to_all x1, waiting for transfers between devices, on_device(): lax.all_to_all(right_part, 'row', split_axis=2, concat_axis=0, tiled=True)  23.1 us
  transfers between devices with their start and end apart: 5, of which 5 were waited for; matrix products, arithmetic and copies ran while one was open for 3% of the time, Pallas kernels for 0%

commit v1 on v0

--- a/solution.py
+++ b/solution.py
@@ -81,10 +81,10 @@
     right_gate = jax.nn.sigmoid(right_proj[channels:])
     left_rows = to_pieces((pair_mask * left_gate * left_lin).astype(jnp.bfloat16), slab_count)
     right_rows = to_pieces((pair_mask * right_gate * right_lin).astype(jnp.bfloat16), slab_count)
-    left_slab, right_slab = (
-        lax.all_to_all(left_rows, "row", split_axis=0, concat_axis=2, tiled=True),
-        lax.all_to_all(right_rows, "row", split_axis=0, concat_axis=2, tiled=True),
-    )
+    both_rows = jnp.concatenate([left_rows, right_rows], axis=1)
+    both_slabs = lax.all_to_all(both_rows, "row", split_axis=0, concat_axis=2, tiled=True)
+    half = channels // slab_count
+    left_slab, right_slab = both_slabs[:, :half], both_slabs[:, half:]
     product_slab = triangle(left_slab, right_slab)
     product_pieces = lax.all_to_all(product_slab, "row", split_axis=2, concat_axis=0, tiled=True)
     product_rows = from_pieces(product_pieces).astype(jnp.float32)
@@ -107,10 +107,9 @@
     grad_rows = to_pieces(product_grad, slab_count)
     grad_slab = lax.all_to_all(grad_rows, "row", split_axis=0, concat_axis=2, tiled=True)
     left_part, right_part = factor_gradients(grad_slab, left_slab, right_slab)
-    left_pieces, right_pieces = (
-        lax.all_to_all(left_part, "row", split_axis=2, concat_axis=0, tiled=True),
-        lax.all_to_all(right_part, "row", split_axis=2, concat_axis=0, tiled=True),
-    )
+    both_parts = jnp.concatenate([left_part, right_part], axis=1)
+    both_pieces = lax.all_to_all(both_parts, "row", split_axis=2, concat_axis=0, tiled=True)
+    left_pieces, right_pieces = both_pieces[:, :half], both_pieces[:, half:]
     left_back = from_pieces(left_pieces).astype(jnp.float32) * pair_mask
     right_back = from_pieces(right_pieces).astype(jnp.float32) * pair_mask
     proj_grad = jnp.concatenate(
@@ -136,10 +135,12 @@
         jnp.einsum("crn,drn->cd", normed_out, mixed_grad, preferred_element_type=jnp.float32)
         / tokens
     )
-    input_gradient, output_gradient = (
-        lax.psum_scatter(input_term, "row", scatter_dimension=0, tiled=True),
-        lax.psum_scatter(output_term, "row", scatter_dimension=0, tiled=True),
-    )
+    both_terms = jnp.concatenate([input_term, output_term], axis=1)
+    both_terms = both_terms.reshape(slab_count, channels // slab_count, 6 * channels)
+    shares = lax.all_to_all(both_terms, "row", split_axis=0, concat_axis=0, tiled=True)
+    both_sums = jnp.sum(shares, axis=0)
+    input_gradient = both_sums[:, : 5 * channels]
+    output_gradient = both_sums[:, 5 * channels :]
     return (pair_gradient, input_gradient, output_gradient)
 
 

time: 880 us -> 297 us (0.34)
  waiting for transfers between devices: 669 us -> 81.1 us
  blocking collectives: 67.5 us -> 97.1 us
  between operations: 15.1 us -> 1.01 us
  starting transfers between devices: 31.1 us -> 18.9 us
    unnamed x2 -> x0, waiting for transfers between devices: 578 us -> none
    all_to_all x1, blocking collectives: 34.1 us -> 63.7 us  [on_device(): lax.all_to_all(both_rows, 'row', split_axis=0, concat_axis=2, tiled=True)]
    all_to_all x3 -> x2, starting transfers between devices: 25.2 us -> 12.7 us  [the longest x1 6.54 us: on_device(): lax.all_to_all(both_terms, 'row', split_axis=0, concat_axis=0, tiled=True)]
    all_to_all x3 -> x2, waiting for transfers between devices: 66.5 us -> 57 us  [the longest x1 47.1 us: on_device(): lax.all_to_all(both_parts, 'row', split_axis=2, concat_axis=0, tiled=True)]
  transfers between devices with their start and end apart: 5 -> 3, of which waited for: 5 -> 3; matrix products, arithmetic and copies ran while one was open for 3% -> 3% of each run, Pallas kernels for 0% -> 0%
where the time goes in v1:
time: 297 us; the launch traced here: 296 us
  blocking collectives  97.1 us (33%)
  waiting for transfers between devices  81.1 us (27%)
  local copies, waits for them, and re-layouts  38.9 us (13%)
  other arithmetic  36.5 us (12%)
  matrix products  22.4 us (8%)
  starting transfers between devices  18.9 us (6%)
    all_to_all x1, blocking collectives, on_device(): lax.all_to_all(both_rows, 'row', split_axis=0, concat_axis=2, tiled=True)  63.7 us
    all_to_all x1, waiting for transfers between devices, on_device(): lax.all_to_all(both_parts, 'row', split_axis=2, concat_axis=0, tiled=True)  47.1 us
    all_to_all x1, blocking collectives, on_device(): lax.all_to_all(grad_rows, 'row', split_axis=0, concat_axis=2, tiled=True)  33.4 us
    all_to_all x1, waiting for transfers between devices, on_device(): lax.all_to_all(product_slab, 'row', split_axis=2, concat_axis=0, tiled=True)  24.1 us
    unnamed x4, other arithmetic  13.1 us
    all_to_all x1, waiting for transfers between devices, on_device(): lax.all_to_all(both_terms, 'row', split_axis=0, concat_axis=0, tiled=True)  9.91 us
    unnamed x39, local copies, waits for them, and re-layouts  9.58 us
    dot_general x3, matrix products, project(): jnp.einsum('rnd,de->ern', normed, weight_block, preferred_element_type=jn...  7.79 us
  transfers between devices with their start and end apart: 3, of which 3 were waited for; matrix products, arithmetic and copies ran while one was open for 3% of the time, Pallas kernels for 0%

profile of v1, /device:TPU:16, one launch (start us, length us, event | category | flops | bytes accessed | tf_op | source)
XLA Modules:
  0.0 295.9 jit_solution(2398687238049624556)
XLA Ops:
  0.6 0.0 copy-start
  0.7 1.6 copy.28
  2.2 0.2 convert_reduce_fusion
  2.4 0.3 fusion.11
  2.8 0.0 copy-done.13
  2.8 2.8 convolution_bitcast_fusion
  5.6 2.7 convolution_bitcast_fusion.1
  8.3 0.1 dynamic_slice.3
  8.4 0.1 broadcast_multiply_fusion
  8.5 4.7 %multiply_convert_fusion.5 = (bf16[128,8,512]{2,0,1:T(8,128)(2,1)S(1)}, bf16[128,8,512]{2,0,1:T(8,128)(2,1)S(1)}) fusion(f32[256,8,512]{2,0,1:T(8,128)} %convolution_bitcast_fusion.1, f32[8,512]{1,0:T(8,128)S(1)} %broadcast_multiply_fusion, f32[256,8,512]{2,0,1:T(8,128)} %convolution_bitcast_fusion), kind=kLoop, calls=%fused_computation.52 | loop fusion | flops 6291456 | bytes 10502144 | tf_op jit(solution)/shard_map/convert_element_type | solution.py:82
  13.2 1.2 reshape.123
  14.5 1.2 reshape.124
  15.7 0.3 copy-done.8
  15.9 3.2 %pad_maximum_fusion = bf16[64,4,8,512]{3,1,0,2:T(4,128)(2,1)S(1)} fusion(bf16[64,2,8,512]{3,1,0,2:T(2,128)(2,1)} %reshape.124, bf16[64,2,8,512]{3,1,0,2:T(2,128)(2,1)S(1)} %copy-done.8), kind=kLoop, calls=%fused_computation.24 | loop fusion | flops 4194304 | bytes 4194304 | tf_op jit(solution)/shard_map/concatenate | solution.py:84
  19.2 1.1 copy.55
  20.3 63.7 %all_to_all.65 = bf16[64,4,8,512]{3,1,2,0:T(4,128)(2,1)S(1)} all-to-all(bf16[64,4,8,512]{3,1,2,0:T(4,128)(2,1)S(1)} %copy.55), channel_id=1, replica_groups=mesh['cplx'=4,'row'=64] {'row'}, dimensions={0} | all-to-all | bytes 4194304 | tf_op jit(solution)/shard_map/all_to_all | solution.py:85
  84.0 0.4 copy.77
  84.4 1.4 copy-done.9
  85.8 0.7 fusion.27
  86.6 0.0 copy-start.11
  86.6 2.0 copy.36
  88.6 6.2 %all-to-all-start.1 = ((bf16[1,2,512,512]{3,1,0,2:T(2,128)(2,1)}), bf16[1,2,512,512]{3,1,0,2:T(2,128)(2,1)S(1)}, u32[]{:S(2)}, u32[]{:S(2)}) async-start(bf16[1,2,512,512]{3,1,0,2:T(2,128)(2,1)} %copy.36), calls=%async_computation.1 | async-start | bytes 2097152 | tf_op jit(solution)/shard_map/all_to_all | solution.py:89
  94.8 1.3 copy.38
  96.2 2.3 add_divide_fusion
  98.4 24.1 %all-to-all-done.1 = bf16[1,2,512,512]{3,1,0,2:T(2,128)(2,1)S(1)} async-done(((bf16[1,2,512,512]{3,1,0,2:T(2,128)(2,1)}), bf16[1,2,512,512]{3,1,0,2:T(2,128)(2,1)S(1)}, u32[]{:S(2)}, u32[]{:S(2)}) %all-to-all-start.1) | async-done | bytes 1048608 | tf_op jit(solution)/shard_map/all_to_all | solution.py:89
  122.5 2.1 copy_bitcast_fusion.1
  124.6 0.8 fusion.53
  125.5 0.0 copy-start.14
  125.5 2.7 reshape.130
  128.2 2.6 multiply_reduce_fusion
  130.8 2.7 bitcast_reduce_fusion
  133.5 1.7 fusion.23
  135.2 2.3 reshape.127
  137.4 2.5 copy.41
  140.0 33.4 %all_to_all.66 = bf16[64,2,8,512]{3,1,2,0:T(2,128)(2,1)S(1)} all-to-all(bf16[64,2,8,512]{3,1,2,0:T(2,128)(2,1)S(1)} %copy.41), channel_id=1, replica_groups=mesh['cplx'=4,'row'=64] {'row'}, dimensions={0} | all-to-all | bytes 2097152 | tf_op jit(solution)/shard_map/all_to_all | solution.py:108
  173.4 0.7 fusion.28
  174.1 0.8 fusion.29
  174.9 0.2 pad_maximum_fusion.1
  175.0 2.9 copy.44
  178.0 6.2 %all-to-all-start.3 = ((bf16[1,4,512,512]{3,1,0,2:T(4,128)(2,1)}), bf16[1,4,512,512]{3,1,0,2:T(4,128)(2,1)}, u32[]{:S(2)}, u32[]{:S(2)}) async-start(bf16[1,4,512,512]{3,1,0,2:T(4,128)(2,1)} %copy.44), calls=%async_computation.3 | async-start | bytes 4194304 | tf_op jit(solution)/shard_map/all_to_all | solution.py:111
  184.2 2.5 fusion.31
  186.7 47.1 %all-to-all-done.3 = bf16[1,4,512,512]{3,1,0,2:T(4,128)(2,1)} async-done(((bf16[1,4,512,512]{3,1,0,2:T(4,128)(2,1)}), bf16[1,4,512,512]{3,1,0,2:T(4,128)(2,1)}, u32[]{:S(2)}, u32[]{:S(2)}) %all-to-all-start.3) | async-done | bytes 2097184 | tf_op jit(solution)/shard_map/all_to_all | solution.py:111
  233.8 2.3 copy.76
  236.1 4.0 %slice_convert_fusion = (f32[64,2,8,512]{3,1,0,2:T(2,128)}, f32[64,2,8,512]{3,1,0,2:T(2,128)}) fusion(bf16[64,4,8,512]{3,1,0,2:T(4,128)(2,1)S(1)} %bitcast.141), kind=kLoop, calls=%fused_computation.69 | loop fusion | flops 1048576 | bytes 6291456 | tf_op jit(solution)/shard_map/convert_element_type | solution.py:114
  240.1 3.7 %reshape.131 = f32[128,8,512]{2,0,1:T(8,128)} reshape(f32[64,2,8,512]{3,1,0,2:T(2,128)} %get-tuple-element.14) | data formatting | bytes 4194304 | tf_op jit(solution)/shard_map/convert_element_type | solution.py:113
  243.7 3.0 %fusion.32 = bf16[640,8,512]{2,0,1:T(8,128)(2,1)S(1)} fusion(f32[128,8,512]{2,0,1:T(8,128)} %reshape.131, f32[8,512]{1,0:T(8,128)S(1)} %broadcast_multiply_fusion, f32[256,8,512]{2,0,1:T(8,128)} %convolution_bitcast_fusion.1), kind=kLoop, calls=%fused_computation.65 | loop fusion | flops 3145727 | bytes 5259264
  246.8 0.4 copy-done.2
  247.2 2.4 fusion.33
  249.6 2.3 copy-done.6
  251.9 3.7 %reshape.132 = f32[128,8,512]{2,0,1:T(8,128)} reshape(f32[64,2,8,512]{3,1,0,2:T(2,128)} %get-tuple-element.13) | data formatting | bytes 4194304 | tf_op jit(solution)/shard_map/convert_element_type | solution.py:114
  255.6 4.0 %fusion.34 = bf16[640,8,512]{2,0,1:T(8,128)(2,1)} fusion(bf16[640,8,512]{2,0,1:T(8,128)(2,1)} %copy-done.6, f32[128,8,512]{2,0,1:T(8,128)} %reshape.132, f32[8,512]{1,0:T(8,128)S(1)} %broadcast_multiply_fusion, f32[256,8,512]{2,0,1:T(8,128)} %convolution_bitcast_fusion), kind=kLoop, calls=%fused_computation.67 | loop fusion | flops 3145728 | bytes 5259264
  259.6 3.6 %fusion.35 = bf16[640,8,512]{2,0,1:T(8,128)(2,1)} fusion(bf16[640,8,512]{2,0,1:T(8,128)(2,1)} %fusion.34, f32[256,8,512]{2,0,1:T(8,128)S(1)} %copy-done.1, f32[128,8,512]{2,0,1:T(8,128)} %reshape.132, f32[8,512]{1,0:T(8,128)S(1)} %broadcast_multiply_fusion), kind=kLoop, calls=%fused_computation.68 | loop fusion | flops 4718592 | bytes 7356416
  263.2 1.9 fusion.26
  265.1 4.4 %fusion.30 = f32[128,640]{1,0:T(8,128)S(1)} fusion(bf16[640,8,512]{2,0,1:T(8,128)(2,1)} %fusion.26, bf16[8,512,128]{1,2,0:T(8,128)(2,1)S(1)} %copy.28, f32[128]{0:T(128)S(1)} %copy-done.15, f32[128]{0:T(128)S(1)} %copy-done.13, f32[8,512]{1,0:T(8,128)S(1)} %add_rsqrt_fusion.1, f32[8,512]{1,0:T(8,128)S(1)} %broadcast_multiply_fusion.6), kind=kOutput, calls=%fused_computation.62 | convolution fusion | flops 674316288 | bytes 6652928 | tf_op jit(solution)/shard_map/rnd,ern->de/dot_general | solution.py:132
  269.5 1.0 multiply_reduce_fusion.1
  270.5 0.8 pad_maximum_fusion.2
  271.3 2.0 reshape.129
  273.3 6.5 %all-to-all-start.4 = ((f32[64,2,768]{2,1,0:T(2,128)}), f32[64,2,768]{2,1,0:T(2,128)}, u32[]{:S(2)}, u32[]{:S(2)}) async-start(f32[64,2,768]{2,1,0:T(2,128)} %reshape.129), calls=%async_computation.4 | async-start | bytes 786432 | tf_op jit(solution)/shard_map/all_to_all | solution.py:140
  279.9 1.6 fusion.10
  281.4 2.3 copy.48
  283.7 9.9 %all-to-all-done.4 = f32[64,2,768]{2,1,0:T(2,128)} async-done(((f32[64,2,768]{2,1,0:T(2,128)}), f32[64,2,768]{2,1,0:T(2,128)}, u32[]{:S(2)}, u32[]{:S(2)}) %all-to-all-start.4) | async-done | bytes 393248 | tf_op jit(solution)/shard_map/all_to_all | solution.py:140
  293.6 1.1 reduce_sum.89
  294.8 0.6 slice.60
  295.3 0.6 slice.61
  (36 shorter events, 0.1 us)
Async XLA Ops:
  0.6 130.2 %copy-start = (bf16[128,128]{1,0:T(8,128)(2,1)S(1)}, bf16[128,128]{1,0:T(8,128)(2,1)}, u32[]{:S(2)}) copy-start(bf16[128,128]{1,0:T(8,128)(2,1)} %param.17) | copy-start | bytes 98308
  0.6 2.1 copy-start.13
  0.7 2.1 copy-start.15
  0.7 2.1 copy-start.12
  5.6 2.7 copy-start.16
  14.5 1.5 copy-start.8
  84.4 1.4 copy-start.9
  86.6 8.3 %copy-start.11 = (bf16[8,512,128]{2,1,0:T(8,128)(2,1)S(1)}, bf16[8,512,128]{2,1,0:T(8,128)(2,1)}, u32[]{:S(2)}) copy-start(bf16[8,512,128]{2,1,0:T(8,128)(2,1)} %param.10) | copy-start | bytes 3145732
  88.6 33.9 %all-to-all-start.1 = ((bf16[1,2,512,512]{3,1,0,2:T(2,128)(2,1)}), bf16[1,2,512,512]{3,1,0,2:T(2,128)(2,1)S(1)}, u32[]{:S(2)}, u32[]{:S(2)}) async-start(bf16[1,2,512,512]{3,1,0,2:T(2,128)(2,1)} %copy.36), calls=%async_computation.1 | async-start | bytes 2097152 | tf_op jit(solution)/shard_map/all_to_all | solution.py:89
  122.5 2.1 copy-start.4
  125.5 5.4 %copy-start.14 = (f32[128]{0:T(128)S(1)}, f32[128]{0:T(128)}, u32[]{:S(2)}) copy-start(f32[128]{0:T(128)} %param.15) | copy-start | bytes 1540
  137.4 35.9 %copy-start.10 = (bf16[1,4,64,8,512]{4,3,2,1,0:T(8,128)(2,1)S(1)}, bf16[1,4,64,8,512]{4,3,2,1,0:T(8,128)(2,1)}, u32[]{:S(2)}) copy-start(bf16[1,4,64,8,512]{4,3,2,1,0:T(8,128)(2,1)} %copy-done.9) | copy-start | bytes 6291460
  178.0 6.2 %copy-start.17 = (f32[128]{0:T(128)S(1)}, f32[128]{0:T(128)}, u32[]{:S(2)}) copy-start(f32[128]{0:T(128)} %param.16) | copy-start | bytes 1540
  178.0 55.8 %all-to-all-start.3 = ((bf16[1,4,512,512]{3,1,0,2:T(4,128)(2,1)}), bf16[1,4,512,512]{3,1,0,2:T(4,128)(2,1)}, u32[]{:S(2)}, u32[]{:S(2)}) async-start(bf16[1,4,512,512]{3,1,0,2:T(4,128)(2,1)} %copy.44), calls=%async_computation.3 | async-start | bytes 4194304 | tf_op jit(solution)/shard_map/all_to_all | solution.py:111
  243.7 3.4 %copy-start.2 = (f32[256,8,512]{2,0,1:T(8,128)S(1)}, f32[256,8,512]{2,0,1:T(8,128)}, u32[]{:S(2)}) copy-start(f32[256,8,512]{2,0,1:T(8,128)} %convolution_bitcast_fusion.1) | copy-start | bytes 12582916
  249.6 2.3 copy-start.6
  255.6 4.0 %copy-start.1 = (f32[256,8,512]{2,0,1:T(8,128)S(1)}, f32[256,8,512]{2,0,1:T(8,128)}, u32[]{:S(2)}) copy-start(f32[256,8,512]{2,0,1:T(8,128)} %convolution_bitcast_fusion) | copy-start | bytes 12582916
  259.6 3.6 %copy-start.3 = (f32[8,512,128]{1,2,0:T(8,128)S(1)}, f32[8,512,128]{1,2,0:T(8,128)}, u32[]{:S(2)}) copy-start(f32[8,512,128]{1,2,0:T(8,128)} %add_divide_fusion) | copy-start | bytes 6291460
  259.6 3.6 %copy-start.5 = (bf16[8,512,128]{1,2,0:T(8,128)(2,1)S(1)}, bf16[8,512,128]{1,2,0:T(8,128)(2,1)}, u32[]{:S(2)}) copy-start(bf16[8,512,128]{1,2,0:T(8,128)(2,1)} %copy.38) | copy-start | bytes 3145732
  265.1 4.4 %copy-start.7 = (bf16[640,8,512]{2,0,1:T(8,128)(2,1)S(1)}, bf16[640,8,512]{2,0,1:T(8,128)(2,1)}, u32[]{:S(2)}) copy-start(bf16[640,8,512]{2,0,1:T(8,128)(2,1)} %fusion.26) | copy-start | bytes 15728644
  273.3 20.3 %all-to-all-start.4 = ((f32[64,2,768]{2,1,0:T(2,128)}), f32[64,2,768]{2,1,0:T(2,128)}, u32[]{:S(2)}, u32[]{:S(2)}) async-start(f32[64,2,768]{2,1,0:T(2,128)} %reshape.129), calls=%async_computation.4 | async-start | bytes 786432 | tf_op jit(solution)/shard_map/all_to_all | solution.py:140

commit v2 on v0

v2 whole, which is shorter than its diff:
```python
import jax
import jax.numpy as jnp
from jax import lax
from jax.experimental import pallas as pl
from jax.experimental.pallas import tpu as pltpu
from jax.sharding import PartitionSpec as P

epsilon = 1e-05
LANES = 128
F32 = jnp.float32
BF16 = jnp.bfloat16


def dot_nn(a, b):
    return lax.dot_general(a, b, (((1,), (0,)), ((), ())), preferred_element_type=F32)


def dot_nt(a, b):
    return lax.dot_general(a, b, (((1,), (1,)), ((), ())), preferred_element_type=F32)


def dot_tn(a, b):
    return lax.dot_general(a, b, (((0,), (0,)), ((), ())), preferred_element_type=F32)


def eye(size, dtype):
    rows = lax.broadcasted_iota(jnp.int32, (size, size), 0)
    cols = lax.broadcasted_iota(jnp.int32, (size, size), 1)
    return jnp.where(rows == cols, 1.0, 0.0).astype(F32).astype(dtype)


def as_column(row):
    return jnp.sum(eye(row.shape[1], F32) * row, axis=1, keepdims=True)


def turned(block):
    rows, lanes, channels = block.shape
    return dot_nt(eye(channels, BF16), block.reshape(rows * lanes, channels))


def norm_columns(values):
    average = jnp.mean(values, axis=0, keepdims=True)
    centered = values - average
    variance = jnp.mean(centered * centered, axis=0, keepdims=True)
    inverse = lax.rsqrt(variance + epsilon)
    return centered * inverse, inverse


def norm_columns_backward(upstream, scaled, inverse):
    first = jnp.mean(upstream, axis=0, keepdims=True)
    second = jnp.mean(upstream * scaled, axis=0, keepdims=True)
    return inverse * (upstream - first - scaled * second)


def normed_columns(block, gain_row, bias_row):
    scaled, inverse = norm_columns(turned(block))
    normed = (scaled * as_column(gain_row) + as_column(bias_row)).astype(BF16)
    return normed, scaled, inverse


def mask_row(start_ref, mask_ref, lane_mask, rows):
    lane_float = lane_mask.astype(F32)
    parts = [
        lane_float * mask_ref[start_ref[0] + row].astype(F32) for row in range(rows)
    ]
    return jnp.concatenate(parts, axis=1)


def front_kernel(
    start_ref, mask_ref, lane_mask_ref, x_ref, gain_ref, bias_ref, weight_ref, out_ref,
    turned_weight, spread,
):
    rows = x_ref.shape[0]
    channels = x_ref.shape[2]

    @pl.when(pl.program_id(0) == 0)
    def _():
        turned_weight[...] = weight_ref[...].astype(F32).T.astype(BF16)

    normed, _, _ = normed_columns(x_ref[...], gain_ref[...], bias_ref[...])
    pair_mask = mask_row(start_ref, mask_ref, lane_mask_ref[...], rows)
    for side in range(2):
        base = 2 * side * channels
        pre = dot_nn(turned_weight[base : base + 2 * channels, :], normed)
        factor = pair_mask * jax.nn.sigmoid(pre[channels:]) * pre[:channels]
        for row in range(rows):
            spread[side, pl.ds(row, channels, stride=rows), :] = factor[
                :, row * LANES : (row + 1) * LANES
            ]
        group = channels * rows // out_ref.shape[0]
        out_ref[:, side * group : (side + 1) * group, :] = (
            spread[side].reshape(out_ref.shape[0], group, LANES).astype(BF16)
        )


def side_kernel(
    start_ref, mask_ref, lane_mask_ref, x_ref, cot_ref, gain_ref, bias_ref, weight_ref,
    out_gain_ref, out_weight_ref,
    h_ref, coef_ref, normed_ref, mixed_ref, gate_coef_ref,
    turned_weight,
):
    rows = x_ref.shape[0]
    channels = x_ref.shape[2]

    @pl.when(pl.program_id(0) == 0)
    def _():
        turned_weight[...] = weight_ref[...].astype(F32).T.astype(BF16)

    normed, _, _ = normed_columns(x_ref[...], gain_ref[...], bias_ref[...])
    normed_ref[0] = normed
    pair_mask = mask_row(start_ref, mask_ref, lane_mask_ref[...], rows)
    for side in range(2):
        base = 2 * side * channels
        pre = dot_nn(turned_weight[base : base + 2 * channels, :], normed)
        gate = jax.nn.sigmoid(pre[channels:])
        coef_ref[0, 2 * side] = pair_mask * gate
        coef_ref[0, 2 * side + 1] = pair_mask * pre[:channels] * gate * (1.0 - gate)
    out_gate = jax.nn.sigmoid(dot_nn(turned_weight[4 * channels :, :], normed))
    upstream = turned(cot_ref[...])
    mixed = (upstream * out_gate).astype(BF16)
    mixed_ref[0] = mixed
    gate_coef_ref[0] = upstream * out_gate * (1.0 - out_gate)
    h = dot_nn(out_weight_ref[...], mixed) * as_column(out_gain_ref[...])
    for row in range(rows):
        h_ref[0, pl.ds(row, channels, stride=rows), :] = h[:, row * LANES : (row + 1) * LANES]


def unpack(recv_ref, base, rows):
    block = recv_ref[:, base : base + 2 * rows, :].astype(F32)
    slabs = block.shape[0]
    return [
        block[:, part * rows : (part + 1) * rows, :].reshape(slabs * rows, LANES).astype(BF16)
        for part in range(2)
    ]


def pack(first, second, slabs):
    rows = first.shape[0] // slabs
    parts = [part.reshape(slabs, rows, LANES) for part in (first, second)]
    return jnp.concatenate(parts, axis=1).astype(BF16)


def slab_unpack_kernel(recv_ref, out_ref):
    slabs = recv_ref.shape[0]
    tokens = out_ref.shape[1]
    rows = tokens // slabs
    for tile in range(tokens // LANES):
        for side in range(2):
            parts = unpack(recv_ref, (tile * 2 + side) * 2 * rows, rows)
            for part in range(2):
                out_ref[side * 2 + part, :, tile * LANES : (tile + 1) * LANES] = parts[part]


def product_kernel(recv_ref, out_ref, slab):
    slabs = recv_ref.shape[0]
    tokens = slab.shape[1]
    slab_unpack_kernel(recv_ref, slab)
    rows = tokens // slabs
    products = [dot_nt(slab[part], slab[2 + part]) for part in range(2)]
    for tile in range(tokens // LANES):
        cols = slice(tile * LANES, (tile + 1) * LANES)
        out_ref[:, tile * 2 * rows : (tile + 1) * 2 * rows, :] = pack(
            products[0][:, cols], products[1][:, cols], slabs
        )


def product_grad_kernel(recv_ref, h_ref, out_ref):
    slabs, group, _ = recv_ref.shape
    rows = h_ref.shape[1] // (2 * slabs)
    product = recv_ref[...].astype(F32).reshape(2 * slabs, rows, LANES)
    h = h_ref[0].reshape(2 * slabs, rows, LANES)
    scaled, inverse = norm_columns(product)
    grad = norm_columns_backward(h, scaled, inverse)
    out_ref[...] = grad.reshape(slabs, group, LANES).astype(BF16)


def gather_rows(spread, channels, rows):
    return jnp.concatenate(
        [spread[pl.ds(row, channels, stride=rows), :] for row in range(rows)], axis=1
    )


def gate_side_kernel(
    recv_ref, normed_ref, mixed_ref, gate_coef_ref, out_gain_ref, out_bias_ref,
    out_weight_ref, gate_weight_ref,
    gate_normed_ref, share_ref,
    spread, gate_term, out_term, laid,
):
    step = pl.program_id(0)
    channels = normed_ref.shape[1]
    rows = normed_ref.shape[2] // LANES

    @pl.when(step == 0)
    def _():
        gate_term[...] = jnp.zeros_like(gate_term)
        out_term[...] = jnp.zeros_like(out_term)

    spread[...] = recv_ref[...].astype(F32).reshape(channels * rows, LANES)
    product = gather_rows(spread, channels, rows)
    scaled, _ = norm_columns(product)
    normed_out = (scaled * as_column(out_gain_ref[...]) + as_column(out_bias_ref[...])).astype(BF16)
    projected = dot_tn(out_weight_ref[...], normed_out)
    gate_grad = (projected * gate_coef_ref[0]).astype(BF16)
    gate_normed_ref[0] = dot_nn(gate_weight_ref[...], gate_grad)
    gate_term[...] += dot_nt(normed_ref[0], gate_grad)
    out_term[...] += dot_nt(normed_out, mixed_ref[0])

    @pl.when(step == pl.num_programs(0) - 1)
    def _():
        half = channels // 2
        for which, term in enumerate((gate_term, out_term)):
            for part in range(2):
                value = term[pl.ds(part, half, stride=2), :]
                high = value.astype(BF16).astype(F32)
                laid[pl.ds(part * 4 + which * 2, half, stride=8), :] = high
                laid[pl.ds(part * 4 + which * 2 + 1, half, stride=8), :] = value - high
        share_ref[...] = laid[...].reshape(half, 8, LANES).astype(BF16)


def factor_grad_kernel(recv_ref, factor_ref, share_ref, out_ref, slab):
    slabs = recv_ref.shape[0]
    tokens = slab.shape[1]
    rows = tokens // slabs
    for tile in range(tokens // LANES):
        parts = unpack(recv_ref, tile * 2 * rows, rows)
        for part in range(2):
            slab[part, :, tile * LANES : (tile + 1) * LANES] = parts[part]
    for side in range(2):
        if side == 0:
            grads = [dot_nn(slab[part], factor_ref[2 + part]) for part in range(2)]
        else:
            grads = [dot_tn(slab[part], factor_ref[part]) for part in range(2)]
        for tile in range(tokens // LANES):
            cols = slice(tile * LANES, (tile + 1) * LANES)
            base = (tile * 2 + side) * 2 * rows
            out_ref[:, base : base + 2 * rows, :] = pack(
                grads[0][:, cols], grads[1][:, cols], slabs
            )
    base = tokens // LANES * 4 * rows
    out_ref[:, base : base + 8, :] = share_ref[...]


def proj_grad_kernel(recv_ref, coef_ref, normed_ref, proj_ref, share_ref, spread, term):
    step = pl.program_id(0)
    channels = normed_ref.shape[1]
    rows = normed_ref.shape[2] // LANES
    group = recv_ref.shape[1] // 2

    @pl.when(step == 0)
    def _():
        term[...] = jnp.zeros_like(term)

    for side in range(2):
        spread[...] = (
            recv_ref[:, side * group : (side + 1) * group, :]
            .astype(F32)
            .reshape(channels * rows, LANES)
        )
        grad = gather_rows(spread, channels, rows)
        for part in range(2):
            block = 2 * side + part
            value = (grad * coef_ref[0, block]).astype(BF16)
            proj_ref[0, block * channels : (block + 1) * channels, :] = value
            term[block] += dot_nt(normed_ref[0], value)

    @pl.when(step == pl.num_programs(0) - 1)
    def _():
        half = channels // 2
        for part in range(2):
            for block in range(4):
                share_ref[pl.ds(part * 4 + block, half, stride=8), :] = term[
                    block, pl.ds(part, half, stride=2), :
                ]


def pair_grad_kernel(proj_ref, gate_normed_ref, x_ref, gain_ref, weight_ref, out_ref):
    rows = x_ref.shape[0]
    scaled, inverse = norm_columns(turned(x_ref[...]))
    normed_grad = dot_nn(weight_ref[...], proj_ref[0]) + gate_normed_ref[0]
    grad = norm_columns_backward(normed_grad * as_column(gain_ref[...]), scaled, inverse)
    for row in range(rows):
        out_ref[row] = grad[:, row * LANES : (row + 1) * LANES].T.astype(BF16)


def weight_sum_kernel(recv_ref, early_ref, in_ref, out_ref, *, tokens):
    late = jnp.sum(recv_ref[...], axis=0) / tokens
    early = jnp.sum(early_ref[...].astype(F32), axis=0) / tokens
    for part in range(2):
        for block in range(4):
            in_ref[part : part + 1, block * LANES : (block + 1) * LANES] = late[
                part * 4 + block : part * 4 + block + 1
            ]
        at = part * 4
        in_ref[part : part + 1, 4 * LANES :] = early[at : at + 1] + early[at + 1 : at + 2]
        out_ref[part : part + 1, :] = early[at + 2 : at + 3] + early[at + 3 : at + 4]


def whole(shape):
    return pl.BlockSpec(shape, lambda *_: (0,) * len(shape))


def exchange(values):
    return lax.all_to_all(values, "row", split_axis=0, concat_axis=0, tiled=True)


def params(**kwargs):
    return pltpu.CompilerParams(vmem_limit_bytes=56 * 1024 * 1024, **kwargs)


def cost(flops, moved):
    return pl.CostEstimate(flops=flops, bytes_accessed=moved, transcendentals=0)


def on_device(
    pair_state,
    cotangent,
    token_mask,
    input_gain,
    input_bias,
    input_weight,
    output_gain,
    output_bias,
    output_weight,
):
    rows, tokens, channels = pair_state.shape
    slabs = lax.axis_size("row")
    tiles = tokens // LANES
    cells = rows * LANES
    start = (lax.axis_index("row") * rows).astype(jnp.int32).reshape(1)
    lane_mask = token_mask.reshape(1, tokens)
    gain, bias = input_gain.reshape(1, channels), input_bias.reshape(1, channels)
    out_gain, out_bias = output_gain.reshape(1, channels), output_bias.reshape(1, channels)
    smem = pl.BlockSpec(memory_space=pltpu.SMEM)
    lane_spec = pl.BlockSpec((1, LANES), lambda t: (0, t))
    cell_spec = pl.BlockSpec((rows, LANES, channels), lambda t: (0, t, 0))
    row_spec = whole((1, channels))
    column_spec = pl.BlockSpec((1, channels, cells), lambda t: (t, 0, 0))

    def wire_spec(height):
        return pl.BlockSpec((slabs, height, LANES), lambda t: (0, t, 0))

    pair = 2 * rows
    sent_factors = pl.pallas_call(
        front_kernel,
        name="front",
        grid=(tiles,),
        in_specs=[
            smem, smem, lane_spec, cell_spec, row_spec, row_spec,
            pl.BlockSpec((channels, 4 * channels), lambda t: (0, 0)),
        ],
        out_specs=wire_spec(2 * pair),
        out_shape=jax.ShapeDtypeStruct((slabs, 2 * pair * tiles, LANES), BF16),
        scratch_shapes=[
            pltpu.VMEM((4 * channels, channels), BF16),
            pltpu.VMEM((2, channels * rows, LANES), F32),
        ],
        compiler_params=params(),
        cost_estimate=cost(6 * 10**8, 4 * 10**6),
    )(start, token_mask, lane_mask, pair_state, gain, bias, input_weight)
    factors = exchange(sent_factors)

    h, coef, normed, mixed, gate_coef = pl.pallas_call(
        side_kernel,
        name="side",
        grid=(tiles,),
        in_specs=[
            smem, smem, lane_spec, cell_spec, cell_spec, row_spec, row_spec,
            whole((channels, 5 * channels)), row_spec, whole((channels, channels)),
        ],
        out_specs=[
            pl.BlockSpec((1, channels * rows, LANES), lambda t: (t, 0, 0)),
            pl.BlockSpec((1, 4, channels, cells), lambda t: (t, 0, 0, 0)),
            column_spec, column_spec, column_spec,
        ],
        out_shape=[
            jax.ShapeDtypeStruct((tiles, channels * rows, LANES), F32),
            jax.ShapeDtypeStruct((tiles, 4, channels, cells), F32),
            jax.ShapeDtypeStruct((tiles, channels, cells), BF16),
            jax.ShapeDtypeStruct((tiles, channels, cells), BF16),
            jax.ShapeDtypeStruct((tiles, channels, cells), F32),
        ],
        scratch_shapes=[pltpu.VMEM((5 * channels, channels), BF16)],
        compiler_params=params(),
        cost_estimate=cost(12 * 10**8, 20 * 10**6),
    )(start, token_mask, lane_mask, pair_state, cotangent, gain, bias, input_weight, out_gain, output_weight)

    sent_product = pl.pallas_call(
        product_kernel,
        name="product",
        in_specs=[whole((slabs, 2 * pair * tiles, LANES))],
        out_specs=whole((slabs, pair * tiles, LANES)),
        out_shape=jax.ShapeDtypeStruct((slabs, pair * tiles, LANES), BF16),
        scratch_shapes=[pltpu.VMEM((4, tokens, tokens), BF16)],
        compiler_params=params(),
        cost_estimate=cost(6 * 10**8, 3 * 10**6),
    )(factors)
    product = exchange(sent_product)

    factor_slab = pl.pallas_call(
        slab_unpack_kernel,
        name="slabs",
        in_specs=[whole((slabs, 2 * pair * tiles, LANES))],
        out_specs=whole((4, tokens, tokens)),
        out_shape=jax.ShapeDtypeStruct((4, tokens, tokens), BF16),
        compiler_params=params(),
        cost_estimate=cost(10**6, 4 * 10**6),
    )(factors)

    sent_grad = pl.pallas_call(
        product_grad_kernel,
        name="product_grad",
        grid=(tiles,),
        in_specs=[wire_spec(pair), pl.BlockSpec((1, channels * rows, LANES), lambda t: (t, 0, 0))],
        out_specs=wire_spec(pair),
        out_shape=jax.ShapeDtypeStruct((slabs, pair * tiles, LANES), BF16),
        compiler_params=params(),
        cost_estimate=cost(10**7, 4 * 10**6),
    )(product, h)
    grad = exchange(sent_grad)

    gate_normed, early_share = pl.pallas_call(
        gate_side_kernel,
        name="gate_side",
        grid=(tiles,),
        in_specs=[
            wire_spec(pair), column_spec, column_spec, column_spec, row_spec, row_spec,
            whole((channels, channels)),
            pl.BlockSpec((channels, channels), lambda t: (0, 4)),
        ],
        out_specs=[column_spec, whole((slabs, 8, LANES))],
        out_shape=[
            jax.ShapeDtypeStruct((tiles, channels, cells), F32),
            jax.ShapeDtypeStruct((slabs, 8, LANES), BF16),
        ],
        scratch_shapes=[
            pltpu.VMEM((channels * rows, LANES), F32),
            pltpu.VMEM((channels, channels), F32),
            pltpu.VMEM((channels, channels), F32),
            pltpu.VMEM((slabs * 8, LANES), F32),
        ],
        compiler_params=params(),
        cost_estimate=cost(6 * 10**8, 8 * 10**6),
    )(product, normed, mixed, gate_coef, out_gain, out_bias, output_weight, input_weight)

    height = 2 * pair * tiles + 8
    sent_parts = pl.pallas_call(
        factor_grad_kernel,
        name="factor_grad",
        in_specs=[
            whole((slabs, pair * tiles, LANES)),
            whole((4, tokens, tokens)),
            whole((slabs, 8, LANES)),
        ],
        out_specs=whole((slabs, height, LANES)),
        out_shape=jax.ShapeDtypeStruct((slabs, height, LANES), BF16),
        scratch_shapes=[pltpu.VMEM((2, tokens, tokens), BF16)],
        compiler_params=params(),
        cost_estimate=cost(11 * 10**8, 5 * 10**6),
    )(grad, factor_slab, early_share)
    parts = exchange(sent_parts)

    proj, late_share = pl.pallas_call(
        proj_grad_kernel,
        name="proj_grad",
        grid=(tiles,),
        in_specs=[
            wire_spec(2 * pair),
            pl.BlockSpec((1, 4, channels, cells), lambda t: (t, 0, 0, 0)),
            column_spec,
        ],
        out_specs=[
            pl.BlockSpec((1, 4 * channels, cells), lambda t: (t, 0, 0)),
            whole((slabs * 8, LANES)),
        ],
        out_shape=[
            jax.ShapeDtypeStruct((tiles, 4 * channels, cells), BF16),
            jax.ShapeDtypeStruct((slabs * 8, LANES), F32),
        ],
        scratch_shapes=[
            pltpu.VMEM((channels * rows, LANES), F32),
            pltpu.VMEM((4, channels, channels), F32),
        ],
        compiler_params=params(),
        cost_estimate=cost(6 * 10**8, 15 * 10**6),
    )(parts, coef, normed)
    late = exchange(late_share.reshape(slabs, 8, LANES))

    pair_gradient = pl.pallas_call(
        pair_grad_kernel,
        name="pair_grad",
        grid=(tiles,),
        in_specs=[
            pl.BlockSpec((1, 4 * channels, cells), lambda t: (t, 0, 0)),
            column_spec, cell_spec, row_spec,
            pl.BlockSpec((channels, 4 * channels), lambda t: (0, 0)),
        ],
        out_specs=cell_spec,
        out_shape=jax.ShapeDtypeStruct((rows, tokens, channels), BF16),
        compiler_params=params(),
        cost_estimate=cost(6 * 10**8, 8 * 10**6),
    )(proj, gate_normed, pair_state, gain, input_weight)

    last = 2 * pair * tiles // 8
    held = channels // slabs
    input_gradient, output_gradient = pl.pallas_call(
        lambda *refs: weight_sum_kernel(*refs, tokens=tokens),
        name="weight_sum",
        grid=(1,),
        in_specs=[whole((slabs, 8, LANES)), pl.BlockSpec((slabs, 8, LANES), lambda t: (0, last, 0))],
        out_specs=[whole((held, 5 * channels)), whole((held, channels))],
        out_shape=[
            jax.ShapeDtypeStruct((held, 5 * channels), F32),
            jax.ShapeDtypeStruct((held, channels), F32),
        ],
        compiler_params=params(),
        cost_estimate=cost(10**5, 4 * 10**5),
    )(late, parts)
    return (pair_gradient, input_gradient, output_gradient)


def solution(mesh):
    return jax.shard_map(
        on_device,
        mesh=mesh,
        in_specs=(
            P(("cplx", "row"), None, None),
            P(("cplx", "row"), None, None),
            P("cplx"),
            P(),
            P(),
            P(),
            P(),
            P(),
            P(),
        ),
        out_specs=(
            P(("cplx", "row"), None, None),
            P(("cplx", "row"), None),
            P(("cplx", "row"), None),
        ),
        check_vma=False,
    )
```

time: 880 us -> 241 us (0.27)
  waiting for transfers between devices: 669 us -> 44.7 us
  blocking collectives: 67.5 us -> 125 us
  Pallas kernels: 0 us -> 51 us
  local copies, waits for them, and re-layouts: 41.9 us -> 2.64 us
  other arithmetic: 27.9 us -> 0 us
  matrix products: 26.7 us -> 0 us
  starting transfers between devices: 31.1 us -> 16.4 us
  between operations: 15.1 us -> 0.67 us
    unnamed x2 -> x0, waiting for transfers between devices: 578 us -> none
    all_to_all x2, blocking collectives: 67.5 us -> 125 us  [exchange(): lax.all_to_all(values, 'row', split_axis=0, concat_axis=0, tiled=True)]
    pallas_call x0 -> x10, Pallas kernels: none -> 51 us  [the longest x1 8.09 us: on_device(): pl.pallas_call(side_kernel, name='side', grid=(tiles,), in_specs=[smem, s...]
    all_to_all x4 -> x3, waiting for transfers between devices: 90.7 us -> 44.7 us  [exchange(): lax.all_to_all(values, 'row', split_axis=0, concat_axis=0, tiled=True)]
    dot_general x11 -> x0, matrix products: 26.7 us -> none  [the longest x3 7.8 us: project(): jnp.einsum('rnd,de->ern', normed, weight_block, preferred_element_type=jn...]
    convert_element_type x7 -> x0, other arithmetic: 16.7 us -> none  [the longest x1 4.73 us: on_device(): (pair_mask * left_gate * left_lin).astype(jnp.bfloat16)]
    convert_element_type x6 -> x0, local copies, waits for them, and re-layouts: 16.2 us -> none  [the longest x2 4.11 us: factor_gradients(): return (left_part.astype(jnp.bfloat16), right_part.astype(jnp.bfloat16))]
    all_to_all x4 -> x3, starting transfers between devices: 31 us -> 16.4 us  [exchange(): lax.all_to_all(values, 'row', split_axis=0, concat_axis=0, tiled=True)]
  transfers between devices with their start and end apart: 5 -> 3, of which waited for: 5 -> 3; matrix products, arithmetic and copies ran while one was open for 3% -> 0% of each run, Pallas kernels for 0% -> 10%
where the time goes in v2:
time: 241 us; the launch traced here: 240 us
  blocking collectives  125 us (52%)
  Pallas kernels  51 us (21%)
  waiting for transfers between devices  44.7 us (19%)
  starting transfers between devices  16.4 us (7%)
  local copies, waits for them, and re-layouts  2.64 us (1%)
    all_to_all x2, blocking collectives, exchange(): lax.all_to_all(values, 'row', split_axis=0, concat_axis=0, tiled=True)  125 us
    all_to_all x3, waiting for transfers between devices, exchange(): lax.all_to_all(values, 'row', split_axis=0, concat_axis=0, tiled=True)  44.7 us
    all_to_all x3, starting transfers between devices, exchange(): lax.all_to_all(values, 'row', split_axis=0, concat_axis=0, tiled=True)  16.4 us
    pallas_call x1, Pallas kernels, on_device(): pl.pallas_call(side_kernel, name='side', grid=(tiles,), in_specs=[smem, s...  8.09 us
    pallas_call x1, Pallas kernels, on_device(): pl.pallas_call(proj_grad_kernel, name='proj_grad', grid=(tiles,), in_spec...  7.62 us
    pallas_call x1, Pallas kernels, on_device(): pl.pallas_call(gate_side_kernel, name='gate_side', grid=(tiles,), in_spec...  6.09 us
    pallas_call x1, Pallas kernels, on_device(): pl.pallas_call(pair_grad_kernel, name='pair_grad', grid=(tiles,), in_spec...  5.73 us
    pallas_call x1, Pallas kernels, on_device(): pl.pallas_call(front_kernel, name='front', grid=(tiles,), in_specs=[smem,...  5.67 us
  transfers between devices with their start and end apart: 3, of which 3 were waited for; matrix products, arithmetic and copies ran while one was open for 0% of the time, Pallas kernels for 10%

profile of v2, /device:TPU:16, one launch (start us, length us, event | category | flops | bytes accessed | tf_op | source)
XLA Modules:
  0.0 240.1 jit_solution(17771504145377137384)
XLA Ops:
  0.6 5.7 %front.1 = bf16[64,128,128]{2,1,0:T(8,128)(2,1)} custom-call(s32[1]{0:T(128)} %bitcast.start_ref, s32[512]{0:T(512)} %mask_ref.3, s32[1,512]{1,0:T(1,128)} %bitcast.8, bf16[8,512,128]{2,1,0:T(8,128)(2,1)} %x_ref.5, f32[1,128]{1,0:T(1,128)} %bitcast.10, f32[1,128]{1,0:T(1,128)} %bitcast.16, bf16[128,640]{1,0:T(8,128)(2,1)} %weight_ref.5), custom_call_target="tpu_custom_call" | custom-call | flops 600000000 | bytes 4000000 | tf_op jit(solution)/shard_map/front/pallas_call | solution.py:343
  6.3 64.0 %all_to_all.25.recv_ref = bf16[64,128,128]{2,1,0:T(8,128)(2,1)} all-to-all(bf16[64,128,128]{2,1,0:T(8,128)(2,1)} %front.1), channel_id=1, replica_groups=mesh['cplx'=4,'row'=64] {'row'}, dimensions={0} | all-to-all | bytes 4194304 | tf_op jit(solution)/shard_map/all_to_all | solution.py:303
  70.3 3.5 %product.1 = bf16[64,64,128]{2,1,0:T(8,128)(2,1)} custom-call(bf16[64,128,128]{2,1,0:T(8,128)(2,1)} %all_to_all.25.recv_ref), custom_call_target="tpu_custom_call" | custom-call | flops 600000000 | bytes 3000000 | tf_op jit(solution)/shard_map/product/pallas_call | solution.py:387
  73.7 6.0 %all-to-all-start.1 = ((bf16[64,64,128]{2,1,0:T(8,128)(2,1)}), bf16[64,64,128]{2,1,0:T(8,128)(2,1)S(1)}, u32[]{:S(2)}, u32[]{:S(2)}) async-start(bf16[64,64,128]{2,1,0:T(8,128)(2,1)} %product.1), calls=%async_computation.1 | async-start | bytes 2097152 | tf_op jit(solution)/shard_map/all_to_all | solution.py:303
  79.8 8.1 %side.1 = (f32[4,1024,128]{2,1,0:T(8,128)}, f32[4,4,128,1024]{3,2,1,0:T(8,128)}, bf16[4,128,1024]{2,1,0:T(8,128)(2,1)}, bf16[4,128,1024]{2,1,0:T(8,128)(2,1)}, f32[4,128,1024]{2,1,0:T(8,128)}) custom-call(s32[1]{0:T(128)} %bitcast.start_ref, s32[512]{0:T(512)} %mask_ref.3, s32[1,512]{1,0:T(1,128)} %bitcast.9, bf16[8,512,128]{2,1,0:T(8,128)(2,1)} %x_ref.5, ...), custom_call_target="tpu_custom_call" | custom-call | flops 1200000000 | bytes 20000000 | tf_op jit(solution)/shard_map/side/pallas_call | solution.py:362
  87.9 19.8 %all-to-all-done.1.recv_ref = bf16[64,64,128]{2,1,0:T(8,128)(2,1)S(1)} async-done(((bf16[64,64,128]{2,1,0:T(8,128)(2,1)}), bf16[64,64,128]{2,1,0:T(8,128)(2,1)S(1)}, u32[]{:S(2)}, u32[]{:S(2)}) %all-to-all-start.1) | async-done | bytes 1048608 | tf_op jit(solution)/shard_map/all_to_all | solution.py:303
  107.6 0.0 copy-start
  107.6 1.0 copy-done
  108.6 4.8 %product_grad.1 = bf16[64,64,128]{2,1,0:T(8,128)(2,1)} custom-call(bf16[64,64,128]{2,1,0:T(8,128)(2,1)} %copy-done, f32[4,1024,128]{2,1,0:T(8,128)} %get-tuple-element.14.h_ref), custom_call_target="tpu_custom_call" | custom-call | flops 10000000 | bytes 4000000 | tf_op jit(solution)/shard_map/product_grad/pallas_call | solution.py:409
  113.4 5.8 %all-to-all-start.2 = ((bf16[64,64,128]{2,1,0:T(8,128)(2,1)}), bf16[64,64,128]{2,1,0:T(8,128)(2,1)S(1)}, u32[]{:S(2)}, u32[]{:S(2)}) async-start(bf16[64,64,128]{2,1,0:T(8,128)(2,1)} %product_grad.1), calls=%async_computation.2 | async-start | bytes 2097152 | tf_op jit(solution)/shard_map/all_to_all | solution.py:303
  119.2 3.3 %slabs.1.factor_ref = bf16[4,512,512]{2,1,0:T(8,128)(2,1)} custom-call(bf16[64,128,128]{2,1,0:T(8,128)(2,1)} %all_to_all.25.recv_ref), custom_call_target="tpu_custom_call" | custom-call | flops 1000000 | bytes 4000000 | tf_op jit(solution)/shard_map/slabs/pallas_call | solution.py:399
  122.5 6.1 %gate_side.1 = (f32[4,128,1024]{2,1,0:T(8,128)}, bf16[64,8,128]{2,1,0:T(8,128)(2,1)}) custom-call(bf16[64,64,128]{2,1,0:T(8,128)(2,1)} %copy-done, bf16[4,128,1024]{2,1,0:T(8,128)(2,1)} %get-tuple-element.15.normed_ref, bf16[4,128,1024]{2,1,0:T(8,128)(2,1)} %get-tuple-element.16.mixed_ref, f32[4,128,1024]{2,1,0:T(8,128)} %get-tuple-element.17.gate_coef_ref, ...), custom_call_target="tpu_custom_call" | custom-call | flops 600000000 | bytes 8000000 | tf_op jit(solution)/shard_map/gate_side/pallas_call | solution.py:421
  128.6 18.4 %all-to-all-done.2.recv_ref = bf16[64,64,128]{2,1,0:T(8,128)(2,1)S(1)} async-done(((bf16[64,64,128]{2,1,0:T(8,128)(2,1)}), bf16[64,64,128]{2,1,0:T(8,128)(2,1)S(1)}, u32[]{:S(2)}, u32[]{:S(2)}) %all-to-all-start.2) | async-done | bytes 1048608 | tf_op jit(solution)/shard_map/all_to_all | solution.py:303
  147.0 0.0 copy-start.1
  147.0 1.0 copy-done.1
  148.0 4.5 %factor_grad.1 = bf16[64,136,128]{2,1,0:T(8,128)(2,1)} custom-call(bf16[64,64,128]{2,1,0:T(8,128)(2,1)} %copy-done.1, bf16[4,512,512]{2,1,0:T(8,128)(2,1)} %slabs.1.factor_ref, bf16[64,8,128]{2,1,0:T(8,128)(2,1)} %get-tuple-element.18.share_ref), custom_call_target="tpu_custom_call" | custom-call | flops 1100000000 | bytes 5000000 | tf_op jit(solution)/shard_map/factor_grad/pallas_call | solution.py:446
  152.5 60.7 %all_to_all.26.recv_ref.refs_1_ = bf16[64,136,128]{2,1,0:T(8,128)(2,1)} all-to-all(bf16[64,136,128]{2,1,0:T(8,128)(2,1)} %factor_grad.1), channel_id=1, replica_groups=mesh['cplx'=4,'row'=64] {'row'}, dimensions={0} | all-to-all | bytes 4456448 | tf_op jit(solution)/shard_map/all_to_all | solution.py:303
  213.3 7.6 %proj_grad.1 = (bf16[4,512,1024]{2,1,0:T(8,128)(2,1)}, f32[512,128]{1,0:T(8,128)}) custom-call(bf16[64,136,128]{2,1,0:T(8,128)(2,1)} %all_to_all.26.recv_ref.refs_1_, f32[4,4,128,1024]{3,2,1,0:T(8,128)} %get-tuple-element.19.coef_ref, bf16[4,128,1024]{2,1,0:T(8,128)(2,1)} %get-tuple-element.15.normed_ref), custom_call_target="tpu_custom_call" | custom-call | flops 600000000 | bytes 15000000 | tf_op jit(solution)/shard_map/proj_grad/pallas_call | solution.py:462
  220.9 4.6 %all-to-all-start.4 = ((f32[64,8,128]{2,1,0:T(8,128)}), f32[64,8,128]{2,1,0:T(8,128)S(1)}, u32[]{:S(2)}, u32[]{:S(2)}) async-start(f32[64,8,128]{2,1,0:T(8,128)} %bitcast.7), calls=%async_computation.4 | async-start | bytes 524288 | tf_op jit(solution)/shard_map/all_to_all | solution.py:303
  225.5 5.7 %pair_grad.1 = bf16[8,512,128]{2,1,0:T(8,128)(2,1)} custom-call(bf16[4,512,1024]{2,1,0:T(8,128)(2,1)} %get-tuple-element.20.proj_ref, f32[4,128,1024]{2,1,0:T(8,128)} %get-tuple-element.21.gate_normed_ref, bf16[8,512,128]{2,1,0:T(8,128)(2,1)} %x_ref.5, f32[1,128]{1,0:T(1,128)} %bitcast.12, bf16[128,640]{1,0:T(8,128)(2,1)} %weight_ref.5), custom_call_target="tpu_custom_call" | custom-call | flops 600000000 | bytes 8000000 | tf_op jit(solution)/shard_map/pair_grad/pallas_call | solution.py:488
  231.2 6.5 %all-to-all-done.4.refs_0_ = f32[64,8,128]{2,1,0:T(8,128)S(1)} async-done(((f32[64,8,128]{2,1,0:T(8,128)}), f32[64,8,128]{2,1,0:T(8,128)S(1)}, u32[]{:S(2)}, u32[]{:S(2)}) %all-to-all-start.4) | async-done | bytes 262176 | tf_op jit(solution)/shard_map/all_to_all | solution.py:303
  237.7 0.0 copy-start.2
  237.7 0.7 copy-done.2
  238.4 1.7 weight_sum.1
Async XLA Ops:
  73.7 33.9 %all-to-all-start.1 = ((bf16[64,64,128]{2,1,0:T(8,128)(2,1)}), bf16[64,64,128]{2,1,0:T(8,128)(2,1)S(1)}, u32[]{:S(2)}, u32[]{:S(2)}) async-start(bf16[64,64,128]{2,1,0:T(8,128)(2,1)} %product.1), calls=%async_computation.1 | async-start | bytes 2097152 | tf_op jit(solution)/shard_map/all_to_all | solution.py:303
  107.6 1.0 copy-start
  113.4 33.6 %all-to-all-start.2 = ((bf16[64,64,128]{2,1,0:T(8,128)(2,1)}), bf16[64,64,128]{2,1,0:T(8,128)(2,1)S(1)}, u32[]{:S(2)}, u32[]{:S(2)}) async-start(bf16[64,64,128]{2,1,0:T(8,128)(2,1)} %product_grad.1), calls=%async_computation.2 | async-start | bytes 2097152 | tf_op jit(solution)/shard_map/all_to_all | solution.py:303
  147.0 1.0 copy-start.1
  220.9 16.9 %all-to-all-start.4 = ((f32[64,8,128]{2,1,0:T(8,128)}), f32[64,8,128]{2,1,0:T(8,128)S(1)}, u32[]{:S(2)}, u32[]{:S(2)}) async-start(f32[64,8,128]{2,1,0:T(8,128)} %bitcast.7), calls=%async_computation.4 | async-start | bytes 524288 | tf_op jit(solution)/shard_map/all_to_all | solution.py:303
  237.7 0.7 copy-start.2

commit v3 on v2

--- a/solution.py
+++ b/solution.py
@@ -77,8 +77,12 @@
     def _():
         turned_weight[...] = weight_ref[...].astype(F32).T.astype(BF16)
 
-    normed, _, _ = normed_columns(x_ref[...], gain_ref[...], bias_ref[...])
-    pair_mask = mask_row(start_ref, mask_ref, lane_mask_ref[...], rows)
+    gain, bias = as_column(gain_ref[...]), as_column(bias_ref[...])
+    lane_mask = lane_mask_ref[...].astype(F32)
+    scaled, _ = norm_columns(turned(x_ref[...]))
+    normed = (scaled * gain + bias).astype(BF16)
+    masks = [lane_mask * mask_ref[start_ref[0] + row].astype(F32) for row in range(rows)]
+    pair_mask = jnp.concatenate(masks, axis=1)
     for side in range(2):
         base = 2 * side * channels
         pre = dot_nn(turned_weight[base : base + 2 * channels, :], normed)
@@ -87,7 +91,8 @@
             spread[side, pl.ds(row, channels, stride=rows), :] = factor[
                 :, row * LANES : (row + 1) * LANES
             ]
-        group = channels * rows // out_ref.shape[0]
+    group = channels * rows // out_ref.shape[0]
+    for side in range(2):
         out_ref[:, side * group : (side + 1) * group, :] = (
             spread[side].reshape(out_ref.shape[0], group, LANES).astype(BF16)
         )
@@ -97,7 +102,7 @@
     start_ref, mask_ref, lane_mask_ref, x_ref, cot_ref, gain_ref, bias_ref, weight_ref,
     out_gain_ref, out_weight_ref,
     h_ref, coef_ref, normed_ref, mixed_ref, gate_coef_ref,
-    turned_weight,
+    turned_weight, spread,
 ):
     rows = x_ref.shape[0]
     channels = x_ref.shape[2]
@@ -113,16 +118,19 @@
         base = 2 * side * channels
         pre = dot_nn(turned_weight[base : base + 2 * channels, :], normed)
         gate = jax.nn.sigmoid(pre[channels:])
-        coef_ref[0, 2 * side] = pair_mask * gate
-        coef_ref[0, 2 * side + 1] = pair_mask * pre[:channels] * gate * (1.0 - gate)
+        coef_ref[0, 2 * side] = (pair_mask * gate).astype(BF16)
+        slope = pair_mask * pre[:channels] * gate * (1.0 - gate)
+        coef_ref[0, 2 * side + 1] = slope.astype(BF16)
     out_gate = jax.nn.sigmoid(dot_nn(turned_weight[4 * channels :, :], normed))
     upstream = turned(cot_ref[...])
     mixed = (upstream * out_gate).astype(BF16)
     mixed_ref[0] = mixed
     gate_coef_ref[0] = upstream * out_gate * (1.0 - out_gate)
     h = dot_nn(out_weight_ref[...], mixed) * as_column(out_gain_ref[...])
+    h = h - jnp.mean(h, axis=0, keepdims=True)
     for row in range(rows):
-        h_ref[0, pl.ds(row, channels, stride=rows), :] = h[:, row * LANES : (row + 1) * LANES]
+        spread[pl.ds(row, channels, stride=rows), :] = h[:, row * LANES : (row + 1) * LANES]
+    h_ref[0] = spread[...].astype(BF16)
 
 
 def unpack(recv_ref, base, rows):
@@ -164,14 +172,39 @@
         )
 
 
-def product_grad_kernel(recv_ref, h_ref, out_ref):
-    slabs, group, _ = recv_ref.shape
-    rows = h_ref.shape[1] // (2 * slabs)
-    product = recv_ref[...].astype(F32).reshape(2 * slabs, rows, LANES)
-    h = h_ref[0].reshape(2 * slabs, rows, LANES)
-    scaled, inverse = norm_columns(product)
-    grad = norm_columns_backward(h, scaled, inverse)
-    out_ref[...] = grad.reshape(slabs, group, LANES).astype(BF16)
+def product_grad_kernel(recv_ref, h_ref, factor_hbm, out_ref):
+    del factor_hbm
+    slabs, group, _ = out_ref.shape
+    rows = group // 2
+    channels = 2 * slabs
+    base = pl.multiple_of(pl.program_id(0) * group, group)
+    chunk = 8
+
+    def product_at(at):
+        block = recv_ref[at : at + chunk, pl.ds(base, group), :].astype(F32)
+        return block.reshape(2 * chunk, rows, LANES)
+
+    def h_at(at):
+        size = 2 * chunk * rows
+        block = h_ref[0, at * group : at * group + size, :].astype(F32)
+        return block.reshape(2 * chunk, rows, LANES)
+
+    total = jnp.zeros((rows, LANES), F32)
+    for at in range(0, slabs, chunk):
+        total = total + jnp.sum(product_at(at), axis=0)
+    average = (total / channels)[None]
+    squares = jnp.zeros((rows, LANES), F32)
+    cross = jnp.zeros((rows, LANES), F32)
+    for at in range(0, slabs, chunk):
+        centered = product_at(at) - average
+        squares = squares + jnp.sum(centered * centered, axis=0)
+        cross = cross + jnp.sum(centered * h_at(at), axis=0)
+    inverse = lax.rsqrt(squares / channels + epsilon)
+    slope = (inverse * inverse * inverse * (cross / channels))[None]
+    inverse = inverse[None]
+    for at in range(0, slabs, chunk):
+        grad = inverse * h_at(at) - (product_at(at) - average) * slope
+        out_ref[at : at + chunk] = grad.reshape(chunk, group, LANES).astype(BF16)
 
 
 def gather_rows(spread, channels, rows):
@@ -189,13 +222,15 @@
     step = pl.program_id(0)
     channels = normed_ref.shape[1]
     rows = normed_ref.shape[2] // LANES
+    group = channels * rows // recv_ref.shape[0]
+    block = recv_ref[:, pl.ds(pl.multiple_of(step * group, group), group), :]
 
     @pl.when(step == 0)
     def _():
         gate_term[...] = jnp.zeros_like(gate_term)
         out_term[...] = jnp.zeros_like(out_term)
 
-    spread[...] = recv_ref[...].astype(F32).reshape(channels * rows, LANES)
+    spread[...] = block.astype(F32).reshape(channels * rows, LANES)
     product = gather_rows(spread, channels, rows)
     scaled, _ = norm_columns(product)
     normed_out = (scaled * as_column(out_gain_ref[...]) + as_column(out_bias_ref[...])).astype(BF16)
@@ -217,19 +252,27 @@
         share_ref[...] = laid[...].reshape(half, 8, LANES).astype(BF16)
 
 
-def factor_grad_kernel(recv_ref, factor_ref, share_ref, out_ref, slab):
+def factor_grad_kernel(recv_ref, factor_hbm, share_ref, out_ref, slab, factor, arrived):
     slabs = recv_ref.shape[0]
     tokens = slab.shape[1]
     rows = tokens // slabs
+    loads = [
+        pltpu.make_async_copy(factor_hbm.at[which], factor.at[which], arrived.at[which])
+        for which in range(4)
+    ]
+    for which in (2, 3, 0, 1):
+        loads[which].start()
     for tile in range(tokens // LANES):
         parts = unpack(recv_ref, tile * 2 * rows, rows)
         for part in range(2):
             slab[part, :, tile * LANES : (tile + 1) * LANES] = parts[part]
     for side in range(2):
-        if side == 0:
-            grads = [dot_nn(slab[part], factor_ref[2 + part]) for part in range(2)]
-        else:
-            grads = [dot_tn(slab[part], factor_ref[part]) for part in range(2)]
+        grads = []
+        for part in range(2):
+            which = 2 + part if side == 0 else part
+            loads[which].wait()
+            dot = dot_nn if side == 0 else dot_tn
+            grads.append(dot(slab[part], factor[which]))
         for tile in range(tokens // LANES):
             cols = slice(tile * LANES, (tile + 1) * LANES)
             base = (tile * 2 + side) * 2 * rows
@@ -240,28 +283,36 @@
     out_ref[:, base : base + 8, :] = share_ref[...]
 
 
-def proj_grad_kernel(recv_ref, coef_ref, normed_ref, proj_ref, share_ref, spread, term):
+def proj_blocks(recv_ref, coef_ref, spread, rows):
+    step = pl.program_id(0)
+    channels = coef_ref.shape[2]
+    group = channels * rows // recv_ref.shape[0]
+    base = pl.multiple_of(step * 2 * group, 2 * group)
+    for side in range(2):
+        spread[side] = (
+            recv_ref[:, pl.ds(base + side * group, group), :]
+            .astype(F32)
+            .reshape(channels * rows, LANES)
+        )
+    blocks = []
+    for side in range(2):
+        grad = gather_rows(spread.at[side], channels, rows)
+        for part in range(2):
+            blocks.append((grad * coef_ref[0, 2 * side + part].astype(F32)).astype(BF16))
+    return blocks
+
+
+def proj_grad_kernel(recv_ref, coef_ref, normed_ref, share_ref, spread, term):
     step = pl.program_id(0)
     channels = normed_ref.shape[1]
     rows = normed_ref.shape[2] // LANES
-    group = recv_ref.shape[1] // 2
 
     @pl.when(step == 0)
     def _():
         term[...] = jnp.zeros_like(term)
 
-    for side in range(2):
-        spread[...] = (
-            recv_ref[:, side * group : (side + 1) * group, :]
-            .astype(F32)
-            .reshape(channels * rows, LANES)
-        )
-        grad = gather_rows(spread, channels, rows)
-        for part in range(2):
-            block = 2 * side + part
-            value = (grad * coef_ref[0, block]).astype(BF16)
-            proj_ref[0, block * channels : (block + 1) * channels, :] = value
-            term[block] += dot_nt(normed_ref[0], value)
+    for block, value in enumerate(proj_blocks(recv_ref, coef_ref, spread, rows)):
+        term[block] += dot_nt(normed_ref[0], value)
 
     @pl.when(step == pl.num_programs(0) - 1)
     def _():
@@ -273,18 +324,22 @@
                 ]
 
 
-def pair_grad_kernel(proj_ref, gate_normed_ref, x_ref, gain_ref, weight_ref, out_ref):
+def pair_grad_kernel(
+    recv_ref, coef_ref, gate_normed_ref, x_ref, gain_ref, weight_ref, out_ref, spread
+):
     rows = x_ref.shape[0]
+    blocks = proj_blocks(recv_ref, coef_ref, spread, rows)
     scaled, inverse = norm_columns(turned(x_ref[...]))
-    normed_grad = dot_nn(weight_ref[...], proj_ref[0]) + gate_normed_ref[0]
+    normed_grad = dot_nn(weight_ref[...], jnp.concatenate(blocks, axis=0)) + gate_normed_ref[0]
     grad = norm_columns_backward(normed_grad * as_column(gain_ref[...]), scaled, inverse)
     for row in range(rows):
         out_ref[row] = grad[:, row * LANES : (row + 1) * LANES].T.astype(BF16)
 
 
 def weight_sum_kernel(recv_ref, early_ref, in_ref, out_ref, *, tokens):
+    last = early_ref.shape[1] - 8
     late = jnp.sum(recv_ref[...], axis=0) / tokens
-    early = jnp.sum(early_ref[...].astype(F32), axis=0) / tokens
+    early = jnp.sum(early_ref[:, last:, :].astype(F32), axis=0) / tokens
     for part in range(2):
         for block in range(4):
             in_ref[part : part + 1, block * LANES : (block + 1) * LANES] = late[
@@ -303,8 +358,12 @@
     return lax.all_to_all(values, "row", split_axis=0, concat_axis=0, tiled=True)
 
 
-def params(**kwargs):
-    return pltpu.CompilerParams(vmem_limit_bytes=56 * 1024 * 1024, **kwargs)
+def params(megabytes):
+    return pltpu.CompilerParams(vmem_limit_bytes=megabytes * 1024 * 1024)
+
+
+def pinned(*arrays):
+    return [pltpu.with_memory_space_constraint(array, pltpu.HBM) for array in arrays]
 
 
 def cost(flops, moved):
@@ -340,13 +399,20 @@
         return pl.BlockSpec((slabs, height, LANES), lambda t: (0, t, 0))
 
     pair = 2 * rows
+    vmem = pl.BlockSpec(memory_space=pltpu.VMEM)
+    h_spec = pl.BlockSpec((1, channels * rows, LANES), lambda t: (t, 0, 0))
+    coef_spec = pl.BlockSpec((1, 4, channels, cells), lambda t: (t, 0, 0, 0))
+    factor_weight_spec = pl.BlockSpec((channels, 4 * channels), lambda t: (0, 0))
+    pair_hbm, cot_hbm, lane_hbm, gain, bias, out_gain, out_bias, weight, out_weight = pinned(
+        pair_state, cotangent, lane_mask, gain, bias, out_gain, out_bias, input_weight, output_weight
+    )
+
     sent_factors = pl.pallas_call(
         front_kernel,
         name="front",
         grid=(tiles,),
         in_specs=[
-            smem, smem, lane_spec, cell_spec, row_spec, row_spec,
-            pl.BlockSpec((channels, 4 * channels), lambda t: (0, 0)),
+            smem, smem, lane_spec, cell_spec, row_spec, row_spec, factor_weight_spec,
         ],
         out_specs=wire_spec(2 * pair),
         out_shape=jax.ShapeDtypeStruct((slabs, 2 * pair * tiles, LANES), BF16),
@@ -354,9 +420,9 @@
             pltpu.VMEM((4 * channels, channels), BF16),
             pltpu.VMEM((2, channels * rows, LANES), F32),
         ],
-        compiler_params=params(),
+        compiler_params=params(16),
         cost_estimate=cost(6 * 10**8, 4 * 10**6),
-    )(start, token_mask, lane_mask, pair_state, gain, bias, input_weight)
+    )(start, token_mask, lane_hbm, pair_hbm, gain, bias, weight)
     factors = exchange(sent_factors)
 
     h, coef, normed, mixed, gate_coef = pl.pallas_call(
@@ -367,31 +433,31 @@
             smem, smem, lane_spec, cell_spec, cell_spec, row_spec, row_spec,
             whole((channels, 5 * channels)), row_spec, whole((channels, channels)),
         ],
-        out_specs=[
-            pl.BlockSpec((1, channels * rows, LANES), lambda t: (t, 0, 0)),
-            pl.BlockSpec((1, 4, channels, cells), lambda t: (t, 0, 0, 0)),
-            column_spec, column_spec, column_spec,
-        ],
+        out_specs=[h_spec, coef_spec, column_spec, column_spec, column_spec],
         out_shape=[
-            jax.ShapeDtypeStruct((tiles, channels * rows, LANES), F32),
-            jax.ShapeDtypeStruct((tiles, 4, channels, cells), F32),
-            jax.ShapeDtypeStruct((tiles, channels, cells), BF16),
-            jax.ShapeDtypeStruct((tiles, channels, cells), BF16),
-            jax.ShapeDtypeStruct((tiles, channels, cells), F32),
-        ],
-        scratch_shapes=[pltpu.VMEM((5 * channels, channels), BF16)],
-        compiler_params=params(),
-        cost_estimate=cost(12 * 10**8, 20 * 10**6),
-    )(start, token_mask, lane_mask, pair_state, cotangent, gain, bias, input_weight, out_gain, output_weight)
+            pltpu.HBM((tiles, channels * rows, LANES), BF16),
+            pltpu.HBM((tiles, 4, channels, cells), BF16),
+            pltpu.HBM((tiles, channels, cells), BF16),
+            pltpu.HBM((tiles, channels, cells), BF16),
+            pltpu.HBM((tiles, channels, cells), F32),
+        ],
+        scratch_shapes=[
+            pltpu.VMEM((5 * channels, channels), BF16),
+            pltpu.VMEM((channels * rows, LANES), F32),
+        ],
+        compiler_params=params(40),
+        cost_estimate=cost(12 * 10**8, 16 * 10**6),
+    )(start, token_mask, lane_hbm, pair_hbm, cot_hbm, gain, bias, weight, out_gain, out_weight)
+    h, coef, normed, mixed, gate_coef = pinned(h, coef, normed, mixed, gate_coef)
 
     sent_product = pl.pallas_call(
         product_kernel,
         name="product",
-        in_specs=[whole((slabs, 2 * pair * tiles, LANES))],
+        in_specs=[vmem],
         out_specs=whole((slabs, pair * tiles, LANES)),
-        out_shape=jax.ShapeDtypeStruct((slabs, pair * tiles, LANES), BF16),
+        out_shape=pltpu.HBM((slabs, pair * tiles, LANES), BF16),
         scratch_shapes=[pltpu.VMEM((4, tokens, tokens), BF16)],
-        compiler_params=params(),
+        compiler_params=params(20),
         cost_estimate=cost(6 * 10**8, 3 * 10**6),
     )(factors)
     product = exchange(sent_product)
@@ -399,23 +465,24 @@
     factor_slab = pl.pallas_call(
         slab_unpack_kernel,
         name="slabs",
-        in_specs=[whole((slabs, 2 * pair * tiles, LANES))],
+        in_specs=[vmem],
         out_specs=whole((4, tokens, tokens)),
-        out_shape=jax.ShapeDtypeStruct((4, tokens, tokens), BF16),
-        compiler_params=params(),
+        out_shape=pltpu.HBM((4, tokens, tokens), BF16),
+        compiler_params=params(20),
         cost_estimate=cost(10**6, 4 * 10**6),
     )(factors)
+    (factor_slab,) = pinned(factor_slab)
 
     sent_grad = pl.pallas_call(
         product_grad_kernel,
         name="product_grad",
         grid=(tiles,),
-        in_specs=[wire_spec(pair), pl.BlockSpec((1, channels * rows, LANES), lambda t: (t, 0, 0))],
+        in_specs=[vmem, h_spec, pl.BlockSpec(memory_space=pl.ANY)],
         out_specs=wire_spec(pair),
-        out_shape=jax.ShapeDtypeStruct((slabs, pair * tiles, LANES), BF16),
-        compiler_params=params(),
+        out_shape=pltpu.HBM((slabs, pair * tiles, LANES), BF16),
+        compiler_params=params(16),
         cost_estimate=cost(10**7, 4 * 10**6),
-    )(product, h)
+    )(product, h, factor_slab)
     grad = exchange(sent_grad)
 
     gate_normed, early_share = pl.pallas_call(
@@ -423,14 +490,14 @@
         name="gate_side",
         grid=(tiles,),
         in_specs=[
-            wire_spec(pair), column_spec, column_spec, column_spec, row_spec, row_spec,
+            vmem, column_spec, column_spec, column_spec, row_spec, row_spec,
             whole((channels, channels)),
             pl.BlockSpec((channels, channels), lambda t: (0, 4)),
         ],
         out_specs=[column_spec, whole((slabs, 8, LANES))],
         out_shape=[
-            jax.ShapeDtypeStruct((tiles, channels, cells), F32),
-            jax.ShapeDtypeStruct((slabs, 8, LANES), BF16),
+            pltpu.HBM((tiles, channels, cells), F32),
+            pltpu.HBM((slabs, 8, LANES), BF16),
         ],
         scratch_shapes=[
             pltpu.VMEM((channels * rows, LANES), F32),
@@ -438,50 +505,41 @@
             pltpu.VMEM((channels, channels), F32),
             pltpu.VMEM((slabs * 8, LANES), F32),
         ],
-        compiler_params=params(),
+        compiler_params=params(24),
         cost_estimate=cost(6 * 10**8, 8 * 10**6),
-    )(product, normed, mixed, gate_coef, out_gain, out_bias, output_weight, input_weight)
+    )(product, normed, mixed, gate_coef, out_gain, out_bias, out_weight, weight)
+    gate_normed, early_share = pinned(gate_normed, early_share)
 
     height = 2 * pair * tiles + 8
     sent_parts = pl.pallas_call(
         factor_grad_kernel,
         name="factor_grad",
-        in_specs=[
-            whole((slabs, pair * tiles, LANES)),
-            whole((4, tokens, tokens)),
-            whole((slabs, 8, LANES)),
-        ],
-        out_specs=whole((slabs, height, LANES)),
+        in_specs=[vmem, pl.BlockSpec(memory_space=pl.ANY), whole((slabs, 8, LANES))],
+        out_specs=vmem,
         out_shape=jax.ShapeDtypeStruct((slabs, height, LANES), BF16),
-        scratch_shapes=[pltpu.VMEM((2, tokens, tokens), BF16)],
-        compiler_params=params(),
+        scratch_shapes=[
+            pltpu.VMEM((2, tokens, tokens), BF16),
+            pltpu.VMEM((4, tokens, tokens), BF16),
+            pltpu.SemaphoreType.DMA((4,)),
+        ],
+        compiler_params=params(20),
         cost_estimate=cost(11 * 10**8, 5 * 10**6),
     )(grad, factor_slab, early_share)
     parts = exchange(sent_parts)
 
-    proj, late_share = pl.pallas_call(
+    late_share = pl.pallas_call(
         proj_grad_kernel,
         name="proj_grad",
         grid=(tiles,),
-        in_specs=[
-            wire_spec(2 * pair),
-            pl.BlockSpec((1, 4, channels, cells), lambda t: (t, 0, 0, 0)),
-            column_spec,
-        ],
-        out_specs=[
-            pl.BlockSpec((1, 4 * channels, cells), lambda t: (t, 0, 0)),
-            whole((slabs * 8, LANES)),
-        ],
-        out_shape=[
-            jax.ShapeDtypeStruct((tiles, 4 * channels, cells), BF16),
-            jax.ShapeDtypeStruct((slabs * 8, LANES), F32),
-        ],
+        in_specs=[vmem, coef_spec, column_spec],
+        out_specs=whole((slabs * 8, LANES)),
+        out_shape=pltpu.HBM((slabs * 8, LANES), F32),
         scratch_shapes=[
-            pltpu.VMEM((channels * rows, LANES), F32),
+            pltpu.VMEM((2, channels * rows, LANES), F32),
             pltpu.VMEM((4, channels, channels), F32),
         ],
-        compiler_params=params(),
-        cost_estimate=cost(6 * 10**8, 15 * 10**6),
+        compiler_params=params(24),
+        cost_estimate=cost(6 * 10**8, 8 * 10**6),
     )(parts, coef, normed)
     late = exchange(late_share.reshape(slabs, 8, LANES))
 
@@ -489,30 +547,25 @@
         pair_grad_kernel,
         name="pair_grad",
         grid=(tiles,),
-        in_specs=[
-            pl.BlockSpec((1, 4 * channels, cells), lambda t: (t, 0, 0)),
-            column_spec, cell_spec, row_spec,
-            pl.BlockSpec((channels, 4 * channels), lambda t: (0, 0)),
-        ],
+        in_specs=[vmem, coef_spec, column_spec, cell_spec, row_spec, factor_weight_spec],
         out_specs=cell_spec,
-        out_shape=jax.ShapeDtypeStruct((rows, tokens, channels), BF16),
-        compiler_params=params(),
+        out_shape=pltpu.HBM((rows, tokens, channels), BF16),
+        scratch_shapes=[pltpu.VMEM((2, channels * rows, LANES), F32)],
+        compiler_params=params(24),
         cost_estimate=cost(6 * 10**8, 8 * 10**6),
-    )(proj, gate_normed, pair_state, gain, input_weight)
-
-    last = 2 * pair * tiles // 8
+    )(parts, coef, gate_normed, pair_hbm, gain, weight)
+
     held = channels // slabs
     input_gradient, output_gradient = pl.pallas_call(
         lambda *refs: weight_sum_kernel(*refs, tokens=tokens),
         name="weight_sum",
-        grid=(1,),
-        in_specs=[whole((slabs, 8, LANES)), pl.BlockSpec((slabs, 8, LANES), lambda t: (0, last, 0))],
+        in_specs=[vmem, vmem],
         out_specs=[whole((held, 5 * channels)), whole((held, channels))],
         out_shape=[
-            jax.ShapeDtypeStruct((held, 5 * channels), F32),
-            jax.ShapeDtypeStruct((held, channels), F32),
-        ],
-        compiler_params=params(),
+            pltpu.HBM((held, 5 * channels), F32),
+            pltpu.HBM((held, channels), F32),
+        ],
+        compiler_params=params(16),
         cost_estimate=cost(10**5, 4 * 10**5),
     )(late, parts)
     return (pair_gradient, input_gradient, output_gradient)

time: 241 us -> 230 us (0.954)
  Pallas kernels: 51 us -> 42.2 us
  local copies, waits for them, and re-layouts: 2.64 us -> 0 us
    pallas_call x3, Pallas kernels: 11.3 us -> 7.52 us  [the longest x1 3.86 us: on_device(): pl.pallas_call(factor_grad_kernel, name='factor_grad', in_specs=[vmem, pl...]
    unnamed x6 -> x0, local copies, waits for them, and re-layouts: 2.64 us -> none
where the time goes in v3:
time: 230 us; the launch traced here: 229 us
  blocking collectives  124 us (54%)
  waiting for transfers between devices  46.1 us (20%)
  Pallas kernels  42.2 us (18%)
  starting transfers between devices  16.4 us (7%)
    all_to_all x2, blocking collectives, exchange(): lax.all_to_all(values, 'row', split_axis=0, concat_axis=0, tiled=True)  124 us
    all_to_all x3, waiting for transfers between devices, exchange(): lax.all_to_all(values, 'row', split_axis=0, concat_axis=0, tiled=True)  46.1 us
    all_to_all x3, starting transfers between devices, exchange(): lax.all_to_all(values, 'row', split_axis=0, concat_axis=0, tiled=True)  16.4 us
    pallas_call x1, Pallas kernels, on_device(): pl.pallas_call(side_kernel, name='side', grid=(tiles,), in_specs=[smem, s...  7.61 us
    pallas_call x1, Pallas kernels, on_device(): pl.pallas_call(pair_grad_kernel, name='pair_grad', grid=(tiles,), in_spec...  6.49 us
    pallas_call x1, Pallas kernels, on_device(): pl.pallas_call(gate_side_kernel, name='gate_side', grid=(tiles,), in_spec...  5.98 us
    pallas_call x1, Pallas kernels, on_device(): pl.pallas_call(proj_grad_kernel, name='proj_grad', grid=(tiles,), in_spec...  5.24 us
    pallas_call x1, Pallas kernels, on_device(): pl.pallas_call(front_kernel, name='front', grid=(tiles,), in_specs=[smem,...  4.77 us
  transfers between devices with their start and end apart: 3, of which 3 were waited for; matrix products, arithmetic and copies ran while one was open for 0% of the time, Pallas kernels for 10%

profile of v3, /device:TPU:16, one launch (start us, length us, event | category | flops | bytes accessed | tf_op | source)
XLA Modules:
  0.0 229.5 jit_solution(8261148666596106006)
XLA Ops:
  0.6 4.8 %front.1 = bf16[64,128,128]{2,1,0:T(8,128)(2,1)S(1)} custom-call(s32[1]{0:T(128)} %bitcast.start_ref, s32[512]{0:T(512)} %mask_ref.3, s32[1,512]{1,0:T(1,128)} %bitcast.8, bf16[8,512,128]{2,1,0:T(8,128)(2,1)} %x_ref.5, f32[1,128]{1,0:T(1,128)} %bitcast.10, f32[1,128]{1,0:T(1,128)} %bitcast.16, bf16[128,640]{1,0:T(8,128)(2,1)} %weight_ref.5), custom_call_target="tpu_custom_call" | custom-call | flops 600000000 | bytes 4000000 | tf_op jit(solution)/shard_map/front/pallas_call | solution.py:410
  5.4 63.7 %all_to_all.25.recv_ref = bf16[64,128,128]{2,1,0:T(8,128)(2,1)S(1)} all-to-all(bf16[64,128,128]{2,1,0:T(8,128)(2,1)S(1)} %front.1), channel_id=1, replica_groups=mesh['cplx'=4,'row'=64] {'row'}, dimensions={0} | all-to-all | bytes 4194304 | tf_op jit(solution)/shard_map/all_to_all | solution.py:358
  69.1 1.9 product.1
  71.0 6.0 %all-to-all-start.1 = ((bf16[64,64,128]{2,1,0:T(8,128)(2,1)}), bf16[64,64,128]{2,1,0:T(8,128)(2,1)S(1)}, u32[]{:S(2)}, u32[]{:S(2)}) async-start(bf16[64,64,128]{2,1,0:T(8,128)(2,1)} %product.1), calls=%async_computation.1 | async-start | bytes 2097152 | tf_op jit(solution)/shard_map/all_to_all | solution.py:358
  77.0 7.6 %side.1 = (bf16[4,1024,128]{2,1,0:T(8,128)(2,1)}, bf16[4,4,128,1024]{3,2,1,0:T(8,128)(2,1)}, bf16[4,128,1024]{2,1,0:T(8,128)(2,1)}, bf16[4,128,1024]{2,1,0:T(8,128)(2,1)}, f32[4,128,1024]{2,1,0:T(8,128)}) custom-call(s32[1]{0:T(128)} %bitcast.start_ref, s32[512]{0:T(512)} %mask_ref.3, s32[1,512]{1,0:T(1,128)} %bitcast.9, bf16[8,512,128]{2,1,0:T(8,128)(2,1)} %x_ref.5, ...), custom_call_target="tpu_custom_call" | custom-call | flops 1200000000 | bytes 16000000 | tf_op jit(solution)/shard_map/side/pallas_call | solution.py:428
  84.6 1.8 slabs.1.factor_hbm
  86.4 18.5 %all-to-all-done.1.recv_ref = bf16[64,64,128]{2,1,0:T(8,128)(2,1)S(1)} async-done(((bf16[64,64,128]{2,1,0:T(8,128)(2,1)}), bf16[64,64,128]{2,1,0:T(8,128)(2,1)S(1)}, u32[]{:S(2)}, u32[]{:S(2)}) %all-to-all-start.1) | async-done | bytes 1048608 | tf_op jit(solution)/shard_map/all_to_all | solution.py:358
  104.9 3.9 %product_grad.1 = bf16[64,64,128]{2,1,0:T(8,128)(2,1)} custom-call(bf16[64,64,128]{2,1,0:T(8,128)(2,1)S(1)} %all-to-all-done.1.recv_ref, bf16[4,1024,128]{2,1,0:T(8,128)(2,1)} %get-tuple-element.12.h_ref, bf16[4,512,512]{2,1,0:T(8,128)(2,1)} %slabs.1.factor_hbm), custom_call_target="tpu_custom_call" | custom-call | flops 10000000 | bytes 4000000 | tf_op jit(solution)/shard_map/product_grad/pallas_call | solution.py:476
  108.8 5.8 %all-to-all-start.2 = ((bf16[64,64,128]{2,1,0:T(8,128)(2,1)}), bf16[64,64,128]{2,1,0:T(8,128)(2,1)S(1)}, u32[]{:S(2)}, u32[]{:S(2)}) async-start(bf16[64,64,128]{2,1,0:T(8,128)(2,1)} %product_grad.1), calls=%async_computation.2 | async-start | bytes 2097152 | tf_op jit(solution)/shard_map/all_to_all | solution.py:358
  114.6 6.0 %gate_side.1 = (f32[4,128,1024]{2,1,0:T(8,128)}, bf16[64,8,128]{2,1,0:T(8,128)(2,1)}) custom-call(bf16[64,64,128]{2,1,0:T(8,128)(2,1)S(1)} %all-to-all-done.1.recv_ref, bf16[4,128,1024]{2,1,0:T(8,128)(2,1)} %get-tuple-element.13.normed_ref, bf16[4,128,1024]{2,1,0:T(8,128)(2,1)} %get-tuple-element.14.mixed_ref, ...), custom_call_target="tpu_custom_call" | custom-call | flops 600000000 | bytes 8000000 | tf_op jit(solution)/shard_map/gate_side/pallas_call | solution.py:488
  120.6 21.8 %all-to-all-done.2.recv_ref = bf16[64,64,128]{2,1,0:T(8,128)(2,1)S(1)} async-done(((bf16[64,64,128]{2,1,0:T(8,128)(2,1)}), bf16[64,64,128]{2,1,0:T(8,128)(2,1)S(1)}, u32[]{:S(2)}, u32[]{:S(2)}) %all-to-all-start.2) | async-done | bytes 1048608 | tf_op jit(solution)/shard_map/all_to_all | solution.py:358
  142.4 3.9 %factor_grad.1 = bf16[64,136,128]{2,1,0:T(8,128)(2,1)S(1)} custom-call(bf16[64,64,128]{2,1,0:T(8,128)(2,1)S(1)} %all-to-all-done.2.recv_ref, bf16[4,512,512]{2,1,0:T(8,128)(2,1)} %slabs.1.factor_hbm, bf16[64,8,128]{2,1,0:T(8,128)(2,1)} %get-tuple-element.16.share_ref), custom_call_target="tpu_custom_call" | custom-call | flops 1100000000 | bytes 5000000 | tf_op jit(solution)/shard_map/factor_grad/pallas_call | solution.py:514
  146.3 60.4 %all_to_all.26.recv_ref.refs_1_ = bf16[64,136,128]{2,1,0:T(8,128)(2,1)S(1)} all-to-all(bf16[64,136,128]{2,1,0:T(8,128)(2,1)S(1)} %factor_grad.1), channel_id=1, replica_groups=mesh['cplx'=4,'row'=64] {'row'}, dimensions={0} | all-to-all | bytes 4456448 | tf_op jit(solution)/shard_map/all_to_all | solution.py:358
  206.7 5.2 %proj_grad.1 = f32[512,128]{1,0:T(8,128)} custom-call(bf16[64,136,128]{2,1,0:T(8,128)(2,1)S(1)} %all_to_all.26.recv_ref.refs_1_, bf16[4,4,128,1024]{3,2,1,0:T(8,128)(2,1)} %get-tuple-element.17.coef_ref, bf16[4,128,1024]{2,1,0:T(8,128)(2,1)} %get-tuple-element.13.normed_ref), custom_call_target="tpu_custom_call" | custom-call | flops 600000000 | bytes 8000000 | tf_op jit(solution)/shard_map/proj_grad/pallas_call | solution.py:530
  211.9 4.6 %all-to-all-start.4 = ((f32[64,8,128]{2,1,0:T(8,128)}), f32[64,8,128]{2,1,0:T(8,128)S(1)}, u32[]{:S(2)}, u32[]{:S(2)}) async-start(f32[64,8,128]{2,1,0:T(8,128)} %bitcast.7), calls=%async_computation.4 | async-start | bytes 524288 | tf_op jit(solution)/shard_map/all_to_all | solution.py:358
  216.6 6.5 %pair_grad.1 = bf16[8,512,128]{2,1,0:T(8,128)(2,1)} custom-call(bf16[64,136,128]{2,1,0:T(8,128)(2,1)S(1)} %all_to_all.26.recv_ref.refs_1_, bf16[4,4,128,1024]{3,2,1,0:T(8,128)(2,1)} %get-tuple-element.17.coef_ref, f32[4,128,1024]{2,1,0:T(8,128)} %get-tuple-element.18.gate_normed_ref, bf16[8,512,128]{2,1,0:T(8,128)(2,1)} %x_ref.5, f32[1,128]{1,0:T(1,128)} %bitcast.12, ...), custom_call_target="tpu_custom_call" | custom-call | flops 600000000 | bytes 8000000 | tf_op jit(solution)/shard_map/pair_grad/pallas_call | solution.py:546
  223.0 5.8 %all-to-all-done.4.refs_0_ = f32[64,8,128]{2,1,0:T(8,128)S(1)} async-done(((f32[64,8,128]{2,1,0:T(8,128)}), f32[64,8,128]{2,1,0:T(8,128)S(1)}, u32[]{:S(2)}, u32[]{:S(2)}) %all-to-all-start.4) | async-done | bytes 262176 | tf_op jit(solution)/shard_map/all_to_all | solution.py:358
  228.8 0.7 weight_sum.1
Async XLA Ops:
  71.0 33.9 %all-to-all-start.1 = ((bf16[64,64,128]{2,1,0:T(8,128)(2,1)}), bf16[64,64,128]{2,1,0:T(8,128)(2,1)S(1)}, u32[]{:S(2)}, u32[]{:S(2)}) async-start(bf16[64,64,128]{2,1,0:T(8,128)(2,1)} %product.1), calls=%async_computation.1 | async-start | bytes 2097152 | tf_op jit(solution)/shard_map/all_to_all | solution.py:358
  108.8 33.6 %all-to-all-start.2 = ((bf16[64,64,128]{2,1,0:T(8,128)(2,1)}), bf16[64,64,128]{2,1,0:T(8,128)(2,1)S(1)}, u32[]{:S(2)}, u32[]{:S(2)}) async-start(bf16[64,64,128]{2,1,0:T(8,128)(2,1)} %product_grad.1), calls=%async_computation.2 | async-start | bytes 2097152 | tf_op jit(solution)/shard_map/all_to_all | solution.py:358
  211.9 16.9 %all-to-all-start.4 = ((f32[64,8,128]{2,1,0:T(8,128)}), f32[64,8,128]{2,1,0:T(8,128)S(1)}, u32[]{:S(2)}, u32[]{:S(2)}) async-start(f32[64,8,128]{2,1,0:T(8,128)} %bitcast.7), calls=%async_computation.4 | async-start | bytes 524288 | tf_op jit(solution)/shard_map/all_to_all | solution.py:358

commit v4 on v3

--- a/solution.py
+++ b/solution.py
@@ -102,7 +102,7 @@
     start_ref, mask_ref, lane_mask_ref, x_ref, cot_ref, gain_ref, bias_ref, weight_ref,
     out_gain_ref, out_weight_ref,
     h_ref, coef_ref, normed_ref, mixed_ref, gate_coef_ref,
-    turned_weight, spread,
+    turned_weight,
 ):
     rows = x_ref.shape[0]
     channels = x_ref.shape[2]
@@ -129,8 +129,7 @@
     h = dot_nn(out_weight_ref[...], mixed) * as_column(out_gain_ref[...])
     h = h - jnp.mean(h, axis=0, keepdims=True)
     for row in range(rows):
-        spread[pl.ds(row, channels, stride=rows), :] = h[:, row * LANES : (row + 1) * LANES]
-    h_ref[0] = spread[...].astype(BF16)
+        h_ref[0, pl.ds(row, channels, stride=rows), :] = h[:, row * LANES : (row + 1) * LANES]
 
 
 def unpack(recv_ref, base, rows):
@@ -172,38 +171,38 @@
         )
 
 
-def product_grad_kernel(recv_ref, h_ref, factor_hbm, out_ref):
+def product_grad_kernel(recv_ref, h_ref, factor_hbm, out_ref, held):
     del factor_hbm
     slabs, group, _ = out_ref.shape
     rows = group // 2
     channels = 2 * slabs
     base = pl.multiple_of(pl.program_id(0) * group, group)
     chunk = 8
-
-    def product_at(at):
-        block = recv_ref[at : at + chunk, pl.ds(base, group), :].astype(F32)
-        return block.reshape(2 * chunk, rows, LANES)
+    size = 2 * chunk * rows
 
     def h_at(at):
-        size = 2 * chunk * rows
-        block = h_ref[0, at * group : at * group + size, :].astype(F32)
-        return block.reshape(2 * chunk, rows, LANES)
+        return h_ref[0, at * group : at * group + size, :].reshape(2 * chunk, rows, LANES)
+
+    def held_at(at):
+        return held[at * group : at * group + size, :].reshape(2 * chunk, rows, LANES)
 
     total = jnp.zeros((rows, LANES), F32)
     for at in range(0, slabs, chunk):
-        total = total + jnp.sum(product_at(at), axis=0)
+        block = recv_ref[at : at + chunk, pl.ds(base, group), :].astype(F32)
+        held[at * group : at * group + size, :] = block.reshape(size, LANES)
+        total = total + jnp.sum(block.reshape(2 * chunk, rows, LANES), axis=0)
     average = (total / channels)[None]
     squares = jnp.zeros((rows, LANES), F32)
     cross = jnp.zeros((rows, LANES), F32)
     for at in range(0, slabs, chunk):
-        centered = product_at(at) - average
+        centered = held_at(at) - average
         squares = squares + jnp.sum(centered * centered, axis=0)
         cross = cross + jnp.sum(centered * h_at(at), axis=0)
     inverse = lax.rsqrt(squares / channels + epsilon)
-    slope = (inverse * inverse * inverse * (cross / channels))[None]
-    inverse = inverse[None]
+    slope = inverse * inverse * inverse * (cross / channels)
+    inverse, slope = inverse[None], slope[None]
     for at in range(0, slabs, chunk):
-        grad = inverse * h_at(at) - (product_at(at) - average) * slope
+        grad = inverse * h_at(at) - (held_at(at) - average) * slope
         out_ref[at : at + chunk] = grad.reshape(chunk, group, LANES).astype(BF16)
 
 
@@ -252,7 +251,10 @@
         share_ref[...] = laid[...].reshape(half, 8, LANES).astype(BF16)
 
 
-def factor_grad_kernel(recv_ref, factor_hbm, share_ref, out_ref, slab, factor, arrived):
+def factor_grad_kernel(
+    recv_ref, factor_hbm, early_hbm, out_ref, slab, turned_slab, factor, arrived
+):
+    del early_hbm
     slabs = recv_ref.shape[0]
     tokens = slab.shape[1]
     rows = tokens // slabs
@@ -267,20 +269,19 @@
         for part in range(2):
             slab[part, :, tile * LANES : (tile + 1) * LANES] = parts[part]
     for side in range(2):
-        grads = []
         for part in range(2):
-            which = 2 + part if side == 0 else part
-            loads[which].wait()
-            dot = dot_nn if side == 0 else dot_tn
-            grads.append(dot(slab[part], factor[which]))
+            loads[2 * (1 - side) + part].wait()
+        if side == 0:
+            for part in range(2):
+                turned_slab[part] = slab[part].T
+        source = slab if side == 0 else turned_slab
+        grads = [dot_nn(source[part], factor[2 * (1 - side) + part]) for part in range(2)]
         for tile in range(tokens // LANES):
             cols = slice(tile * LANES, (tile + 1) * LANES)
             base = (tile * 2 + side) * 2 * rows
             out_ref[:, base : base + 2 * rows, :] = pack(
                 grads[0][:, cols], grads[1][:, cols], slabs
             )
-    base = tokens // LANES * 4 * rows
-    out_ref[:, base : base + 8, :] = share_ref[...]
 
 
 def proj_blocks(recv_ref, coef_ref, spread, rows):
@@ -302,7 +303,9 @@
     return blocks
 
 
-def proj_grad_kernel(recv_ref, coef_ref, normed_ref, share_ref, spread, term):
+def proj_grad_kernel(
+    recv_ref, coef_ref, normed_ref, early_ref, share_ref, spread, term, laid
+):
     step = pl.program_id(0)
     channels = normed_ref.shape[1]
     rows = normed_ref.shape[2] // LANES
@@ -311,17 +314,23 @@
     def _():
         term[...] = jnp.zeros_like(term)
 
-    for block, value in enumerate(proj_blocks(recv_ref, coef_ref, spread, rows)):
-        term[block] += dot_nt(normed_ref[0], value)
+    blocks = proj_blocks(recv_ref, coef_ref, spread, rows)
+    for side in range(2):
+        both = dot_nt(normed_ref[0], jnp.concatenate(blocks[2 * side : 2 * side + 2], axis=0))
+        for part in range(2):
+            term[2 * side + part] += both[:, part * channels : (part + 1) * channels]
 
     @pl.when(step == pl.num_programs(0) - 1)
     def _():
         half = channels // 2
         for part in range(2):
             for block in range(4):
-                share_ref[pl.ds(part * 4 + block, half, stride=8), :] = term[
+                laid[pl.ds(part * 4 + block, half, stride=8), :] = term[
                     block, pl.ds(part, half, stride=2), :
                 ]
+        late = laid[...].reshape(half, 8, LANES)
+        early = early_ref[...].astype(F32)
+        share_ref[...] = jnp.concatenate([late, early], axis=1).astype(BF16)
 
 
 def pair_grad_kernel(
@@ -336,18 +345,15 @@
         out_ref[row] = grad[:, row * LANES : (row + 1) * LANES].T.astype(BF16)
 
 
-def weight_sum_kernel(recv_ref, early_ref, in_ref, out_ref, *, tokens):
-    last = early_ref.shape[1] - 8
-    late = jnp.sum(recv_ref[...], axis=0) / tokens
-    early = jnp.sum(early_ref[:, last:, :].astype(F32), axis=0) / tokens
+def weight_sum_kernel(recv_ref, in_ref, out_ref, *, tokens):
+    total = jnp.sum(recv_ref[...].astype(F32), axis=0) / tokens
     for part in range(2):
         for block in range(4):
-            in_ref[part : part + 1, block * LANES : (block + 1) * LANES] = late[
-                part * 4 + block : part * 4 + block + 1
-            ]
-        at = part * 4
-        in_ref[part : part + 1, 4 * LANES :] = early[at : at + 1] + early[at + 1 : at + 2]
-        out_ref[part : part + 1, :] = early[at + 2 : at + 3] + early[at + 3 : at + 4]
+            at = part * 4 + block
+            in_ref[part : part + 1, block * LANES : (block + 1) * LANES] = total[at : at + 1]
+        at = 8 + part * 4
+        in_ref[part : part + 1, 4 * LANES :] = total[at : at + 1] + total[at + 1 : at + 2]
+        out_ref[part : part + 1, :] = total[at + 2 : at + 3] + total[at + 3 : at + 4]
 
 
 def whole(shape):
@@ -435,16 +441,13 @@
         ],
         out_specs=[h_spec, coef_spec, column_spec, column_spec, column_spec],
         out_shape=[
-            pltpu.HBM((tiles, channels * rows, LANES), BF16),
+            pltpu.HBM((tiles, channels * rows, LANES), F32),
             pltpu.HBM((tiles, 4, channels, cells), BF16),
             pltpu.HBM((tiles, channels, cells), BF16),
             pltpu.HBM((tiles, channels, cells), BF16),
             pltpu.HBM((tiles, channels, cells), F32),
         ],
-        scratch_shapes=[
-            pltpu.VMEM((5 * channels, channels), BF16),
-            pltpu.VMEM((channels * rows, LANES), F32),
-        ],
+        scratch_shapes=[pltpu.VMEM((5 * channels, channels), BF16)],
         compiler_params=params(40),
         cost_estimate=cost(12 * 10**8, 16 * 10**6),
     )(start, token_mask, lane_hbm, pair_hbm, cot_hbm, gain, bias, weight, out_gain, out_weight)
@@ -480,6 +483,7 @@
         in_specs=[vmem, h_spec, pl.BlockSpec(memory_space=pl.ANY)],
         out_specs=wire_spec(pair),
         out_shape=pltpu.HBM((slabs, pair * tiles, LANES), BF16),
+        scratch_shapes=[pltpu.VMEM((channels * rows, LANES), F32)],
         compiler_params=params(16),
         cost_estimate=cost(10**7, 4 * 10**6),
     )(product, h, factor_slab)
@@ -510,15 +514,16 @@
     )(product, normed, mixed, gate_coef, out_gain, out_bias, out_weight, weight)
     gate_normed, early_share = pinned(gate_normed, early_share)
 
-    height = 2 * pair * tiles + 8
+    height = 2 * pair * tiles
     sent_parts = pl.pallas_call(
         factor_grad_kernel,
         name="factor_grad",
-        in_specs=[vmem, pl.BlockSpec(memory_space=pl.ANY), whole((slabs, 8, LANES))],
+        in_specs=[vmem, pl.BlockSpec(memory_space=pl.ANY), pl.BlockSpec(memory_space=pl.ANY)],
         out_specs=vmem,
         out_shape=jax.ShapeDtypeStruct((slabs, height, LANES), BF16),
         scratch_shapes=[
             pltpu.VMEM((2, tokens, tokens), BF16),
+            pltpu.VMEM((2, tokens, tokens), BF16),
             pltpu.VMEM((4, tokens, tokens), BF16),
             pltpu.SemaphoreType.DMA((4,)),
         ],
@@ -531,17 +536,18 @@
         proj_grad_kernel,
         name="proj_grad",
         grid=(tiles,),
-        in_specs=[vmem, coef_spec, column_spec],
-        out_specs=whole((slabs * 8, LANES)),
-        out_shape=pltpu.HBM((slabs * 8, LANES), F32),
+        in_specs=[vmem, coef_spec, column_spec, whole((slabs, 8, LANES))],
+        out_specs=whole((slabs, 16, LANES)),
+        out_shape=pltpu.HBM((slabs, 16, LANES), BF16),
         scratch_shapes=[
             pltpu.VMEM((2, channels * rows, LANES), F32),
             pltpu.VMEM((4, channels, channels), F32),
+            pltpu.VMEM((slabs * 8, LANES), F32),
         ],
         compiler_params=params(24),
         cost_estimate=cost(6 * 10**8, 8 * 10**6),
-    )(parts, coef, normed)
-    late = exchange(late_share.reshape(slabs, 8, LANES))
+    )(parts, coef, normed, early_share)
+    shares = exchange(late_share)
 
     pair_gradient = pl.pallas_call(
         pair_grad_kernel,
@@ -559,7 +565,7 @@
     input_gradient, output_gradient = pl.pallas_call(
         lambda *refs: weight_sum_kernel(*refs, tokens=tokens),
         name="weight_sum",
-        in_specs=[vmem, vmem],
+        in_specs=[vmem],
         out_specs=[whole((held, 5 * channels)), whole((held, channels))],
         out_shape=[
             pltpu.HBM((held, 5 * channels), F32),
@@ -567,7 +573,7 @@
         ],
         compiler_params=params(16),
         cost_estimate=cost(10**5, 4 * 10**5),
-    )(late, parts)
+    )(shares)
     return (pair_gradient, input_gradient, output_gradient)
 
 

time: 230 us -> 226 us (0.983)
  blocking collectives: 124 us -> 119 us
    all_to_all x2, blocking collectives: 124 us -> 119 us  [exchange(): lax.all_to_all(values, 'row', split_axis=0, concat_axis=0, tiled=True)]
where the time goes in v4:
time: 226 us; the launch traced here: 225 us
  blocking collectives  119 us (53%)
  waiting for transfers between devices  46 us (20%)
  Pallas kernels  41.4 us (18%)
  starting transfers between devices  18.1 us (8%)
    all_to_all x2, blocking collectives, exchange(): lax.all_to_all(values, 'row', split_axis=0, concat_axis=0, tiled=True)  119 us
    all_to_all x3, waiting for transfers between devices, exchange(): lax.all_to_all(values, 'row', split_axis=0, concat_axis=0, tiled=True)  46 us
    all_to_all x3, starting transfers between devices, exchange(): lax.all_to_all(values, 'row', split_axis=0, concat_axis=0, tiled=True)  18.1 us
    pallas_call x1, Pallas kernels, on_device(): pl.pallas_call(side_kernel, name='side', grid=(tiles,), in_specs=[smem, s...  7.66 us
    pallas_call x1, Pallas kernels, on_device(): pl.pallas_call(pair_grad_kernel, name='pair_grad', grid=(tiles,), in_spec...  6.51 us
    pallas_call x1, Pallas kernels, on_device(): pl.pallas_call(gate_side_kernel, name='gate_side', grid=(tiles,), in_spec...  5.99 us
    pallas_call x1, Pallas kernels, on_device(): pl.pallas_call(proj_grad_kernel, name='proj_grad', grid=(tiles,), in_spec...  5.5 us
    pallas_call x1, Pallas kernels, on_device(): pl.pallas_call(front_kernel, name='front', grid=(tiles,), in_specs=[smem,...  4.77 us
  transfers between devices with their start and end apart: 3, of which 3 were waited for; matrix products, arithmetic and copies ran while one was open for 0% of the time, Pallas kernels for 10%

profile of v4, /device:TPU:16, one launch (start us, length us, event | category | flops | bytes accessed | tf_op | source)
XLA Modules:
  0.0 225.2 jit_solution(7341308036571858624)
XLA Ops:
  0.6 4.8 %front.1 = bf16[64,128,128]{2,1,0:T(8,128)(2,1)S(1)} custom-call(s32[1]{0:T(128)} %bitcast.start_ref, s32[512]{0:T(512)} %mask_ref.3, s32[1,512]{1,0:T(1,128)} %bitcast.6, bf16[8,512,128]{2,1,0:T(8,128)(2,1)} %x_ref.5, f32[1,128]{1,0:T(1,128)} %bitcast.8, f32[1,128]{1,0:T(1,128)} %bitcast.14, bf16[128,640]{1,0:T(8,128)(2,1)} %weight_ref.5), custom_call_target="tpu_custom_call" | custom-call | flops 600000000 | bytes 4000000 | tf_op jit(solution)/shard_map/front/pallas_call | solution.py:416
  5.4 63.7 %all_to_all.25.recv_ref = bf16[64,128,128]{2,1,0:T(8,128)(2,1)S(1)} all-to-all(bf16[64,128,128]{2,1,0:T(8,128)(2,1)S(1)} %front.1), channel_id=1, replica_groups=mesh['cplx'=4,'row'=64] {'row'}, dimensions={0} | all-to-all | bytes 4194304 | tf_op jit(solution)/shard_map/all_to_all | solution.py:364
  69.1 1.9 product.1
  71.0 6.0 %all-to-all-start.1 = ((bf16[64,64,128]{2,1,0:T(8,128)(2,1)}), bf16[64,64,128]{2,1,0:T(8,128)(2,1)S(1)}, u32[]{:S(2)}, u32[]{:S(2)}) async-start(bf16[64,64,128]{2,1,0:T(8,128)(2,1)} %product.1), calls=%async_computation.1 | async-start | bytes 2097152 | tf_op jit(solution)/shard_map/all_to_all | solution.py:364
  77.0 7.7 %side.1 = (f32[4,1024,128]{2,1,0:T(8,128)}, bf16[4,4,128,1024]{3,2,1,0:T(8,128)(2,1)}, bf16[4,128,1024]{2,1,0:T(8,128)(2,1)}, bf16[4,128,1024]{2,1,0:T(8,128)(2,1)}, f32[4,128,1024]{2,1,0:T(8,128)}) custom-call(s32[1]{0:T(128)} %bitcast.start_ref, s32[512]{0:T(512)} %mask_ref.3, s32[1,512]{1,0:T(1,128)} %bitcast.7, bf16[8,512,128]{2,1,0:T(8,128)(2,1)} %x_ref.5, ...), custom_call_target="tpu_custom_call" | custom-call | flops 1200000000 | bytes 16000000 | tf_op jit(solution)/shard_map/side/pallas_call | solution.py:434
  84.7 1.8 slabs.1.factor_hbm
  86.4 18.5 %all-to-all-done.1.recv_ref = bf16[64,64,128]{2,1,0:T(8,128)(2,1)S(1)} async-done(((bf16[64,64,128]{2,1,0:T(8,128)(2,1)}), bf16[64,64,128]{2,1,0:T(8,128)(2,1)S(1)}, u32[]{:S(2)}, u32[]{:S(2)}) %all-to-all-start.1) | async-done | bytes 1048608 | tf_op jit(solution)/shard_map/all_to_all | solution.py:364
  104.9 4.0 %product_grad.1 = bf16[64,64,128]{2,1,0:T(8,128)(2,1)} custom-call(bf16[64,64,128]{2,1,0:T(8,128)(2,1)S(1)} %all-to-all-done.1.recv_ref, f32[4,1024,128]{2,1,0:T(8,128)} %get-tuple-element.12.h_ref, bf16[4,512,512]{2,1,0:T(8,128)(2,1)} %slabs.1.factor_hbm), custom_call_target="tpu_custom_call" | custom-call | flops 10000000 | bytes 4000000 | tf_op jit(solution)/shard_map/product_grad/pallas_call | solution.py:479
  108.9 5.8 %all-to-all-start.2 = ((bf16[64,64,128]{2,1,0:T(8,128)(2,1)}), bf16[64,64,128]{2,1,0:T(8,128)(2,1)S(1)}, u32[]{:S(2)}, u32[]{:S(2)}) async-start(bf16[64,64,128]{2,1,0:T(8,128)(2,1)} %product_grad.1), calls=%async_computation.2 | async-start | bytes 2097152 | tf_op jit(solution)/shard_map/all_to_all | solution.py:364
  114.6 6.0 %gate_side.1 = (f32[4,128,1024]{2,1,0:T(8,128)}, bf16[64,8,128]{2,1,0:T(8,128)(2,1)}) custom-call(bf16[64,64,128]{2,1,0:T(8,128)(2,1)S(1)} %all-to-all-done.1.recv_ref, bf16[4,128,1024]{2,1,0:T(8,128)(2,1)} %get-tuple-element.13.normed_ref, bf16[4,128,1024]{2,1,0:T(8,128)(2,1)} %get-tuple-element.14.mixed_ref, ...), custom_call_target="tpu_custom_call" | custom-call | flops 600000000 | bytes 8000000 | tf_op jit(solution)/shard_map/gate_side/pallas_call | solution.py:492
  120.6 21.8 %all-to-all-done.2.recv_ref = bf16[64,64,128]{2,1,0:T(8,128)(2,1)S(1)} async-done(((bf16[64,64,128]{2,1,0:T(8,128)(2,1)}), bf16[64,64,128]{2,1,0:T(8,128)(2,1)S(1)}, u32[]{:S(2)}, u32[]{:S(2)}) %all-to-all-start.2) | async-done | bytes 1048608 | tf_op jit(solution)/shard_map/all_to_all | solution.py:364
  142.5 2.7 %factor_grad.1 = bf16[64,128,128]{2,1,0:T(8,128)(2,1)S(1)} custom-call(bf16[64,64,128]{2,1,0:T(8,128)(2,1)S(1)} %all-to-all-done.2.recv_ref, bf16[4,512,512]{2,1,0:T(8,128)(2,1)} %slabs.1.factor_hbm, bf16[64,8,128]{2,1,0:T(8,128)(2,1)} %get-tuple-element.16.early_hbm.early_ref), custom_call_target="tpu_custom_call" | custom-call | flops 1100000000 | bytes 5000000 | tf_op jit(solution)/shard_map/factor_grad/pallas_call | solution.py:518
  145.1 55.3 %all_to_all.26.recv_ref = bf16[64,128,128]{2,1,0:T(8,128)(2,1)S(1)} all-to-all(bf16[64,128,128]{2,1,0:T(8,128)(2,1)S(1)} %factor_grad.1), channel_id=1, replica_groups=mesh['cplx'=4,'row'=64] {'row'}, dimensions={0} | all-to-all | bytes 4194304 | tf_op jit(solution)/shard_map/all_to_all | solution.py:364
  200.5 5.5 %proj_grad.1 = bf16[64,16,128]{2,1,0:T(8,128)(2,1)} custom-call(bf16[64,128,128]{2,1,0:T(8,128)(2,1)S(1)} %all_to_all.26.recv_ref, bf16[4,4,128,1024]{3,2,1,0:T(8,128)(2,1)} %get-tuple-element.17.coef_ref, bf16[4,128,1024]{2,1,0:T(8,128)(2,1)} %get-tuple-element.13.normed_ref, bf16[64,8,128]{2,1,0:T(8,128)(2,1)} %get-tuple-element.16.early_hbm.early_ref), custom_call_target="tpu_custom_call" | custom-call | flops 600000000 | bytes 8000000 | tf_op jit(solution)/shard_map/proj_grad/pallas_call | solution.py:535
  206.0 6.3 %all-to-all-start.4 = ((bf16[64,16,128]{2,1,0:T(8,128)(2,1)}), bf16[64,16,128]{2,1,0:T(8,128)(2,1)S(1)}, u32[]{:S(2)}, u32[]{:S(2)}) async-start(bf16[64,16,128]{2,1,0:T(8,128)(2,1)} %proj_grad.1), calls=%async_computation.4 | async-start | bytes 524288 | tf_op jit(solution)/shard_map/all_to_all | solution.py:364
  212.3 6.5 %pair_grad.1 = bf16[8,512,128]{2,1,0:T(8,128)(2,1)} custom-call(bf16[64,128,128]{2,1,0:T(8,128)(2,1)S(1)} %all_to_all.26.recv_ref, bf16[4,4,128,1024]{3,2,1,0:T(8,128)(2,1)} %get-tuple-element.17.coef_ref, f32[4,128,1024]{2,1,0:T(8,128)} %get-tuple-element.18.gate_normed_ref, bf16[8,512,128]{2,1,0:T(8,128)(2,1)} %x_ref.5, f32[1,128]{1,0:T(1,128)} %bitcast.10, ...), custom_call_target="tpu_custom_call" | custom-call | flops 600000000 | bytes 8000000 | tf_op jit(solution)/shard_map/pair_grad/pallas_call | solution.py:552
  218.8 5.7 %all-to-all-done.4.refs_0_ = bf16[64,16,128]{2,1,0:T(8,128)(2,1)S(1)} async-done(((bf16[64,16,128]{2,1,0:T(8,128)(2,1)}), bf16[64,16,128]{2,1,0:T(8,128)(2,1)S(1)}, u32[]{:S(2)}, u32[]{:S(2)}) %all-to-all-start.4) | async-done | bytes 262176 | tf_op jit(solution)/shard_map/all_to_all | solution.py:364
  224.5 0.7 weight_sum.1
Async XLA Ops:
  71.0 33.9 %all-to-all-start.1 = ((bf16[64,64,128]{2,1,0:T(8,128)(2,1)}), bf16[64,64,128]{2,1,0:T(8,128)(2,1)S(1)}, u32[]{:S(2)}, u32[]{:S(2)}) async-start(bf16[64,64,128]{2,1,0:T(8,128)(2,1)} %product.1), calls=%async_computation.1 | async-start | bytes 2097152 | tf_op jit(solution)/shard_map/all_to_all | solution.py:364
  108.9 33.6 %all-to-all-start.2 = ((bf16[64,64,128]{2,1,0:T(8,128)(2,1)}), bf16[64,64,128]{2,1,0:T(8,128)(2,1)S(1)}, u32[]{:S(2)}, u32[]{:S(2)}) async-start(bf16[64,64,128]{2,1,0:T(8,128)(2,1)} %product_grad.1), calls=%async_computation.2 | async-start | bytes 2097152 | tf_op jit(solution)/shard_map/all_to_all | solution.py:364
  206.0 18.6 %all-to-all-start.4 = ((bf16[64,16,128]{2,1,0:T(8,128)(2,1)}), bf16[64,16,128]{2,1,0:T(8,128)(2,1)S(1)}, u32[]{:S(2)}, u32[]{:S(2)}) async-start(bf16[64,16,128]{2,1,0:T(8,128)(2,1)} %proj_grad.1), calls=%async_computation.4 | async-start | bytes 524288 | tf_op jit(solution)/shard_map/all_to_all | solution.py:364

commit v5 on v4

--- a/solution.py
+++ b/solution.py
@@ -92,8 +92,9 @@
                 :, row * LANES : (row + 1) * LANES
             ]
     group = channels * rows // out_ref.shape[0]
+    base = pl.multiple_of(pl.program_id(0) * 2 * group, 2 * group)
     for side in range(2):
-        out_ref[:, side * group : (side + 1) * group, :] = (
+        out_ref[:, pl.ds(base + side * group, group), :] = (
             spread[side].reshape(out_ref.shape[0], group, LANES).astype(BF16)
         )
 
@@ -171,17 +172,24 @@
         )
 
 
-def product_grad_kernel(recv_ref, h_ref, factor_hbm, out_ref, held):
+def product_grad_kernel(recv_ref, h_hbm, factor_hbm, out_ref, held, h_ref, arrived):
     del factor_hbm
+    step = pl.program_id(0)
+
+    @pl.when(step == 0)
+    def _():
+        for tile in range(h_hbm.shape[0]):
+            pltpu.make_async_copy(h_hbm.at[tile], h_ref.at[tile], arrived.at[tile]).start()
+
     slabs, group, _ = out_ref.shape
     rows = group // 2
     channels = 2 * slabs
-    base = pl.multiple_of(pl.program_id(0) * group, group)
+    base = pl.multiple_of(step * group, group)
     chunk = 8
     size = 2 * chunk * rows
 
     def h_at(at):
-        return h_ref[0, at * group : at * group + size, :].reshape(2 * chunk, rows, LANES)
+        return h_ref[step, at * group : at * group + size, :].reshape(2 * chunk, rows, LANES)
 
     def held_at(at):
         return held[at * group : at * group + size, :].reshape(2 * chunk, rows, LANES)
@@ -192,6 +200,7 @@
         held[at * group : at * group + size, :] = block.reshape(size, LANES)
         total = total + jnp.sum(block.reshape(2 * chunk, rows, LANES), axis=0)
     average = (total / channels)[None]
+    pltpu.make_async_copy(h_hbm.at[step], h_ref.at[step], arrived.at[step]).wait()
     squares = jnp.zeros((rows, LANES), F32)
     cross = jnp.zeros((rows, LANES), F32)
     for at in range(0, slabs, chunk):
@@ -284,9 +293,9 @@
             )
 
 
-def proj_blocks(recv_ref, coef_ref, spread, rows):
+def spread_parts(recv_ref, spread, rows):
     step = pl.program_id(0)
-    channels = coef_ref.shape[2]
+    channels = spread.shape[1] // rows
     group = channels * rows // recv_ref.shape[0]
     base = pl.multiple_of(step * 2 * group, 2 * group)
     for side in range(2):
@@ -295,6 +304,11 @@
             .astype(F32)
             .reshape(channels * rows, LANES)
         )
+
+
+def proj_blocks(recv_ref, coef_ref, spread, rows):
+    channels = coef_ref.shape[2]
+    spread_parts(recv_ref, spread, rows)
     blocks = []
     for side in range(2):
         grad = gather_rows(spread.at[side], channels, rows)
@@ -314,9 +328,21 @@
     def _():
         term[...] = jnp.zeros_like(term)
 
-    blocks = proj_blocks(recv_ref, coef_ref, spread, rows)
+    spread_parts(recv_ref, spread, rows)
     for side in range(2):
-        both = dot_nt(normed_ref[0], jnp.concatenate(blocks[2 * side : 2 * side + 2], axis=0))
+        both = None
+        for row in range(0, rows, 4):
+            cols = slice(row * LANES, (row + 4) * LANES)
+            grad = jnp.concatenate(
+                [spread[side, pl.ds(at, channels, stride=rows), :] for at in range(row, row + 4)],
+                axis=1,
+            )
+            values = [
+                (grad * coef_ref[0, 2 * side + part, :, cols].astype(F32)).astype(BF16)
+                for part in range(2)
+            ]
+            piece = dot_nt(normed_ref[0, :, cols], jnp.concatenate(values, axis=0))
+            both = piece if both is None else both + piece
         for part in range(2):
             term[2 * side + part] += both[:, part * channels : (part + 1) * channels]
 
@@ -406,6 +432,7 @@
 
     pair = 2 * rows
     vmem = pl.BlockSpec(memory_space=pltpu.VMEM)
+    anywhere = pl.BlockSpec(memory_space=pl.ANY)
     h_spec = pl.BlockSpec((1, channels * rows, LANES), lambda t: (t, 0, 0))
     coef_spec = pl.BlockSpec((1, 4, channels, cells), lambda t: (t, 0, 0, 0))
     factor_weight_spec = pl.BlockSpec((channels, 4 * channels), lambda t: (0, 0))
@@ -420,7 +447,7 @@
         in_specs=[
             smem, smem, lane_spec, cell_spec, row_spec, row_spec, factor_weight_spec,
         ],
-        out_specs=wire_spec(2 * pair),
+        out_specs=vmem,
         out_shape=jax.ShapeDtypeStruct((slabs, 2 * pair * tiles, LANES), BF16),
         scratch_shapes=[
             pltpu.VMEM((4 * channels, channels), BF16),
@@ -480,10 +507,14 @@
         product_grad_kernel,
         name="product_grad",
         grid=(tiles,),
-        in_specs=[vmem, h_spec, pl.BlockSpec(memory_space=pl.ANY)],
+        in_specs=[vmem, anywhere, anywhere],
         out_specs=wire_spec(pair),
         out_shape=pltpu.HBM((slabs, pair * tiles, LANES), BF16),
-        scratch_shapes=[pltpu.VMEM((channels * rows, LANES), F32)],
+        scratch_shapes=[
+            pltpu.VMEM((channels * rows, LANES), F32),
+            pltpu.VMEM((tiles, channels * rows, LANES), F32),
+            pltpu.SemaphoreType.DMA((tiles,)),
+        ],
         compiler_params=params(16),
         cost_estimate=cost(10**7, 4 * 10**6),
     )(product, h, factor_slab)
@@ -518,7 +549,7 @@
     sent_parts = pl.pallas_call(
         factor_grad_kernel,
         name="factor_grad",
-        in_specs=[vmem, pl.BlockSpec(memory_space=pl.ANY), pl.BlockSpec(memory_space=pl.ANY)],
+        in_specs=[vmem, anywhere, anywhere],
         out_specs=vmem,
         out_shape=jax.ShapeDtypeStruct((slabs, height, LANES), BF16),
         scratch_shapes=[

time: 226 us -> 225 us (level)
  no operation moved by 1% of the time
where the time goes in v5:
time: 225 us; the launch traced here: 224 us
  blocking collectives  119 us (53%)
  waiting for transfers between devices  46 us (20%)
  Pallas kernels  40.4 us (18%)
  starting transfers between devices  18.1 us (8%)
    all_to_all x2, blocking collectives, exchange(): lax.all_to_all(values, 'row', split_axis=0, concat_axis=0, tiled=True)  119 us
    all_to_all x3, waiting for transfers between devices, exchange(): lax.all_to_all(values, 'row', split_axis=0, concat_axis=0, tiled=True)  46 us
    all_to_all x3, starting transfers between devices, exchange(): lax.all_to_all(values, 'row', split_axis=0, concat_axis=0, tiled=True)  18.1 us
    pallas_call x1, Pallas kernels, on_device(): pl.pallas_call(side_kernel, name='side', grid=(tiles,), in_specs=[smem, s...  7.66 us
    pallas_call x1, Pallas kernels, on_device(): pl.pallas_call(pair_grad_kernel, name='pair_grad', grid=(tiles,), in_spec...  6.51 us
    pallas_call x1, Pallas kernels, on_device(): pl.pallas_call(gate_side_kernel, name='gate_side', grid=(tiles,), in_spec...  5.98 us
    pallas_call x1, Pallas kernels, on_device(): pl.pallas_call(proj_grad_kernel, name='proj_grad', grid=(tiles,), in_spec...  5.48 us
    pallas_call x1, Pallas kernels, on_device(): pl.pallas_call(front_kernel, name='front', grid=(tiles,), in_specs=[smem,...  4.67 us
  transfers between devices with their start and end apart: 3, of which 3 were waited for; matrix products, arithmetic and copies ran while one was open for 0% of the time, Pallas kernels for 10%

profile of v5, /device:TPU:16, one launch (start us, length us, event | category | flops | bytes accessed | tf_op | source)
XLA Modules:
  0.0 224.3 jit_solution(12635338024795104870)
XLA Ops:
  0.6 4.7 %front.1 = bf16[64,128,128]{2,1,0:T(8,128)(2,1)S(1)} custom-call(s32[1]{0:T(128)} %bitcast.start_ref, s32[512]{0:T(512)} %mask_ref.3, s32[1,512]{1,0:T(1,128)} %bitcast.6, bf16[8,512,128]{2,1,0:T(8,128)(2,1)} %x_ref.5, f32[1,128]{1,0:T(1,128)} %bitcast.8, f32[1,128]{1,0:T(1,128)} %bitcast.14, bf16[128,640]{1,0:T(8,128)(2,1)} %weight_ref.5), custom_call_target="tpu_custom_call" | custom-call | flops 600000000 | bytes 4000000 | tf_op jit(solution)/shard_map/front/pallas_call | solution.py:443
  5.3 63.7 %all_to_all.25.recv_ref = bf16[64,128,128]{2,1,0:T(8,128)(2,1)S(1)} all-to-all(bf16[64,128,128]{2,1,0:T(8,128)(2,1)S(1)} %front.1), channel_id=1, replica_groups=mesh['cplx'=4,'row'=64] {'row'}, dimensions={0} | all-to-all | bytes 4194304 | tf_op jit(solution)/shard_map/all_to_all | solution.py:390
  69.0 1.9 product.1
  70.9 6.0 %all-to-all-start.1 = ((bf16[64,64,128]{2,1,0:T(8,128)(2,1)}), bf16[64,64,128]{2,1,0:T(8,128)(2,1)S(1)}, u32[]{:S(2)}, u32[]{:S(2)}) async-start(bf16[64,64,128]{2,1,0:T(8,128)(2,1)} %product.1), calls=%async_computation.1 | async-start | bytes 2097152 | tf_op jit(solution)/shard_map/all_to_all | solution.py:390
  76.9 7.7 %side.1 = (f32[4,1024,128]{2,1,0:T(8,128)}, bf16[4,4,128,1024]{3,2,1,0:T(8,128)(2,1)}, bf16[4,128,1024]{2,1,0:T(8,128)(2,1)}, bf16[4,128,1024]{2,1,0:T(8,128)(2,1)}, f32[4,128,1024]{2,1,0:T(8,128)}) custom-call(s32[1]{0:T(128)} %bitcast.start_ref, s32[512]{0:T(512)} %mask_ref.3, s32[1,512]{1,0:T(1,128)} %bitcast.7, bf16[8,512,128]{2,1,0:T(8,128)(2,1)} %x_ref.5, ...), custom_call_target="tpu_custom_call" | custom-call | flops 1200000000 | bytes 16000000 | tf_op jit(solution)/shard_map/side/pallas_call | solution.py:461
  84.6 1.8 slabs.1.factor_hbm
  86.3 18.5 %all-to-all-done.1.recv_ref = bf16[64,64,128]{2,1,0:T(8,128)(2,1)S(1)} async-done(((bf16[64,64,128]{2,1,0:T(8,128)(2,1)}), bf16[64,64,128]{2,1,0:T(8,128)(2,1)S(1)}, u32[]{:S(2)}, u32[]{:S(2)}) %all-to-all-start.1) | async-done | bytes 1048608 | tf_op jit(solution)/shard_map/all_to_all | solution.py:390
  104.8 3.2 %product_grad.1 = bf16[64,64,128]{2,1,0:T(8,128)(2,1)} custom-call(bf16[64,64,128]{2,1,0:T(8,128)(2,1)S(1)} %all-to-all-done.1.recv_ref, f32[4,1024,128]{2,1,0:T(8,128)} %get-tuple-element.12.h_hbm, bf16[4,512,512]{2,1,0:T(8,128)(2,1)} %slabs.1.factor_hbm), custom_call_target="tpu_custom_call" | custom-call | flops 10000000 | bytes 4000000 | tf_op jit(solution)/shard_map/product_grad/pallas_call | solution.py:506
  107.9 5.8 %all-to-all-start.2 = ((bf16[64,64,128]{2,1,0:T(8,128)(2,1)}), bf16[64,64,128]{2,1,0:T(8,128)(2,1)S(1)}, u32[]{:S(2)}, u32[]{:S(2)}) async-start(bf16[64,64,128]{2,1,0:T(8,128)(2,1)} %product_grad.1), calls=%async_computation.2 | async-start | bytes 2097152 | tf_op jit(solution)/shard_map/all_to_all | solution.py:390
  113.7 6.0 %gate_side.1 = (f32[4,128,1024]{2,1,0:T(8,128)}, bf16[64,8,128]{2,1,0:T(8,128)(2,1)}) custom-call(bf16[64,64,128]{2,1,0:T(8,128)(2,1)S(1)} %all-to-all-done.1.recv_ref, bf16[4,128,1024]{2,1,0:T(8,128)(2,1)} %get-tuple-element.13.normed_ref, bf16[4,128,1024]{2,1,0:T(8,128)(2,1)} %get-tuple-element.14.mixed_ref, ...), custom_call_target="tpu_custom_call" | custom-call | flops 600000000 | bytes 8000000 | tf_op jit(solution)/shard_map/gate_side/pallas_call | solution.py:523
  119.7 21.8 %all-to-all-done.2.recv_ref = bf16[64,64,128]{2,1,0:T(8,128)(2,1)S(1)} async-done(((bf16[64,64,128]{2,1,0:T(8,128)(2,1)}), bf16[64,64,128]{2,1,0:T(8,128)(2,1)S(1)}, u32[]{:S(2)}, u32[]{:S(2)}) %all-to-all-start.2) | async-done | bytes 1048608 | tf_op jit(solution)/shard_map/all_to_all | solution.py:390
  141.6 2.7 %factor_grad.1 = bf16[64,128,128]{2,1,0:T(8,128)(2,1)S(1)} custom-call(bf16[64,64,128]{2,1,0:T(8,128)(2,1)S(1)} %all-to-all-done.2.recv_ref, bf16[4,512,512]{2,1,0:T(8,128)(2,1)} %slabs.1.factor_hbm, bf16[64,8,128]{2,1,0:T(8,128)(2,1)} %get-tuple-element.16.early_hbm.early_ref), custom_call_target="tpu_custom_call" | custom-call | flops 1100000000 | bytes 5000000 | tf_op jit(solution)/shard_map/factor_grad/pallas_call | solution.py:549
  144.2 55.3 %all_to_all.26.recv_ref = bf16[64,128,128]{2,1,0:T(8,128)(2,1)S(1)} all-to-all(bf16[64,128,128]{2,1,0:T(8,128)(2,1)S(1)} %factor_grad.1), channel_id=1, replica_groups=mesh['cplx'=4,'row'=64] {'row'}, dimensions={0} | all-to-all | bytes 4194304 | tf_op jit(solution)/shard_map/all_to_all | solution.py:390
  199.6 5.5 %proj_grad.1 = bf16[64,16,128]{2,1,0:T(8,128)(2,1)} custom-call(bf16[64,128,128]{2,1,0:T(8,128)(2,1)S(1)} %all_to_all.26.recv_ref, bf16[4,4,128,1024]{3,2,1,0:T(8,128)(2,1)} %get-tuple-element.17.coef_ref, bf16[4,128,1024]{2,1,0:T(8,128)(2,1)} %get-tuple-element.13.normed_ref, bf16[64,8,128]{2,1,0:T(8,128)(2,1)} %get-tuple-element.16.early_hbm.early_ref), custom_call_target="tpu_custom_call" | custom-call | flops 600000000 | bytes 8000000 | tf_op jit(solution)/shard_map/proj_grad/pallas_call | solution.py:566
  205.0 6.3 %all-to-all-start.4 = ((bf16[64,16,128]{2,1,0:T(8,128)(2,1)}), bf16[64,16,128]{2,1,0:T(8,128)(2,1)S(1)}, u32[]{:S(2)}, u32[]{:S(2)}) async-start(bf16[64,16,128]{2,1,0:T(8,128)(2,1)} %proj_grad.1), calls=%async_computation.4 | async-start | bytes 524288 | tf_op jit(solution)/shard_map/all_to_all | solution.py:390
  211.4 6.5 %pair_grad.1 = bf16[8,512,128]{2,1,0:T(8,128)(2,1)} custom-call(bf16[64,128,128]{2,1,0:T(8,128)(2,1)S(1)} %all_to_all.26.recv_ref, bf16[4,4,128,1024]{3,2,1,0:T(8,128)(2,1)} %get-tuple-element.17.coef_ref, f32[4,128,1024]{2,1,0:T(8,128)} %get-tuple-element.18.gate_normed_ref, bf16[8,512,128]{2,1,0:T(8,128)(2,1)} %x_ref.5, f32[1,128]{1,0:T(1,128)} %bitcast.10, ...), custom_call_target="tpu_custom_call" | custom-call | flops 600000000 | bytes 8000000 | tf_op jit(solution)/shard_map/pair_grad/pallas_call | solution.py:583
  217.9 5.7 %all-to-all-done.4.refs_0_ = bf16[64,16,128]{2,1,0:T(8,128)(2,1)S(1)} async-done(((bf16[64,16,128]{2,1,0:T(8,128)(2,1)}), bf16[64,16,128]{2,1,0:T(8,128)(2,1)S(1)}, u32[]{:S(2)}, u32[]{:S(2)}) %all-to-all-start.4) | async-done | bytes 262176 | tf_op jit(solution)/shard_map/all_to_all | solution.py:390
  223.6 0.7 weight_sum.1
Async XLA Ops:
  70.9 33.9 %all-to-all-start.1 = ((bf16[64,64,128]{2,1,0:T(8,128)(2,1)}), bf16[64,64,128]{2,1,0:T(8,128)(2,1)S(1)}, u32[]{:S(2)}, u32[]{:S(2)}) async-start(bf16[64,64,128]{2,1,0:T(8,128)(2,1)} %product.1), calls=%async_computation.1 | async-start | bytes 2097152 | tf_op jit(solution)/shard_map/all_to_all | solution.py:390
  107.9 33.6 %all-to-all-start.2 = ((bf16[64,64,128]{2,1,0:T(8,128)(2,1)}), bf16[64,64,128]{2,1,0:T(8,128)(2,1)S(1)}, u32[]{:S(2)}, u32[]{:S(2)}) async-start(bf16[64,64,128]{2,1,0:T(8,128)(2,1)} %product_grad.1), calls=%async_computation.2 | async-start | bytes 2097152 | tf_op jit(solution)/shard_map/all_to_all | solution.py:390
  205.0 18.6 %all-to-all-start.4 = ((bf16[64,16,128]{2,1,0:T(8,128)(2,1)}), bf16[64,16,128]{2,1,0:T(8,128)(2,1)S(1)}, u32[]{:S(2)}, u32[]{:S(2)}) async-start(bf16[64,16,128]{2,1,0:T(8,128)(2,1)} %proj_grad.1), calls=%async_computation.4 | async-start | bytes 524288 | tf_op jit(solution)/shard_map/all_to_all | solution.py:390

commit v6 on v5

--- a/solution.py
+++ b/solution.py
@@ -311,9 +311,9 @@
     spread_parts(recv_ref, spread, rows)
     blocks = []
     for side in range(2):
-        grad = gather_rows(spread.at[side], channels, rows)
+        grad = gather_rows(spread.at[side], channels, rows).astype(BF16)
         for part in range(2):
-            blocks.append((grad * coef_ref[0, 2 * side + part].astype(F32)).astype(BF16))
+            blocks.append(grad * coef_ref[0, 2 * side + part])
     return blocks
 
 
@@ -337,10 +337,8 @@
                 [spread[side, pl.ds(at, channels, stride=rows), :] for at in range(row, row + 4)],
                 axis=1,
             )
-            values = [
-                (grad * coef_ref[0, 2 * side + part, :, cols].astype(F32)).astype(BF16)
-                for part in range(2)
-            ]
+            grad = grad.astype(BF16)
+            values = [grad * coef_ref[0, 2 * side + part, :, cols] for part in range(2)]
             piece = dot_nt(normed_ref[0, :, cols], jnp.concatenate(values, axis=0))
             both = piece if both is None else both + piece
         for part in range(2):

time: 225 us -> 225 us (level)
  no operation moved by 1% of the time
where the time goes in v6:
time: 225 us; the launch traced here: 224 us
  blocking collectives  119 us (53%)
  waiting for transfers between devices  46.2 us (21%)
  Pallas kernels  40 us (18%)
  starting transfers between devices  18.1 us (8%)
    all_to_all x2, blocking collectives, exchange(): lax.all_to_all(values, 'row', split_axis=0, concat_axis=0, tiled=True)  119 us
    all_to_all x3, waiting for transfers between devices, exchange(): lax.all_to_all(values, 'row', split_axis=0, concat_axis=0, tiled=True)  46.2 us
    all_to_all x3, starting transfers between devices, exchange(): lax.all_to_all(values, 'row', split_axis=0, concat_axis=0, tiled=True)  18.1 us
    pallas_call x1, Pallas kernels, on_device(): pl.pallas_call(side_kernel, name='side', grid=(tiles,), in_specs=[smem, s...  7.66 us
    pallas_call x1, Pallas kernels, on_device(): pl.pallas_call(pair_grad_kernel, name='pair_grad', grid=(tiles,), in_spec...  6.31 us
    pallas_call x1, Pallas kernels, on_device(): pl.pallas_call(gate_side_kernel, name='gate_side', grid=(tiles,), in_spec...  5.98 us
    pallas_call x1, Pallas kernels, on_device(): pl.pallas_call(proj_grad_kernel, name='proj_grad', grid=(tiles,), in_spec...  5.23 us
    pallas_call x1, Pallas kernels, on_device(): pl.pallas_call(front_kernel, name='front', grid=(tiles,), in_specs=[smem,...  4.67 us
  transfers between devices with their start and end apart: 3, of which 3 were waited for; matrix products, arithmetic and copies ran while one was open for 0% of the time, Pallas kernels for 10%

profile of v6, /device:TPU:16, one launch (start us, length us, event | category | flops | bytes accessed | tf_op | source)
XLA Modules:
  0.0 224.0 jit_solution(6333582938928888348)
XLA Ops:
  0.6 4.7 %front.1 = bf16[64,128,128]{2,1,0:T(8,128)(2,1)S(1)} custom-call(s32[1]{0:T(128)} %bitcast.start_ref, s32[512]{0:T(512)} %mask_ref.3, s32[1,512]{1,0:T(1,128)} %bitcast.6, bf16[8,512,128]{2,1,0:T(8,128)(2,1)} %x_ref.5, f32[1,128]{1,0:T(1,128)} %bitcast.8, f32[1,128]{1,0:T(1,128)} %bitcast.14, bf16[128,640]{1,0:T(8,128)(2,1)} %weight_ref.5), custom_call_target="tpu_custom_call" | custom-call | flops 600000000 | bytes 4000000 | tf_op jit(solution)/shard_map/front/pallas_call | solution.py:441
  5.3 63.7 %all_to_all.25.recv_ref = bf16[64,128,128]{2,1,0:T(8,128)(2,1)S(1)} all-to-all(bf16[64,128,128]{2,1,0:T(8,128)(2,1)S(1)} %front.1), channel_id=1, replica_groups=mesh['cplx'=4,'row'=64] {'row'}, dimensions={0} | all-to-all | bytes 4194304 | tf_op jit(solution)/shard_map/all_to_all | solution.py:388
  69.0 1.9 product.1
  70.9 6.0 %all-to-all-start.1 = ((bf16[64,64,128]{2,1,0:T(8,128)(2,1)}), bf16[64,64,128]{2,1,0:T(8,128)(2,1)S(1)}, u32[]{:S(2)}, u32[]{:S(2)}) async-start(bf16[64,64,128]{2,1,0:T(8,128)(2,1)} %product.1), calls=%async_computation.1 | async-start | bytes 2097152 | tf_op jit(solution)/shard_map/all_to_all | solution.py:388
  76.9 7.7 %side.1 = (f32[4,1024,128]{2,1,0:T(8,128)}, bf16[4,4,128,1024]{3,2,1,0:T(8,128)(2,1)}, bf16[4,128,1024]{2,1,0:T(8,128)(2,1)}, bf16[4,128,1024]{2,1,0:T(8,128)(2,1)}, f32[4,128,1024]{2,1,0:T(8,128)}) custom-call(s32[1]{0:T(128)} %bitcast.start_ref, s32[512]{0:T(512)} %mask_ref.3, s32[1,512]{1,0:T(1,128)} %bitcast.7, bf16[8,512,128]{2,1,0:T(8,128)(2,1)} %x_ref.5, ...), custom_call_target="tpu_custom_call" | custom-call | flops 1200000000 | bytes 16000000 | tf_op jit(solution)/shard_map/side/pallas_call | solution.py:459
  84.6 1.8 slabs.1.factor_hbm
  86.3 18.5 %all-to-all-done.1.recv_ref = bf16[64,64,128]{2,1,0:T(8,128)(2,1)S(1)} async-done(((bf16[64,64,128]{2,1,0:T(8,128)(2,1)}), bf16[64,64,128]{2,1,0:T(8,128)(2,1)S(1)}, u32[]{:S(2)}, u32[]{:S(2)}) %all-to-all-start.1) | async-done | bytes 1048608 | tf_op jit(solution)/shard_map/all_to_all | solution.py:388
  104.8 3.2 %product_grad.1 = bf16[64,64,128]{2,1,0:T(8,128)(2,1)} custom-call(bf16[64,64,128]{2,1,0:T(8,128)(2,1)S(1)} %all-to-all-done.1.recv_ref, f32[4,1024,128]{2,1,0:T(8,128)} %get-tuple-element.12.h_hbm, bf16[4,512,512]{2,1,0:T(8,128)(2,1)} %slabs.1.factor_hbm), custom_call_target="tpu_custom_call" | custom-call | flops 10000000 | bytes 4000000 | tf_op jit(solution)/shard_map/product_grad/pallas_call | solution.py:504
  107.9 5.8 %all-to-all-start.2 = ((bf16[64,64,128]{2,1,0:T(8,128)(2,1)}), bf16[64,64,128]{2,1,0:T(8,128)(2,1)S(1)}, u32[]{:S(2)}, u32[]{:S(2)}) async-start(bf16[64,64,128]{2,1,0:T(8,128)(2,1)} %product_grad.1), calls=%async_computation.2 | async-start | bytes 2097152 | tf_op jit(solution)/shard_map/all_to_all | solution.py:388
  113.7 6.0 %gate_side.1 = (f32[4,128,1024]{2,1,0:T(8,128)}, bf16[64,8,128]{2,1,0:T(8,128)(2,1)}) custom-call(bf16[64,64,128]{2,1,0:T(8,128)(2,1)S(1)} %all-to-all-done.1.recv_ref, bf16[4,128,1024]{2,1,0:T(8,128)(2,1)} %get-tuple-element.13.normed_ref, bf16[4,128,1024]{2,1,0:T(8,128)(2,1)} %get-tuple-element.14.mixed_ref, ...), custom_call_target="tpu_custom_call" | custom-call | flops 600000000 | bytes 8000000 | tf_op jit(solution)/shard_map/gate_side/pallas_call | solution.py:521
  119.7 21.8 %all-to-all-done.2.recv_ref = bf16[64,64,128]{2,1,0:T(8,128)(2,1)S(1)} async-done(((bf16[64,64,128]{2,1,0:T(8,128)(2,1)}), bf16[64,64,128]{2,1,0:T(8,128)(2,1)S(1)}, u32[]{:S(2)}, u32[]{:S(2)}) %all-to-all-start.2) | async-done | bytes 1048608 | tf_op jit(solution)/shard_map/all_to_all | solution.py:388
  141.6 2.7 %factor_grad.1 = bf16[64,128,128]{2,1,0:T(8,128)(2,1)S(1)} custom-call(bf16[64,64,128]{2,1,0:T(8,128)(2,1)S(1)} %all-to-all-done.2.recv_ref, bf16[4,512,512]{2,1,0:T(8,128)(2,1)} %slabs.1.factor_hbm, bf16[64,8,128]{2,1,0:T(8,128)(2,1)} %get-tuple-element.16.early_hbm.early_ref), custom_call_target="tpu_custom_call" | custom-call | flops 1100000000 | bytes 5000000 | tf_op jit(solution)/shard_map/factor_grad/pallas_call | solution.py:547
  144.2 55.3 %all_to_all.26.recv_ref = bf16[64,128,128]{2,1,0:T(8,128)(2,1)S(1)} all-to-all(bf16[64,128,128]{2,1,0:T(8,128)(2,1)S(1)} %factor_grad.1), channel_id=1, replica_groups=mesh['cplx'=4,'row'=64] {'row'}, dimensions={0} | all-to-all | bytes 4194304 | tf_op jit(solution)/shard_map/all_to_all | solution.py:388
  199.6 5.2 %proj_grad.1 = bf16[64,16,128]{2,1,0:T(8,128)(2,1)} custom-call(bf16[64,128,128]{2,1,0:T(8,128)(2,1)S(1)} %all_to_all.26.recv_ref, bf16[4,4,128,1024]{3,2,1,0:T(8,128)(2,1)} %get-tuple-element.17.coef_ref, bf16[4,128,1024]{2,1,0:T(8,128)(2,1)} %get-tuple-element.13.normed_ref, bf16[64,8,128]{2,1,0:T(8,128)(2,1)} %get-tuple-element.16.early_hbm.early_ref), custom_call_target="tpu_custom_call" | custom-call | flops 600000000 | bytes 8000000 | tf_op jit(solution)/shard_map/proj_grad/pallas_call | solution.py:564
  204.8 6.3 %all-to-all-start.4 = ((bf16[64,16,128]{2,1,0:T(8,128)(2,1)}), bf16[64,16,128]{2,1,0:T(8,128)(2,1)S(1)}, u32[]{:S(2)}, u32[]{:S(2)}) async-start(bf16[64,16,128]{2,1,0:T(8,128)(2,1)} %proj_grad.1), calls=%async_computation.4 | async-start | bytes 524288 | tf_op jit(solution)/shard_map/all_to_all | solution.py:388
  211.1 6.3 %pair_grad.1 = bf16[8,512,128]{2,1,0:T(8,128)(2,1)} custom-call(bf16[64,128,128]{2,1,0:T(8,128)(2,1)S(1)} %all_to_all.26.recv_ref, bf16[4,4,128,1024]{3,2,1,0:T(8,128)(2,1)} %get-tuple-element.17.coef_ref, f32[4,128,1024]{2,1,0:T(8,128)} %get-tuple-element.18.gate_normed_ref, bf16[8,512,128]{2,1,0:T(8,128)(2,1)} %x_ref.5, f32[1,128]{1,0:T(1,128)} %bitcast.10, ...), custom_call_target="tpu_custom_call" | custom-call | flops 600000000 | bytes 8000000 | tf_op jit(solution)/shard_map/pair_grad/pallas_call | solution.py:581
  217.4 5.9 %all-to-all-done.4.refs_0_ = bf16[64,16,128]{2,1,0:T(8,128)(2,1)S(1)} async-done(((bf16[64,16,128]{2,1,0:T(8,128)(2,1)}), bf16[64,16,128]{2,1,0:T(8,128)(2,1)S(1)}, u32[]{:S(2)}, u32[]{:S(2)}) %all-to-all-start.4) | async-done | bytes 262176 | tf_op jit(solution)/shard_map/all_to_all | solution.py:388
  223.4 0.7 weight_sum.1
Async XLA Ops:
  70.9 33.9 %all-to-all-start.1 = ((bf16[64,64,128]{2,1,0:T(8,128)(2,1)}), bf16[64,64,128]{2,1,0:T(8,128)(2,1)S(1)}, u32[]{:S(2)}, u32[]{:S(2)}) async-start(bf16[64,64,128]{2,1,0:T(8,128)(2,1)} %product.1), calls=%async_computation.1 | async-start | bytes 2097152 | tf_op jit(solution)/shard_map/all_to_all | solution.py:388
  107.9 33.6 %all-to-all-start.2 = ((bf16[64,64,128]{2,1,0:T(8,128)(2,1)}), bf16[64,64,128]{2,1,0:T(8,128)(2,1)S(1)}, u32[]{:S(2)}, u32[]{:S(2)}) async-start(bf16[64,64,128]{2,1,0:T(8,128)(2,1)} %product_grad.1), calls=%async_computation.2 | async-start | bytes 2097152 | tf_op jit(solution)/shard_map/all_to_all | solution.py:388
  204.8 18.6 %all-to-all-start.4 = ((bf16[64,16,128]{2,1,0:T(8,128)(2,1)}), bf16[64,16,128]{2,1,0:T(8,128)(2,1)S(1)}, u32[]{:S(2)}, u32[]{:S(2)}) async-start(bf16[64,16,128]{2,1,0:T(8,128)(2,1)} %proj_grad.1), calls=%async_computation.4 | async-start | bytes 524288 | tf_op jit(solution)/shard_map/all_to_all | solution.py:388

commit v7 on v6

--- a/solution.py
+++ b/solution.py
@@ -338,8 +338,8 @@
                 axis=1,
             )
             grad = grad.astype(BF16)
-            values = [grad * coef_ref[0, 2 * side + part, :, cols] for part in range(2)]
-            piece = dot_nt(normed_ref[0, :, cols], jnp.concatenate(values, axis=0))
+            values = [grad * coef_ref[step, 2 * side + part, :, cols] for part in range(2)]
+            piece = dot_nt(normed_ref[step, :, cols], jnp.concatenate(values, axis=0))
             both = piece if both is None else both + piece
         for part in range(2):
             term[2 * side + part] += both[:, part * channels : (part + 1) * channels]
@@ -476,6 +476,7 @@
         compiler_params=params(40),
         cost_estimate=cost(12 * 10**8, 16 * 10**6),
     )(start, token_mask, lane_hbm, pair_hbm, cot_hbm, gain, bias, weight, out_gain, out_weight)
+    near = (coef, normed)
     h, coef, normed, mixed, gate_coef = pinned(h, coef, normed, mixed, gate_coef)
 
     sent_product = pl.pallas_call(
@@ -565,7 +566,7 @@
         proj_grad_kernel,
         name="proj_grad",
         grid=(tiles,),
-        in_specs=[vmem, coef_spec, column_spec, whole((slabs, 8, LANES))],
+        in_specs=[vmem, vmem, vmem, whole((slabs, 8, LANES))],
         out_specs=whole((slabs, 16, LANES)),
         out_shape=pltpu.HBM((slabs, 16, LANES), BF16),
         scratch_shapes=[
@@ -575,7 +576,7 @@
         ],
         compiler_params=params(24),
         cost_estimate=cost(6 * 10**8, 8 * 10**6),
-    )(parts, coef, normed, early_share)
+    )(parts, *near, early_share)
     shares = exchange(late_share)
 
     pair_gradient = pl.pallas_call(

time: 225 us -> 224 us (level)
  no operation moved by 1% of the time
where the time goes in v7:
time: 224 us; the launch traced here: 223 us
  blocking collectives  119 us (53%)
  waiting for transfers between devices  46.2 us (21%)
  Pallas kernels  38.9 us (17%)
  starting transfers between devices  18.1 us (8%)
    all_to_all x2, blocking collectives, exchange(): lax.all_to_all(values, 'row', split_axis=0, concat_axis=0, tiled=True)  119 us
    all_to_all x3, waiting for transfers between devices, exchange(): lax.all_to_all(values, 'row', split_axis=0, concat_axis=0, tiled=True)  46.2 us
    all_to_all x3, starting transfers between devices, exchange(): lax.all_to_all(values, 'row', split_axis=0, concat_axis=0, tiled=True)  18.1 us
    pallas_call x1, Pallas kernels, on_device(): pl.pallas_call(side_kernel, name='side', grid=(tiles,), in_specs=[smem, s...  7.65 us
    pallas_call x1, Pallas kernels, on_device(): pl.pallas_call(pair_grad_kernel, name='pair_grad', grid=(tiles,), in_spec...  6.31 us
    pallas_call x1, Pallas kernels, on_device(): pl.pallas_call(gate_side_kernel, name='gate_side', grid=(tiles,), in_spec...  6.01 us
    pallas_call x1, Pallas kernels, on_device(): pl.pallas_call(front_kernel, name='front', grid=(tiles,), in_specs=[smem,...  4.67 us
  transfers between devices with their start and end apart: 3, of which 3 were waited for; matrix products, arithmetic and copies ran while one was open for 0% of the time, Pallas kernels for 10%

profile of v7, /device:TPU:16, one launch (start us, length us, event | category | flops | bytes accessed | tf_op | source)
XLA Modules:
  0.0 223.2 jit_solution(14924419386059839112)
XLA Ops:
  0.6 4.7 %front.1 = bf16[64,128,128]{2,1,0:T(8,128)(2,1)S(1)} custom-call(s32[1]{0:T(128)} %bitcast.start_ref, s32[512]{0:T(512)} %mask_ref.3, s32[1,512]{1,0:T(1,128)} %bitcast.6, bf16[8,512,128]{2,1,0:T(8,128)(2,1)} %x_ref.5, f32[1,128]{1,0:T(1,128)} %bitcast.8, f32[1,128]{1,0:T(1,128)} %bitcast.14, bf16[128,640]{1,0:T(8,128)(2,1)} %weight_ref.5), custom_call_target="tpu_custom_call" | custom-call | flops 600000000 | bytes 4000000 | tf_op jit(solution)/shard_map/front/pallas_call | solution.py:441
  5.3 63.7 %all_to_all.25.recv_ref = bf16[64,128,128]{2,1,0:T(8,128)(2,1)S(1)} all-to-all(bf16[64,128,128]{2,1,0:T(8,128)(2,1)S(1)} %front.1), channel_id=1, replica_groups=mesh['cplx'=4,'row'=64] {'row'}, dimensions={0} | all-to-all | bytes 4194304 | tf_op jit(solution)/shard_map/all_to_all | solution.py:388
  69.0 1.9 product.1
  70.9 6.0 %all-to-all-start.1 = ((bf16[64,64,128]{2,1,0:T(8,128)(2,1)}), bf16[64,64,128]{2,1,0:T(8,128)(2,1)S(1)}, u32[]{:S(2)}, u32[]{:S(2)}) async-start(bf16[64,64,128]{2,1,0:T(8,128)(2,1)} %product.1), calls=%async_computation.1 | async-start | bytes 2097152 | tf_op jit(solution)/shard_map/all_to_all | solution.py:388
  76.9 7.6 %side.1 = (f32[4,1024,128]{2,1,0:T(8,128)}, bf16[4,4,128,1024]{3,2,1,0:T(8,128)(2,1)}, bf16[4,128,1024]{2,1,0:T(8,128)(2,1)}, bf16[4,128,1024]{2,1,0:T(8,128)(2,1)}, f32[4,128,1024]{2,1,0:T(8,128)}) custom-call(s32[1]{0:T(128)} %bitcast.start_ref, s32[512]{0:T(512)} %mask_ref.3, s32[1,512]{1,0:T(1,128)} %bitcast.7, bf16[8,512,128]{2,1,0:T(8,128)(2,1)} %x_ref.5, ...), custom_call_target="tpu_custom_call" | custom-call | flops 1200000000 | bytes 16000000 | tf_op jit(solution)/shard_map/side/pallas_call | solution.py:459
  84.5 1.8 slabs.1.factor_hbm
  86.3 18.5 %all-to-all-done.1.recv_ref = bf16[64,64,128]{2,1,0:T(8,128)(2,1)S(1)} async-done(((bf16[64,64,128]{2,1,0:T(8,128)(2,1)}), bf16[64,64,128]{2,1,0:T(8,128)(2,1)S(1)}, u32[]{:S(2)}, u32[]{:S(2)}) %all-to-all-start.1) | async-done | bytes 1048608 | tf_op jit(solution)/shard_map/all_to_all | solution.py:388
  104.8 3.2 %product_grad.1 = bf16[64,64,128]{2,1,0:T(8,128)(2,1)} custom-call(bf16[64,64,128]{2,1,0:T(8,128)(2,1)S(1)} %all-to-all-done.1.recv_ref, f32[4,1024,128]{2,1,0:T(8,128)} %get-tuple-element.12.h_hbm, bf16[4,512,512]{2,1,0:T(8,128)(2,1)} %slabs.1.factor_hbm), custom_call_target="tpu_custom_call" | custom-call | flops 10000000 | bytes 4000000 | tf_op jit(solution)/shard_map/product_grad/pallas_call | solution.py:505
  107.9 5.8 %all-to-all-start.2 = ((bf16[64,64,128]{2,1,0:T(8,128)(2,1)}), bf16[64,64,128]{2,1,0:T(8,128)(2,1)S(1)}, u32[]{:S(2)}, u32[]{:S(2)}) async-start(bf16[64,64,128]{2,1,0:T(8,128)(2,1)} %product_grad.1), calls=%async_computation.2 | async-start | bytes 2097152 | tf_op jit(solution)/shard_map/all_to_all | solution.py:388
  113.7 6.0 %gate_side.1 = (f32[4,128,1024]{2,1,0:T(8,128)}, bf16[64,8,128]{2,1,0:T(8,128)(2,1)}) custom-call(bf16[64,64,128]{2,1,0:T(8,128)(2,1)S(1)} %all-to-all-done.1.recv_ref, bf16[4,128,1024]{2,1,0:T(8,128)(2,1)} %get-tuple-element.13.normed_ref, bf16[4,128,1024]{2,1,0:T(8,128)(2,1)} %get-tuple-element.14.mixed_ref, ...), custom_call_target="tpu_custom_call" | custom-call | flops 600000000 | bytes 8000000 | tf_op jit(solution)/shard_map/gate_side/pallas_call | solution.py:522
  119.7 21.8 %all-to-all-done.2.recv_ref = bf16[64,64,128]{2,1,0:T(8,128)(2,1)S(1)} async-done(((bf16[64,64,128]{2,1,0:T(8,128)(2,1)}), bf16[64,64,128]{2,1,0:T(8,128)(2,1)S(1)}, u32[]{:S(2)}, u32[]{:S(2)}) %all-to-all-start.2) | async-done | bytes 1048608 | tf_op jit(solution)/shard_map/all_to_all | solution.py:388
  141.6 0.0 copy-start.1
  141.6 2.8 %factor_grad.1 = bf16[64,128,128]{2,1,0:T(8,128)(2,1)S(1)} custom-call(bf16[64,64,128]{2,1,0:T(8,128)(2,1)S(1)} %all-to-all-done.2.recv_ref, bf16[4,512,512]{2,1,0:T(8,128)(2,1)} %slabs.1.factor_hbm, bf16[64,8,128]{2,1,0:T(8,128)(2,1)} %get-tuple-element.16.early_hbm.early_ref), custom_call_target="tpu_custom_call" | custom-call | flops 1100000000 | bytes 5000000 | tf_op jit(solution)/shard_map/factor_grad/pallas_call | solution.py:548
  144.3 0.0 copy-start
  144.3 55.6 %all_to_all.26.recv_ref = bf16[64,128,128]{2,1,0:T(8,128)(2,1)S(1)} all-to-all(bf16[64,128,128]{2,1,0:T(8,128)(2,1)S(1)} %factor_grad.1), channel_id=1, replica_groups=mesh['cplx'=4,'row'=64] {'row'}, dimensions={0} | all-to-all | bytes 4194304 | tf_op jit(solution)/shard_map/all_to_all | solution.py:388
  199.9 0.0 copy-done.1
  199.9 0.0 copy-done
  199.9 4.0 %proj_grad.1 = bf16[64,16,128]{2,1,0:T(8,128)(2,1)} custom-call(bf16[64,128,128]{2,1,0:T(8,128)(2,1)S(1)} %all_to_all.26.recv_ref, bf16[4,4,128,1024]{3,2,1,0:T(8,128)(2,1)S(1)} %copy-done, bf16[4,128,1024]{2,1,0:T(8,128)(2,1)S(1)} %copy-done.1, bf16[64,8,128]{2,1,0:T(8,128)(2,1)} %get-tuple-element.16.early_hbm.early_ref), custom_call_target="tpu_custom_call" | custom-call | flops 600000000 | bytes 8000000 | tf_op jit(solution)/shard_map/proj_grad/pallas_call | solution.py:565
  204.0 6.3 %all-to-all-start.4 = ((bf16[64,16,128]{2,1,0:T(8,128)(2,1)}), bf16[64,16,128]{2,1,0:T(8,128)(2,1)S(1)}, u32[]{:S(2)}, u32[]{:S(2)}) async-start(bf16[64,16,128]{2,1,0:T(8,128)(2,1)} %proj_grad.1), calls=%async_computation.4 | async-start | bytes 524288 | tf_op jit(solution)/shard_map/all_to_all | solution.py:388
  210.3 6.3 %pair_grad.1 = bf16[8,512,128]{2,1,0:T(8,128)(2,1)} custom-call(bf16[64,128,128]{2,1,0:T(8,128)(2,1)S(1)} %all_to_all.26.recv_ref, bf16[4,4,128,1024]{3,2,1,0:T(8,128)(2,1)} %get-tuple-element.17.coef_ref, f32[4,128,1024]{2,1,0:T(8,128)} %get-tuple-element.18.gate_normed_ref, bf16[8,512,128]{2,1,0:T(8,128)(2,1)} %x_ref.5, f32[1,128]{1,0:T(1,128)} %bitcast.10, ...), custom_call_target="tpu_custom_call" | custom-call | flops 600000000 | bytes 8000000 | tf_op jit(solution)/shard_map/pair_grad/pallas_call | solution.py:582
  216.6 5.9 %all-to-all-done.4.refs_0_ = bf16[64,16,128]{2,1,0:T(8,128)(2,1)S(1)} async-done(((bf16[64,16,128]{2,1,0:T(8,128)(2,1)}), bf16[64,16,128]{2,1,0:T(8,128)(2,1)S(1)}, u32[]{:S(2)}, u32[]{:S(2)}) %all-to-all-start.4) | async-done | bytes 262176 | tf_op jit(solution)/shard_map/all_to_all | solution.py:388
  222.5 0.7 weight_sum.1
Async XLA Ops:
  70.9 33.9 %all-to-all-start.1 = ((bf16[64,64,128]{2,1,0:T(8,128)(2,1)}), bf16[64,64,128]{2,1,0:T(8,128)(2,1)S(1)}, u32[]{:S(2)}, u32[]{:S(2)}) async-start(bf16[64,64,128]{2,1,0:T(8,128)(2,1)} %product.1), calls=%async_computation.1 | async-start | bytes 2097152 | tf_op jit(solution)/shard_map/all_to_all | solution.py:388
  107.9 33.6 %all-to-all-start.2 = ((bf16[64,64,128]{2,1,0:T(8,128)(2,1)}), bf16[64,64,128]{2,1,0:T(8,128)(2,1)S(1)}, u32[]{:S(2)}, u32[]{:S(2)}) async-start(bf16[64,64,128]{2,1,0:T(8,128)(2,1)} %product_grad.1), calls=%async_computation.2 | async-start | bytes 2097152 | tf_op jit(solution)/shard_map/all_to_all | solution.py:388
  141.6 58.4 %copy-start.1 = (bf16[4,128,1024]{2,1,0:T(8,128)(2,1)S(1)}, bf16[4,128,1024]{2,1,0:T(8,128)(2,1)}, u32[]{:S(2)}) copy-start(bf16[4,128,1024]{2,1,0:T(8,128)(2,1)} %get-tuple-element.13.normed_ref) | copy-start | bytes 3145732
  144.3 55.6 %copy-start = (bf16[4,4,128,1024]{3,2,1,0:T(8,128)(2,1)S(1)}, bf16[4,4,128,1024]{3,2,1,0:T(8,128)(2,1)}, u32[]{:S(2)}) copy-start(bf16[4,4,128,1024]{3,2,1,0:T(8,128)(2,1)} %get-tuple-element.17.coef_ref) | copy-start | bytes 12582916
  204.0 18.6 %all-to-all-start.4 = ((bf16[64,16,128]{2,1,0:T(8,128)(2,1)}), bf16[64,16,128]{2,1,0:T(8,128)(2,1)S(1)}, u32[]{:S(2)}, u32[]{:S(2)}) async-start(bf16[64,16,128]{2,1,0:T(8,128)(2,1)} %proj_grad.1), calls=%async_computation.4 | async-start | bytes 524288 | tf_op jit(solution)/shard_map/all_to_all | solution.py:388

commit v8 on v7

--- a/solution.py
+++ b/solution.py
@@ -159,17 +159,26 @@
                 out_ref[side * 2 + part, :, tile * LANES : (tile + 1) * LANES] = parts[part]
 
 
-def product_kernel(recv_ref, out_ref, slab):
+def product_kernel(recv_ref, out_hbm, slab, out_ref, sent):
     slabs = recv_ref.shape[0]
     tokens = slab.shape[1]
     slab_unpack_kernel(recv_ref, slab)
     rows = tokens // slabs
     products = [dot_nt(slab[part], slab[2 + part]) for part in range(2)]
-    for tile in range(tokens // LANES):
+    tiles = tokens // LANES
+    group = 2 * rows
+    stores = []
+    for tile in range(tiles):
         cols = slice(tile * LANES, (tile + 1) * LANES)
-        out_ref[:, tile * 2 * rows : (tile + 1) * 2 * rows, :] = pack(
-            products[0][:, cols], products[1][:, cols], slabs
+        out_ref[tile] = pack(products[0][:, cols], products[1][:, cols], slabs)
+        stores.append(
+            pltpu.make_async_copy(
+                out_ref.at[tile], out_hbm.at[:, pl.ds(tile * group, group), :], sent.at[tile]
+            )
         )
+        stores[tile].start()
+    for store in stores:
+        store.wait()
 
 
 def product_grad_kernel(recv_ref, h_hbm, factor_hbm, out_ref, held, h_ref, arrived):
@@ -483,9 +492,13 @@
         product_kernel,
         name="product",
         in_specs=[vmem],
-        out_specs=whole((slabs, pair * tiles, LANES)),
+        out_specs=anywhere,
         out_shape=pltpu.HBM((slabs, pair * tiles, LANES), BF16),
-        scratch_shapes=[pltpu.VMEM((4, tokens, tokens), BF16)],
+        scratch_shapes=[
+            pltpu.VMEM((4, tokens, tokens), BF16),
+            pltpu.VMEM((tiles, slabs, pair, LANES), BF16),
+            pltpu.SemaphoreType.DMA((tiles,)),
+        ],
         compiler_params=params(20),
         cost_estimate=cost(6 * 10**8, 3 * 10**6),
     )(factors)

time: 224 us -> 224 us (level)
  no operation moved by 1% of the time
where the time goes in v8:
time: 224 us; the launch traced here: 223 us
  blocking collectives  119 us (53%)
  waiting for transfers between devices  46.2 us (21%)
  Pallas kernels  38.9 us (17%)
  starting transfers between devices  18.1 us (8%)
    all_to_all x2, blocking collectives, exchange(): lax.all_to_all(values, 'row', split_axis=0, concat_axis=0, tiled=True)  119 us
    all_to_all x3, waiting for transfers between devices, exchange(): lax.all_to_all(values, 'row', split_axis=0, concat_axis=0, tiled=True)  46.2 us
    all_to_all x3, starting transfers between devices, exchange(): lax.all_to_all(values, 'row', split_axis=0, concat_axis=0, tiled=True)  18.1 us
    pallas_call x1, Pallas kernels, on_device(): pl.pallas_call(side_kernel, name='side', grid=(tiles,), in_specs=[smem, s...  7.65 us
    pallas_call x1, Pallas kernels, on_device(): pl.pallas_call(pair_grad_kernel, name='pair_grad', grid=(tiles,), in_spec...  6.31 us
    pallas_call x1, Pallas kernels, on_device(): pl.pallas_call(gate_side_kernel, name='gate_side', grid=(tiles,), in_spec...  6.01 us
    pallas_call x1, Pallas kernels, on_device(): pl.pallas_call(front_kernel, name='front', grid=(tiles,), in_specs=[smem,...  4.67 us
  transfers between devices with their start and end apart: 3, of which 3 were waited for; matrix products, arithmetic and copies ran while one was open for 0% of the time, Pallas kernels for 10%

profile of v8, /device:TPU:16, one launch (start us, length us, event | category | flops | bytes accessed | tf_op | source)
XLA Modules:
  0.0 223.2 jit_solution(3688532878065661921)
XLA Ops:
  0.6 4.7 %front.1 = bf16[64,128,128]{2,1,0:T(8,128)(2,1)S(1)} custom-call(s32[1]{0:T(128)} %bitcast.start_ref, s32[512]{0:T(512)} %mask_ref.3, s32[1,512]{1,0:T(1,128)} %bitcast.6, bf16[8,512,128]{2,1,0:T(8,128)(2,1)} %x_ref.5, f32[1,128]{1,0:T(1,128)} %bitcast.8, f32[1,128]{1,0:T(1,128)} %bitcast.14, bf16[128,640]{1,0:T(8,128)(2,1)} %weight_ref.5), custom_call_target="tpu_custom_call" | custom-call | flops 600000000 | bytes 4000000 | tf_op jit(solution)/shard_map/front/pallas_call | solution.py:450
  5.3 63.7 %all_to_all.25.recv_ref = bf16[64,128,128]{2,1,0:T(8,128)(2,1)S(1)} all-to-all(bf16[64,128,128]{2,1,0:T(8,128)(2,1)S(1)} %front.1), channel_id=1, replica_groups=mesh['cplx'=4,'row'=64] {'row'}, dimensions={0} | all-to-all | bytes 4194304 | tf_op jit(solution)/shard_map/all_to_all | solution.py:397
  69.0 1.9 product.1
  70.9 6.0 %all-to-all-start.1 = ((bf16[64,64,128]{2,1,0:T(8,128)(2,1)}), bf16[64,64,128]{2,1,0:T(8,128)(2,1)S(1)}, u32[]{:S(2)}, u32[]{:S(2)}) async-start(bf16[64,64,128]{2,1,0:T(8,128)(2,1)} %product.1), calls=%async_computation.1 | async-start | bytes 2097152 | tf_op jit(solution)/shard_map/all_to_all | solution.py:397
  76.9 7.6 %side.1 = (f32[4,1024,128]{2,1,0:T(8,128)}, bf16[4,4,128,1024]{3,2,1,0:T(8,128)(2,1)}, bf16[4,128,1024]{2,1,0:T(8,128)(2,1)}, bf16[4,128,1024]{2,1,0:T(8,128)(2,1)}, f32[4,128,1024]{2,1,0:T(8,128)}) custom-call(s32[1]{0:T(128)} %bitcast.start_ref, s32[512]{0:T(512)} %mask_ref.3, s32[1,512]{1,0:T(1,128)} %bitcast.7, bf16[8,512,128]{2,1,0:T(8,128)(2,1)} %x_ref.5, ...), custom_call_target="tpu_custom_call" | custom-call | flops 1200000000 | bytes 16000000 | tf_op jit(solution)/shard_map/side/pallas_call | solution.py:468
  84.6 1.8 slabs.1.factor_hbm
  86.4 18.5 %all-to-all-done.1.recv_ref = bf16[64,64,128]{2,1,0:T(8,128)(2,1)S(1)} async-done(((bf16[64,64,128]{2,1,0:T(8,128)(2,1)}), bf16[64,64,128]{2,1,0:T(8,128)(2,1)S(1)}, u32[]{:S(2)}, u32[]{:S(2)}) %all-to-all-start.1) | async-done | bytes 1048608 | tf_op jit(solution)/shard_map/all_to_all | solution.py:397
  104.8 3.2 %product_grad.1 = bf16[64,64,128]{2,1,0:T(8,128)(2,1)} custom-call(bf16[64,64,128]{2,1,0:T(8,128)(2,1)S(1)} %all-to-all-done.1.recv_ref, f32[4,1024,128]{2,1,0:T(8,128)} %get-tuple-element.12.h_hbm, bf16[4,512,512]{2,1,0:T(8,128)(2,1)} %slabs.1.factor_hbm), custom_call_target="tpu_custom_call" | custom-call | flops 10000000 | bytes 4000000 | tf_op jit(solution)/shard_map/product_grad/pallas_call | solution.py:518
  108.0 5.8 %all-to-all-start.2 = ((bf16[64,64,128]{2,1,0:T(8,128)(2,1)}), bf16[64,64,128]{2,1,0:T(8,128)(2,1)S(1)}, u32[]{:S(2)}, u32[]{:S(2)}) async-start(bf16[64,64,128]{2,1,0:T(8,128)(2,1)} %product_grad.1), calls=%async_computation.2 | async-start | bytes 2097152 | tf_op jit(solution)/shard_map/all_to_all | solution.py:397
  113.8 6.0 %gate_side.1 = (f32[4,128,1024]{2,1,0:T(8,128)}, bf16[64,8,128]{2,1,0:T(8,128)(2,1)}) custom-call(bf16[64,64,128]{2,1,0:T(8,128)(2,1)S(1)} %all-to-all-done.1.recv_ref, bf16[4,128,1024]{2,1,0:T(8,128)(2,1)} %get-tuple-element.13.normed_ref, bf16[4,128,1024]{2,1,0:T(8,128)(2,1)} %get-tuple-element.14.mixed_ref, ...), custom_call_target="tpu_custom_call" | custom-call | flops 600000000 | bytes 8000000 | tf_op jit(solution)/shard_map/gate_side/pallas_call | solution.py:535
  119.8 21.8 %all-to-all-done.2.recv_ref = bf16[64,64,128]{2,1,0:T(8,128)(2,1)S(1)} async-done(((bf16[64,64,128]{2,1,0:T(8,128)(2,1)}), bf16[64,64,128]{2,1,0:T(8,128)(2,1)S(1)}, u32[]{:S(2)}, u32[]{:S(2)}) %all-to-all-start.2) | async-done | bytes 1048608 | tf_op jit(solution)/shard_map/all_to_all | solution.py:397
  141.6 0.0 copy-start.1
  141.6 2.8 %factor_grad.1 = bf16[64,128,128]{2,1,0:T(8,128)(2,1)S(1)} custom-call(bf16[64,64,128]{2,1,0:T(8,128)(2,1)S(1)} %all-to-all-done.2.recv_ref, bf16[4,512,512]{2,1,0:T(8,128)(2,1)} %slabs.1.factor_hbm, bf16[64,8,128]{2,1,0:T(8,128)(2,1)} %get-tuple-element.16.early_hbm.early_ref), custom_call_target="tpu_custom_call" | custom-call | flops 1100000000 | bytes 5000000 | tf_op jit(solution)/shard_map/factor_grad/pallas_call | solution.py:561
  144.4 0.0 copy-start
  144.4 55.6 %all_to_all.26.recv_ref = bf16[64,128,128]{2,1,0:T(8,128)(2,1)S(1)} all-to-all(bf16[64,128,128]{2,1,0:T(8,128)(2,1)S(1)} %factor_grad.1), channel_id=1, replica_groups=mesh['cplx'=4,'row'=64] {'row'}, dimensions={0} | all-to-all | bytes 4194304 | tf_op jit(solution)/shard_map/all_to_all | solution.py:397
  200.0 0.0 copy-done.1
  200.0 0.0 copy-done
  200.0 4.0 %proj_grad.1 = bf16[64,16,128]{2,1,0:T(8,128)(2,1)} custom-call(bf16[64,128,128]{2,1,0:T(8,128)(2,1)S(1)} %all_to_all.26.recv_ref, bf16[4,4,128,1024]{3,2,1,0:T(8,128)(2,1)S(1)} %copy-done, bf16[4,128,1024]{2,1,0:T(8,128)(2,1)S(1)} %copy-done.1, bf16[64,8,128]{2,1,0:T(8,128)(2,1)} %get-tuple-element.16.early_hbm.early_ref), custom_call_target="tpu_custom_call" | custom-call | flops 600000000 | bytes 8000000 | tf_op jit(solution)/shard_map/proj_grad/pallas_call | solution.py:578
  204.0 6.3 %all-to-all-start.4 = ((bf16[64,16,128]{2,1,0:T(8,128)(2,1)}), bf16[64,16,128]{2,1,0:T(8,128)(2,1)S(1)}, u32[]{:S(2)}, u32[]{:S(2)}) async-start(bf16[64,16,128]{2,1,0:T(8,128)(2,1)} %proj_grad.1), calls=%async_computation.4 | async-start | bytes 524288 | tf_op jit(solution)/shard_map/all_to_all | solution.py:397
  210.3 6.3 %pair_grad.1 = bf16[8,512,128]{2,1,0:T(8,128)(2,1)} custom-call(bf16[64,128,128]{2,1,0:T(8,128)(2,1)S(1)} %all_to_all.26.recv_ref, bf16[4,4,128,1024]{3,2,1,0:T(8,128)(2,1)} %get-tuple-element.17.coef_ref, f32[4,128,1024]{2,1,0:T(8,128)} %get-tuple-element.18.gate_normed_ref, bf16[8,512,128]{2,1,0:T(8,128)(2,1)} %x_ref.5, f32[1,128]{1,0:T(1,128)} %bitcast.10, ...), custom_call_target="tpu_custom_call" | custom-call | flops 600000000 | bytes 8000000 | tf_op jit(solution)/shard_map/pair_grad/pallas_call | solution.py:595
  216.6 5.9 %all-to-all-done.4.refs_0_ = bf16[64,16,128]{2,1,0:T(8,128)(2,1)S(1)} async-done(((bf16[64,16,128]{2,1,0:T(8,128)(2,1)}), bf16[64,16,128]{2,1,0:T(8,128)(2,1)S(1)}, u32[]{:S(2)}, u32[]{:S(2)}) %all-to-all-start.4) | async-done | bytes 262176 | tf_op jit(solution)/shard_map/all_to_all | solution.py:397
  222.6 0.7 weight_sum.1
Async XLA Ops:
  70.9 33.9 %all-to-all-start.1 = ((bf16[64,64,128]{2,1,0:T(8,128)(2,1)}), bf16[64,64,128]{2,1,0:T(8,128)(2,1)S(1)}, u32[]{:S(2)}, u32[]{:S(2)}) async-start(bf16[64,64,128]{2,1,0:T(8,128)(2,1)} %product.1), calls=%async_computation.1 | async-start | bytes 2097152 | tf_op jit(solution)/shard_map/all_to_all | solution.py:397
  108.0 33.6 %all-to-all-start.2 = ((bf16[64,64,128]{2,1,0:T(8,128)(2,1)}), bf16[64,64,128]{2,1,0:T(8,128)(2,1)S(1)}, u32[]{:S(2)}, u32[]{:S(2)}) async-start(bf16[64,64,128]{2,1,0:T(8,128)(2,1)} %product_grad.1), calls=%async_computation.2 | async-start | bytes 2097152 | tf_op jit(solution)/shard_map/all_to_all | solution.py:397
  141.6 58.4 %copy-start.1 = (bf16[4,128,1024]{2,1,0:T(8,128)(2,1)S(1)}, bf16[4,128,1024]{2,1,0:T(8,128)(2,1)}, u32[]{:S(2)}) copy-start(bf16[4,128,1024]{2,1,0:T(8,128)(2,1)} %get-tuple-element.13.normed_ref) | copy-start | bytes 3145732
  144.4 55.6 %copy-start = (bf16[4,4,128,1024]{3,2,1,0:T(8,128)(2,1)S(1)}, bf16[4,4,128,1024]{3,2,1,0:T(8,128)(2,1)}, u32[]{:S(2)}) copy-start(bf16[4,4,128,1024]{3,2,1,0:T(8,128)(2,1)} %get-tuple-element.17.coef_ref) | copy-start | bytes 12582916
  204.0 18.6 %all-to-all-start.4 = ((bf16[64,16,128]{2,1,0:T(8,128)(2,1)}), bf16[64,16,128]{2,1,0:T(8,128)(2,1)S(1)}, u32[]{:S(2)}, u32[]{:S(2)}) async-start(bf16[64,16,128]{2,1,0:T(8,128)(2,1)} %proj_grad.1), calls=%async_computation.4 | async-start | bytes 524288 | tf_op jit(solution)/shard_map/all_to_all | solution.py:397
